TPU v7x, 256 devices: a whole 4x4x8 slice. The times are simulated.
256 devices in a mesh: gx: 16 (over x, y), gy: 8 (over z), gz: 2 (over core).
Axes of the slice: x: 4, y: 4, z: 8, core: 2. Of those that a mesh axis runs over, the one named last changes fastest.
Arguments:
- well_sources: float32 [12288, 64], P(('gx', 'gy'), 'gz'), may hold values from -6 to 6
- well_owner: int32 [12288, 1], P(('gx', 'gy')), may hold values from 0 to 127; in each aligned block of 96 rows (0 to 95, 96 to 191, ...) at most 2 rows name the same one
- well_cell: int32 [12288], P(('gx', 'gy')), may hold values from 0 to 2047
- flow_sign: int32 [3, 64, 256, 1024], P(None, 'gz', 'gx', 'gy'), may hold values from 0 to 7
- courant: float32 [3, 64, 256, 1024], P(None, 'gz', 'gx', 'gy'), may hold values from 0.01 to 0.3
- tracer: float32 [3, 64, 256, 1024], P(None, 'gz', 'gx', 'gy'), may hold values from -6 to 6
Outputs:
- lambda_start: float32 [64, 256, 1024], P('gz', 'gx', 'gy')
- smoothed: float32 [1024, 64, 256], P(('gx', 'gy', 'gz'))
Inputs may be any that keep to these rules, and one draw needn't show every extreme that they name: `well_owner`: among the wells of one index of gx+gy at most 2 name the same owner, a bound that some block of them reaches.
All inputs are finite; a program needn't handle non-finite values.
Results may differ from a plain program's by a relative error of at most 0.00015.
Values sent between devices are 32-bit elements; how exact they have to be, the bound alone decides.
No kernel may reach another device: no remote copies, remote signals or barrier semaphores. Data moves between devices by JAX's collectives and lax.ppermute only.
A program may use at most 128 MiB of HBM per device.

v0:
```python
import math

import jax
import jax.numpy as jnp
from jax import lax
from jax.sharding import PartitionSpec as P

STEPS = 3


def with_halo(block, sides, width):
    for axis, dim in sides:
        count = lax.axis_size(axis)
        forward = [(i, i + 1) for i in range(count - 1)]
        backward = [(target, source) for source, target in forward]
        low = lax.ppermute(
            lax.slice_in_dim(block, block.shape[dim] - width, None, axis=dim), axis, forward
        )
        high = lax.ppermute(lax.slice_in_dim(block, 0, width, axis=dim), axis, backward)
        block = jnp.concatenate([low, block, high], axis=dim)
    return block


def correlation(extent, length):
    places = jnp.arange(extent).astype(jnp.float32)
    spacing = jnp.abs(places[:, None] - places[None, :])
    return jnp.exp(-spacing / length) / math.sqrt(length)


def advance_weights(adjoint, rising_pad, falling_pad, staying):
    padded = with_halo(adjoint, (("gx", 1), ("gy", 2), ("gz", 0)), 1)
    updated = staying * adjoint
    updated = (
        updated
        + rising_pad[0, 1:-1, 2:, 1:-1] * padded[1:-1, 2:, 1:-1]
        + falling_pad[0, 1:-1, :-2, 1:-1] * padded[1:-1, :-2, 1:-1]
    )
    updated = (
        updated
        + rising_pad[1, 1:-1, 1:-1, 2:] * padded[1:-1, 1:-1, 2:]
        + falling_pad[1, 1:-1, 1:-1, :-2] * padded[1:-1, 1:-1, :-2]
    )
    updated = (
        updated
        + rising_pad[2, 2:, 1:-1, 1:-1] * padded[2:, 1:-1, 1:-1]
        + falling_pad[2, :-2, 1:-1, 1:-1] * padded[:-2, 1:-1, 1:-1]
    )
    return updated


def per_device(well_sources, well_owner, well_cell, flow_sign, courant, tracer):
    brick_z, brick_x, brick_y = (courant.shape[1], courant.shape[2], courant.shape[3])
    columns = brick_x * brick_y
    groups = lax.axis_size("gx") * lax.axis_size("gy")
    my_owner = lax.axis_index("gx") * lax.axis_size("gy") + lax.axis_index("gy")
    owners = well_owner[:, 0]
    all_sources, all_owner, all_cell = (
        lax.all_gather(well_sources, ("gx", "gy"), axis=0, tiled=True),
        lax.all_gather(owners, ("gx", "gy"), axis=0, tiled=True),
        lax.all_gather(well_cell, ("gx", "gy"), axis=0, tiled=True),
    )
    target = jnp.where(all_owner == my_owner, all_cell, columns)
    landed = (
        jnp.zeros((brick_z, columns), jnp.float32)
        .at[:, target]
        .add(jnp.transpose(all_sources), mode="drop")
    )
    adjoint = landed.reshape(brick_z, brick_x, brick_y)
    upward = jnp.stack([flow_sign // 1 % 2, flow_sign // 2 % 2, flow_sign // 4 % 2], axis=1).astype(
        jnp.float32
    )
    staying = 1.0 - (courant[0] + courant[1] + courant[2])
    gradient = jnp.zeros((brick_z, brick_x, brick_y), jnp.float32)
    weights = jnp.stack([courant[None] * upward, courant[None] * (1.0 - upward)])
    weight_pad = with_halo(weights, (("gx", 4), ("gy", 5), ("gz", 3)), 1)
    for step in reversed(range(STEPS)):
        adjoint = advance_weights(adjoint, weight_pad[0, step], weight_pad[1, step], staying)
        gradient = gradient + adjoint * tracer[step]
    highest = lax.Precision.HIGHEST
    y_lines = lax.all_to_all(gradient, "gy", split_axis=1, concat_axis=2, tiled=True)
    x_share = y_lines.shape[1]
    full_y = y_lines.shape[2]
    line_count = y_lines.shape[0] * x_share
    smooth_y = lax.dot_general(
        correlation(full_y, 2 * brick_y),
        y_lines.reshape(line_count, full_y),
        (((1,), (1,)), ((), ())),
        precision=highest,
        preferred_element_type=jnp.float32,
    )
    planes = lax.all_to_all(
        lax.all_to_all(smooth_y, ("gx", "gy"), split_axis=0, concat_axis=1, tiled=True),
        "gz",
        split_axis=0,
        concat_axis=1,
        tiled=True,
    )
    y_rows = planes.shape[0]
    depth_groups = lax.axis_size("gz")
    plane_view = planes.reshape(y_rows, depth_groups, groups, brick_z, x_share)
    full_x = groups * x_share
    table_x = correlation(full_x, 2 * brick_x).reshape(full_x, groups, x_share)
    smooth_x = jnp.einsum("ykdza,jda->ykzj", plane_view, table_x, precision=highest)
    full_z = depth_groups * brick_z
    smooth_x = smooth_x.reshape(y_rows, full_z, full_x)
    smoothed = jnp.einsum(
        "yzj,iz->yij", smooth_x, correlation(full_z, 2 * brick_z), precision=highest
    )
    return (adjoint, smoothed)


def solution(mesh):
    return jax.shard_map(
        per_device,
        mesh=mesh,
        in_specs=(
            P(("gx", "gy"), "gz"),
            P(("gx", "gy"), None),
            P(("gx", "gy")),
            P(None, "gz", "gx", "gy"),
            P(None, "gz", "gx", "gy"),
            P(None, "gz", "gx", "gy"),
        ),
        out_specs=(P("gz", "gx", "gy"), P(("gx", "gy", "gz"), None, None)),
        check_vma=False,
    )
```

profile of v0, /device:TPU:1, one launch (start us, length us, event | category | flops | bytes accessed | tf_op | source)
XLA Modules:
  0.0 618.9 jit_solution(1753815041108908470)
XLA Ops:
  7.2 1.3 dynamic-slice
  12.2 1.4 copy.58
  13.6 2.7 fusion.12
  17.0 1.4 copy-done
  18.4 0.9 pad_maximum_fusion.9
  19.3 4.0 collective-permute-start
  23.3 1.3 collective-permute-start.1
  24.7 4.7 collective-permute-done
  29.3 3.9 collective-permute-done.1
  33.3 2.7 pad_maximum_fusion.1
  35.9 6.3 %fusion.95 = (f32[2,3,3,32,18,1]{5,3,4,2,1,0:T(8,128)}, f32[2,3,3,32,18,1]{5,3,4,2,1,0:T(8,128)}) fusion(f32[2,3,3,32,18,128]{5,3,4,2,1,0:T(8,128)S(1)} %pad_maximum_fusion.1), kind=kLoop, calls=%fused_computation.232 | loop fusion | bytes 165888 | tf_op jit(solution)/shard_map/slice | solution.py:17
  42.2 3.9 copy.71
  46.1 3.5 collective-permute-start.2
  49.7 4.4 copy.72
  54.1 1.3 collective-permute-start.3
  55.4 172.0 %all-reduce.5.cloned.1.call-done = (s32[12288]{0:T(1024)}, s32[12288]{0:T(1024)}) async-done(((s32[12288]{0:T(1024)}, s32[12288]{0:T(1024)}), (s32[12288]{0:T(1024)}, s32[12288]{0:T(1024)})) %all-reduce.5.cloned.1.call-update) | async-done | bytes 98320
  228.2 3.6 copy.73
  231.8 4.5 copy.74
  236.2 107.2 %all-gather.4.cloned.1.call-done = f32[128,96,32]{1,2,0:T(8,128)} async-done(((f32[1,96,32]{1,2,0:T(8,128)}), f32[128,96,32]{1,2,0:T(8,128)}) %all-gather.4.cloned.1.call-update) | async-done | bytes 1572880 | tf_op jit(solution)/shard_map/all_gather | solution.py:58
  343.4 5.3 copy.90
  348.7 67.0 %scatter_custom_fusion = f32[32,2048]{0,1:T(8,128)} fusion(s32[12288]{0:T(1024)S(1)} %compare_select_fusion, f32[12288,32]{1,0:T(8,128)} %bitcast.160, f32[]{:T(128)} %constant.79.clone.1), kind=kCustom, calls=%fused_computation.47 | custom fusion | flops 393216 | bytes 262656 | tf_op jit(solution)/shard_map/scatter-add | solution.py:66
  415.7 1.5 copy.63
  417.2 1.3 collective-permute-start.6
  418.6 4.6 collective-permute-start.7
  423.1 6.4 %pad_maximum_fusion.7 = (f32[2,3,3,1,18,130]{5,3,4,2,1,0:T(1,128)S(1)}, f32[2,3,3,1,18,130]{5,3,4,2,1,0:T(1,128)S(1)}) fusion(f32[2,3,3,32,18,1]{5,3,4,2,1,0:T(8,128)} %copy.74, f32[2,3,3,32,18,1]{5,3,4,2,1,0:T(8,128)} %copy.73, f32[2,3,3,32,1,128]{5,3,4,2,1,0:T(8,128)} %collective-permute-done.1, f32[2,3,3,32,1,128]{5,3,4,2,1,0:T(8,128)} %copy-done.2, ...), kind=kLoop, calls=%fused_computation.55 | loop fusion | flops 421200 | bytes 5728320 | tf_op jit(solution)/shard_map/slice | solution.py:17
  429.6 1.3 collective-permute-start.4
  430.9 8.1 %collective-permute-start.5 = (f32[2,3,3,1,18,130]{5,3,4,2,1,0:T(1,128)S(1)}, f32[2,3,3,1,18,130]{5,3,4,2,1,0:T(1,128)S(1)}, u32[]{:S(2)}, u32[]{:S(2)}) collective-permute-start(f32[2,3,3,1,18,130]{5,3,4,2,1,0:T(1,128)S(1)} %get-tuple-element.13), channel_id=1, source_target_pairs={{1,0},{3,2},{5,4},{7,6},{9,8},{11,10},{13,12},{15,14},{17,16},{19,... | collective-permute-start | bytes 505448 | tf_op jit(solution)/shard_map/ppermute | solution.py:19
  439.2 1.3 collective-permute-start.8
  440.5 4.0 collective-permute-start.9
  444.6 17.7 %pad_maximum_fusion = f32[2,3,3,34,18,130]{5,3,4,2,1,0:T(8,128)} fusion(f32[2,3,3,1,18,130]{5,3,4,2,1,0:T(1,128)S(1)} %collective-permute-done.5, f32[2,3,3,32,18,1]{5,3,4,2,1,0:T(8,128)S(1)} %bitcast.158, f32[2,3,3,32,1,128]{5,3,4,2,1,0:T(8,128)} %collective-permute-done.1, f32[1,3,3,32,16,128]{5,3,4,2,1,0:T(8,128)S(1)} %copy-done.1, ...), kind=kLoop, calls=%fused_computation.1 | loop fusion | flops 10024560 | bytes 11456640 | tf_op jit(solution)/shard_map/concatenate | solution.py:20
  462.5 1.8 collective-permute-start.10
  464.3 1.3 collective-permute-start.11
  465.6 9.0 %slice_bitcast_fusion.1 = (f32[3,34,18,130]{3,1,2,0:T(8,128)S(1)}, f32[3,34,18,130]{3,1,2,0:T(8,128)}, f32[3,34,18,130]{3,1,2,0:T(8,128)}, f32[3,34,18,130]{3,1,...) fusion(f32[2,3,3,34,18,130]{5,3,4,2,1,0:T(8,128)} %pad_maximum_fusion), kind=kLoop, calls=%fused_computation.13 | loop fusion | bytes 11456640 | tf_op jit(solution)/shard_map/squeeze | solution.py:77
  474.7 3.1 fusion.47
  477.8 1.3 collective-permute-start.12
  479.1 4.1 collective-permute-start.13
  484.2 1.3 collective-permute-start.14
  485.5 4.0 collective-permute-start.15
  489.5 2.9 collective-permute-done.14
  493.4 5.5 collective-permute-start.16
  498.8 1.3 collective-permute-start.17
  500.1 1.8 collective-permute-done.17
  501.9 2.8 fusion.35
  504.7 1.3 collective-permute-start.18
  506.0 4.4 collective-permute-start.19
  511.4 1.3 collective-permute-start.20
  512.7 4.8 collective-permute-start.21
  517.5 4.4 collective-permute-done.20
  521.9 0.9 collective-permute-done.21
  523.0 3.8 collective-permute-start.22
  526.7 1.3 collective-permute-start.23
  528.1 1.7 collective-permute-done.23
  529.8 2.9 fusion.61
  532.7 9.9 %all-to-all-start = ((f32[32,16,128]{2,0,1:T(8,128)}), f32[32,16,128]{2,0,1:T(8,128)S(1)}, u32[]{:S(2)}, u32[]{:S(2)}) async-start(f32[32,16,128]{2,0,1:T(8,128)} %get-tuple-element.8), calls=%async_computation | async-start | bytes 524288 | tf_op jit(solution)/shard_map/all_to_all | solution.py:80
  542.6 12.2 %all-to-all-done = f32[32,16,128]{2,0,1:T(8,128)S(1)} async-done(((f32[32,16,128]{2,0,1:T(8,128)}), f32[32,16,128]{2,0,1:T(8,128)S(1)}, u32[]{:S(2)}, u32[]{:S(2)}) %all-to-all-start) | async-done | bytes 262176 | tf_op jit(solution)/shard_map/all_to_all | solution.py:80
  555.1 5.0 fusion
  560.3 1.0 reshape.198
  561.3 14.9 %all-to-all-start.1 = ((f32[128,1,512]{2,1,0:T(1,128)}), f32[128,1,512]{2,1,0:T(1,128)S(1)}, u32[]{:S(2)}, u32[]{:S(2)}) async-start(f32[128,1,512]{2,1,0:T(1,128)} %reshape.198), calls=%async_computation.1 | async-start | bytes 524288 | tf_op jit(solution)/shard_map/all_to_all | solution.py:92
  577.1 13.1 %all-to-all-done.1 = f32[128,1,512]{2,1,0:T(1,128)S(1)} async-done(((f32[128,1,512]{2,1,0:T(1,128)}), f32[128,1,512]{2,1,0:T(1,128)S(1)}, u32[]{:S(2)}, u32[]{:S(2)}) %all-to-all-start.1) | async-done | bytes 262176 | tf_op jit(solution)/shard_map/all_to_all | solution.py:92
  590.7 1.3 reduce
  592.5 5.6 all_to_all.44
  598.1 5.1 copy.86
  603.2 7.2 %copy.87 = f32[4,2,32,2,128]{4,2,1,3,0:T(8,128)S(1)} copy(f32[4,2,32,2,128]{0,3,2,4,1:T(2,128)} %bitcast.159) | data formatting | bytes 524288 | tf_op jit(solution)/shard_map/ykdza,jda->ykzj/dot_general | solution.py:103
  610.9 1.1 convolution_bitcast_fusion.1
  (81 shorter events, 11.0 us)
Async XLA Ops:
  7.2 220.2 %all-reduce.5.cloned.1.call-start = ((), (), s32[]{:S(2)}) async-start(), calls=%async_computation.4 | async-start | bytes 196608
  9.9 0.9 copy-start.8
  10.8 0.6 copy-start.7
  11.5 331.9 %all-gather.4.cloned.1.call-start = ((), (), s32[]{:S(2)}) async-start(), calls=%async_computation.3 | async-start | bytes 2113536 | tf_op jit(solution)/shard_map/all_gather | solution.py:58
  17.0 1.4 copy-start
  19.3 10.0 %collective-permute-start = (f32[2,3,3,32,1,128]{5,3,4,2,1,0:T(8,128)}, f32[2,3,3,32,1,128]{5,3,4,2,1,0:T(8,128)S(1)}, u32[]{:S(2)}, u32[]{:S(2)}) collective-permute-start(f32[2,3,3,32,1,128]{5,3,4,2,1,0:T(8,128)} %get-tuple-element.22), channel_id=1, source_target_pairs={{0,16},{16,32},{32,48},{48,64},{64,80},{80,96},{96,112},{112,128},... | collective-permute-start | bytes 884744 | tf_op jit(solution)/shard_map/ppermute | solution.py:16
  23.3 9.9 %collective-permute-start.1 = (f32[2,3,3,32,1,128]{5,3,4,2,1,0:T(8,128)}, f32[2,3,3,32,1,128]{5,3,4,2,1,0:T(8,128)}, u32[]{:S(2)}, u32[]{:S(2)}) collective-permute-start(f32[2,3,3,32,1,128]{5,3,4,2,1,0:T(8,128)} %get-tuple-element.23), channel_id=1, source_target_pairs={{16,0},{32,16},{48,32},{64,48},{80,64},{96,80},{112,96},{128,112},... | collective-permute-start | bytes 884744 | tf_op jit(solution)/shard_map/ppermute | solution.py:19
  29.3 6.6 %copy-start.2 = (f32[2,3,3,32,1,128]{5,3,4,2,1,0:T(8,128)}, f32[2,3,3,32,1,128]{5,3,4,2,1,0:T(8,128)S(1)}, u32[]{:S(2)}) copy-start(f32[2,3,3,32,1,128]{5,3,4,2,1,0:T(8,128)S(1)} %collective-permute-done) | copy-start | bytes 884740
  46.1 182.1 %collective-permute-start.2 = (f32[2,3,3,32,18,1]{3,0,5,4,2,1:T(2,128)S(1)}, f32[2,3,3,32,18,1]{3,0,5,4,2,1:T(2,128)S(1)}, u32[]{:S(2)}, u32[]{:S(2)}) collective-permute-start(f32[2,3,3,32,18,1]{3,0,5,4,2,1:T(2,128)S(1)} %copy.71), channel_id=1, source_target_pairs={{0,2},{2,4},{4,6},{6,8},{8,10},{10,12},{12,14},{1,3},{3,5},{5,7},{... | collective-permute-start | bytes 124424 | tf_op jit(solution)/shard_map/ppermute | solution.py:16
  54.1 177.7 %collective-permute-start.3 = (f32[2,3,3,32,18,1]{3,0,5,4,2,1:T(2,128)}, f32[2,3,3,32,18,1]{3,0,5,4,2,1:T(2,128)}, u32[]{:S(2)}, u32[]{:S(2)}) collective-permute-start(f32[2,3,3,32,18,1]{3,0,5,4,2,1:T(2,128)} %copy.72), channel_id=1, source_target_pairs={{2,0},{4,2},{6,4},{8,6},{10,8},{12,10},{14,12},{3,1},{5,3},{7,5},{... | collective-permute-start | bytes 124424 | tf_op jit(solution)/shard_map/ppermute | solution.py:19
  417.2 21.8 %collective-permute-start.6 = (f32[32,1,128]{2,0,1:T(8,128)S(1)}, f32[32,1,128]{2,0,1:T(8,128)S(1)}, u32[]{:S(2)}, u32[]{:S(2)}) collective-permute-start(f32[32,1,128]{2,0,1:T(8,128)S(1)} %get-tuple-element.49), channel_id=1, source_target_pairs={{16,0},{32,16},{48,32},{64,48},{80,64},{96,80},{112,96},{128,112},... | collective-permute-start | bytes 49160 | tf_op jit(solution)/shard_map/ppermute | solution.py:19
  418.5 26.0 %slice-start = ((s8[5308416]{0:T(1024)(128)(4,1)}), s8[4194304]{0:T(1024)(128)(4,1)S(1)}, s32[]{:S(2)}) async-start(s8[5308416]{0:T(1024)(128)(4,1)} %bitcast.155), calls=%async_computation.5 | async-start | bytes 8388608
  418.5 26.0 %slice-start.2 = ((s8[5308416]{0:T(1024)(128)(4,1)}), s8[4194304]{0:T(1024)(128)(4,1)S(1)}, s32[]{:S(2)}) async-start(s8[5308416]{0:T(1024)(128)(4,1)} %bitcast.157), calls=%async_computation.7 | async-start | bytes 8388608
  418.5 26.0 %copy-start.1 = (f32[1,3,3,32,16,128]{5,3,4,2,1,0:T(8,128)S(1)}, f32[1,3,3,32,16,128]{5,3,4,2,1,0:T(8,128)}, u32[]{:S(2)}) copy-start(f32[1,3,3,32,16,128]{5,3,4,2,1,0:T(8,128)} %copy-done) | copy-start | bytes 7077892
  418.5 26.0 %slice-start.1 = ((s8[5308416]{0:T(1024)(128)(4,1)}), s8[1114112]{0:T(1024)(128)(4,1)S(1)}, s32[]{:S(2)}) async-start(s8[5308416]{0:T(1024)(128)(4,1)} %bitcast.155), calls=%async_computation.6 | async-start | bytes 2228224
  418.6 26.0 %slice-start.3 = ((s8[5308416]{0:T(1024)(128)(4,1)}), s8[1114112]{0:T(1024)(128)(4,1)S(1)}, s32[]{:S(2)}) async-start(s8[5308416]{0:T(1024)(128)(4,1)} %bitcast.157), calls=%async_computation.8 | async-start | bytes 2228224
  418.6 26.0 %copy-start.3 = (f32[2,3,3,32,1,128]{5,3,4,2,1,0:T(8,128)S(1)}, f32[2,3,3,32,1,128]{5,3,4,2,1,0:T(8,128)}, u32[]{:S(2)}) copy-start(f32[2,3,3,32,1,128]{5,3,4,2,1,0:T(8,128)} %copy-done.2) | copy-start | bytes 884740
  418.6 20.4 %collective-permute-start.7 = (f32[32,1,128]{2,0,1:T(8,128)S(1)}, f32[32,1,128]{2,0,1:T(8,128)S(1)}, u32[]{:S(2)}, u32[]{:S(2)}) collective-permute-start(f32[32,1,128]{2,0,1:T(8,128)S(1)} %get-tuple-element.48), channel_id=1, source_target_pairs={{0,16},{16,32},{32,48},{48,64},{64,80},{80,96},{96,112},{112,128},... | collective-permute-start | bytes 49160 | tf_op jit(solution)/shard_map/ppermute | solution.py:16
  429.6 14.9 %collective-permute-start.4 = (f32[2,3,3,1,18,130]{5,3,4,2,1,0:T(1,128)S(1)}, f32[2,3,3,1,18,130]{5,3,4,2,1,0:T(1,128)S(1)}, u32[]{:S(2)}, u32[]{:S(2)}) collective-permute-start(f32[2,3,3,1,18,130]{5,3,4,2,1,0:T(1,128)S(1)} %get-tuple-element.12), channel_id=1, source_target_pairs={{0,1},{2,3},{4,5},{6,7},{8,9},{10,11},{12,13},{14,15},{16,17},{18,... | collective-permute-start | bytes 505448 | tf_op jit(solution)/shard_map/ppermute | solution.py:16
  430.9 13.6 %collective-permute-start.5 = (f32[2,3,3,1,18,130]{5,3,4,2,1,0:T(1,128)S(1)}, f32[2,3,3,1,18,130]{5,3,4,2,1,0:T(1,128)S(1)}, u32[]{:S(2)}, u32[]{:S(2)}) collective-permute-start(f32[2,3,3,1,18,130]{5,3,4,2,1,0:T(1,128)S(1)} %get-tuple-element.13), channel_id=1, source_target_pairs={{1,0},{3,2},{5,4},{7,6},{9,8},{11,10},{13,12},{15,14},{17,16},{19,... | collective-permute-start | bytes 505448 | tf_op jit(solution)/shard_map/ppermute | solution.py:19
  439.2 23.1 %collective-permute-start.8 = (f32[32,18,1]{2,0,1:T(8,128)S(1)}, f32[32,18,1]{2,0,1:T(8,128)S(1)}, u32[]{:S(2)}, u32[]{:S(2)}) collective-permute-start(f32[32,18,1]{2,0,1:T(8,128)S(1)} %get-tuple-element.43), channel_id=1, source_target_pairs={{2,0},{4,2},{6,4},{8,6},{10,8},{12,10},{14,12},{3,1},{5,3},{7,5},{... | collective-permute-start | bytes 6920 | tf_op jit(solution)/shard_map/ppermute | solution.py:19
  440.5 21.8 %collective-permute-start.9 = (f32[32,18,1]{2,0,1:T(8,128)S(1)}, f32[32,18,1]{2,0,1:T(8,128)S(1)}, u32[]{:S(2)}, u32[]{:S(2)}) collective-permute-start(f32[32,18,1]{2,0,1:T(8,128)S(1)} %get-tuple-element.42), channel_id=1, source_target_pairs={{0,2},{2,4},{4,6},{6,8},{8,10},{10,12},{12,14},{1,3},{3,5},{5,7},{... | collective-permute-start | bytes 6920 | tf_op jit(solution)/shard_map/ppermute | solution.py:16
  462.3 2.0 copy-start.4
  462.3 2.0 copy-start.5
  462.5 12.2 %collective-permute-start.10 = (f32[1,18,130]{2,0,1:T(1,128)S(1)}, f32[1,18,130]{2,0,1:T(1,128)S(1)}, u32[]{:S(2)}, u32[]{:S(2)}) collective-permute-start(f32[1,18,130]{2,0,1:T(1,128)S(1)} %get-tuple-element.30), channel_id=1, source_target_pairs={{1,0},{3,2},{5,4},{7,6},{9,8},{11,10},{13,12},{15,14},{17,16},{19,... | collective-permute-start | bytes 28088 | tf_op jit(solution)/shard_map/ppermute | solution.py:19
  464.3 10.3 %collective-permute-start.11 = (f32[1,18,130]{2,0,1:T(1,128)S(1)}, f32[1,18,130]{2,0,1:T(1,128)S(1)}, u32[]{:S(2)}, u32[]{:S(2)}) collective-permute-start(f32[1,18,130]{2,0,1:T(1,128)S(1)} %get-tuple-element.31), channel_id=1, source_target_pairs={{0,1},{2,3},{4,5},{6,7},{8,9},{10,11},{12,13},{14,15},{16,17},{18,... | collective-permute-start | bytes 28088 | tf_op jit(solution)/shard_map/ppermute | solution.py:16
  477.8 5.4 collective-permute-start.12
  479.1 49.0 %copy-start.6 = (f32[3,32,16,128]{3,2,1,0:T(8,128)S(1)}, f32[3,32,16,128]{3,2,1,0:T(8,128)}, u32[]{:S(2)}) copy-start(f32[3,32,16,128]{3,2,1,0:T(8,128)} %param.11) | copy-start | bytes 2359300
  479.1 5.0 collective-permute-start.13
  484.2 8.2 %collective-permute-start.14 = (f32[32,18,1]{2,0,1:T(8,128)S(1)}, f32[32,18,1]{2,0,1:T(8,128)S(1)}, u32[]{:S(2)}, u32[]{:S(2)}) collective-permute-start(f32[32,18,1]{2,0,1:T(8,128)S(1)} %get-tuple-element.41), channel_id=1, source_target_pairs={{2,0},{4,2},{6,4},{8,6},{10,8},{12,10},{14,12},{3,1},{5,3},{7,5},{... | collective-permute-start | bytes 6920 | tf_op jit(solution)/shard_map/ppermute | solution.py:19
  485.5 7.6 %collective-permute-start.15 = (f32[32,18,1]{2,0,1:T(8,128)S(1)}, f32[32,18,1]{2,0,1:T(8,128)S(1)}, u32[]{:S(2)}, u32[]{:S(2)}) collective-permute-start(f32[32,18,1]{2,0,1:T(8,128)S(1)} %get-tuple-element.40), channel_id=1, source_target_pairs={{0,2},{2,4},{4,6},{6,8},{8,10},{10,12},{12,14},{1,3},{3,5},{5,7},{... | collective-permute-start | bytes 6920 | tf_op jit(solution)/shard_map/ppermute | solution.py:16
  493.4 6.8 %collective-permute-start.16 = (f32[1,18,130]{2,0,1:T(1,128)S(1)}, f32[1,18,130]{2,0,1:T(1,128)S(1)}, u32[]{:S(2)}, u32[]{:S(2)}) collective-permute-start(f32[1,18,130]{2,0,1:T(1,128)S(1)} %get-tuple-element.28), channel_id=1, source_target_pairs={{1,0},{3,2},{5,4},{7,6},{9,8},{11,10},{13,12},{15,14},{17,16},{19,... | collective-permute-start | bytes 28088 | tf_op jit(solution)/shard_map/ppermute | solution.py:19
  498.8 3.1 collective-permute-start.17
  504.7 5.7 collective-permute-start.18
  506.0 5.2 collective-permute-start.19
  511.4 10.5 %collective-permute-start.20 = (f32[32,18,1]{2,0,1:T(8,128)S(1)}, f32[32,18,1]{2,0,1:T(8,128)S(1)}, u32[]{:S(2)}, u32[]{:S(2)}) collective-permute-start(f32[32,18,1]{2,0,1:T(8,128)S(1)} %get-tuple-element.39), channel_id=1, source_target_pairs={{2,0},{4,2},{6,4},{8,6},{10,8},{12,10},{14,12},{3,1},{5,3},{7,5},{... | collective-permute-start | bytes 6920 | tf_op jit(solution)/shard_map/ppermute | solution.py:19
  512.7 10.1 %collective-permute-start.21 = (f32[32,18,1]{2,0,1:T(8,128)S(1)}, f32[32,18,1]{2,0,1:T(8,128)S(1)}, u32[]{:S(2)}, u32[]{:S(2)}) collective-permute-start(f32[32,18,1]{2,0,1:T(8,128)S(1)} %get-tuple-element.38), channel_id=1, source_target_pairs={{0,2},{2,4},{4,6},{6,8},{8,10},{10,12},{12,14},{1,3},{3,5},{5,7},{... | collective-permute-start | bytes 6920 | tf_op jit(solution)/shard_map/ppermute | solution.py:16
  523.0 5.2 collective-permute-start.22
  526.7 3.1 collective-permute-start.23
  532.7 22.2 %all-to-all-start = ((f32[32,16,128]{2,0,1:T(8,128)}), f32[32,16,128]{2,0,1:T(8,128)S(1)}, u32[]{:S(2)}, u32[]{:S(2)}) async-start(f32[32,16,128]{2,0,1:T(8,128)} %get-tuple-element.8), calls=%async_computation | async-start | bytes 524288 | tf_op jit(solution)/shard_map/all_to_all | solution.py:80
  561.3 28.9 %all-to-all-start.1 = ((f32[128,1,512]{2,1,0:T(1,128)}), f32[128,1,512]{2,1,0:T(1,128)S(1)}, u32[]{:S(2)}, u32[]{:S(2)}) async-start(f32[128,1,512]{2,1,0:T(1,128)} %reshape.198), calls=%async_computation.1 | async-start | bytes 524288 | tf_op jit(solution)/shard_map/all_to_all | solution.py:92
Sparse Core Ops, SparseCore 0:
  14.1 213.2 all-reduce.4
  231.1 112.2 all-gather.3
where the time goes:
time: 620 us; the launch traced here: 619 us
  waiting for transfers between devices  328 us (53%)
  other arithmetic  109 us (18%)
  starting transfers between devices  92.9 us (15%)
  local copies, waits for them, and re-layouts  61 us (10%)
  between operations  15.4 us (2%)
  matrix products  6.64 us (1%)
    unnamed x3, waiting for transfers between devices  173 us
    all_gather x1, waiting for transfers between devices, per_device(): lax.all_gather(well_sources, ('gx', 'gy'), axis=0, tiled=True)  107 us
    scatter-add x1, other arithmetic, per_device(): landed = jnp.zeros((brick_z, columns), jnp.float32).at[:, target].add(jnp...  67 us
    ppermute x12, starting transfers between devices, with_halo(): lax.ppermute(lax.slice_in_dim(block, block.shape[dim] - width, None, axis...  38.6 us
    ppermute x12, starting transfers between devices, with_halo(): lax.ppermute(lax.slice_in_dim(block, 0, width, axis=dim), axis, backward)  29.5 us
    concatenate x5, other arithmetic, with_halo(): block = jnp.concatenate([low, block, high], axis=dim)  20.4 us
    all_to_all x1, starting transfers between devices, per_device(): lax.all_to_all(smooth_y, ('gx', 'gy'), split_axis=0, concat_axis=1, tiled...  14.9 us
    unnamed x36, local copies, waits for them, and re-layouts  13.7 us
  transfers between devices with their start and end apart: 28, of which 14 were waited for; matrix products, arithmetic and copies ran while one was open for 11% of the time, Pallas kernels for 0%

commit v1 on v0

v1 whole, which is shorter than its diff:
```python
import functools
import math

import jax
import jax.numpy as jnp
from jax import lax
from jax.experimental import pallas as pl
from jax.experimental.pallas import tpu as pltpu
from jax.sharding import PartitionSpec as P

F32 = jnp.float32
BF16 = jnp.bfloat16
CAP = 2


def iota(shape, dim):
    return lax.broadcasted_iota(jnp.int32, shape, dim)


def thirds(value):
    high = value.astype(BF16)
    left = value - high.astype(F32)
    middle = left.astype(BF16)
    low = (left - middle.astype(F32)).astype(BF16)
    return high, middle, low


def halves(value):
    high = value.astype(BF16)
    return high, (value - high.astype(F32)).astype(BF16)


def dot(left, right, dims):
    return lax.dot_general(left, right, (dims, ((), ())), preferred_element_type=F32)


def dot3(left, right, dims):
    lh, ll = halves(left)
    rh, rl = halves(right)
    return dot(lh, rh, dims) + (dot(lh, rl, dims) + dot(ll, rh, dims))


def dispatch_kernel(place_ref, sources_ref, owner_ref, cell_ref, out_ref):
    wells, depth = sources_ref.shape
    chunks, lanes = out_ref.shape
    half = lanes // CAP
    owner = owner_ref[...]
    owner_row = owner.astype(F32)
    owner_col = jnp.transpose(jnp.broadcast_to(owner_row, (8, wells)))[:, :1]
    earlier = iota((wells, wells), 0) < iota((wells, wells), 1)
    same = (owner_col == owner_row) & earlier
    rank = jnp.sum(same.astype(F32), axis=0, keepdims=True)
    target = (2 * owner + place_ref[2]).astype(F32)
    row = iota((chunks, wells), 0).astype(F32)
    cell_col = jnp.transpose(jnp.broadcast_to(cell_ref[...].astype(F32), (8, wells)))[:, :1]
    total = jnp.zeros((chunks, lanes), F32)
    payload = jnp.concatenate(
        [sources_ref[...], jnp.broadcast_to(cell_col, (wells, half - depth))], axis=1
    )
    blank = jnp.zeros((wells, half), F32)
    for slot in range(CAP):
        chosen = jnp.where((row == target) & (rank == float(slot)), 1.0, 0.0).astype(BF16)
        parts = [blank] * CAP
        parts[slot] = payload
        for piece in thirds(jnp.concatenate(parts, axis=1)):
            total = total + dot(chosen, piece, ((1,), (0,)))
    out_ref[...] = total


def landing(received_ref, depth, rows, lanes):
    pairs = received_ref.shape[0] // 2
    half = received_ref.shape[1] // CAP
    across = rows // depth
    received = received_ref[pl.ds(0, pairs, stride=2), :] + received_ref[pl.ds(1, pairs, stride=2), :]
    landed = jnp.zeros((rows, lanes), F32)
    pieces = thirds(received)
    for slot in range(CAP):
        cell = received[:, slot * half + depth : slot * half + depth + 1].astype(jnp.int32)
        spread = jnp.where(
            iota((2 * half, rows), 0) == slot * half + iota((2 * half, rows), 1) // across, 1.0, 0.0
        ).astype(BF16)
        at_x = iota((pairs, rows), 1) % across == cell // lanes
        at_y = jnp.where(iota((pairs, lanes), 1) == cell % lanes, 1.0, 0.0).astype(BF16)
        for piece in reversed(pieces):
            wide = jnp.where(at_x, dot(piece, spread, ((1,), (0,))), 0.0).astype(BF16)
            landed = landed + dot(wide, at_y, ((0,), (0,)))
    return landed


def spread_step(place_ref, adjoint, courant_ref, sign_ref, depth, faces):
    rows, lanes = adjoint.shape
    across = rows // depth
    xe_ref, xo_ref, ye_ref, yo_ref, z_ref = faces
    gx, gy, gz = place_ref[0], place_ref[1], place_ref[2]
    sign = sign_ref[0]
    row_x = iota((rows, lanes), 0) % across
    lane = iota((rows, lanes), 1)
    flow = [courant_ref[axis] * adjoint for axis in range(3)]
    rising = [jnp.where((sign & (1 << axis)) != 0, flow[axis], 0.0) for axis in range(3)]
    falling = [flow[axis] - rising[axis] for axis in range(3)]
    up = jnp.where(row_x == across - 1, 0.0, pltpu.roll(rising[0], rows - 1, 0))
    down = jnp.where(row_x == 0, 0.0, pltpu.roll(falling[0], 1, 0))
    rise3 = rising[0].reshape(depth, across, lanes)
    fall3 = falling[0].reshape(depth, across, lanes)
    low, high = rise3[:, 0, :], fall3[:, across - 1, :]
    even = (gx % 2) == 0
    xe_ref[...] = jnp.where(even, high, low)
    xo_ref[...] = jnp.where(even, low, high)
    staying = 1.0 - (courant_ref[0] + courant_ref[1] + courant_ref[2])
    kept = staying * adjoint + up + down
    up = jnp.where(lane == lanes - 1, 0.0, pltpu.roll(rising[1], lanes - 1, 1))
    down = jnp.where(lane == 0, 0.0, pltpu.roll(falling[1], 1, 1))
    ends = jnp.transpose(jnp.where(lane == 0, rising[1], falling[1]))
    low, high = ends[0:1, :], ends[lanes - 1 : lanes, :]
    even = (gy % 2) == 0
    ye_ref[...] = jnp.where(even, high, low)
    yo_ref[...] = jnp.where(even, low, high)
    kept = kept + up + down
    blank = jnp.zeros((across, lanes), F32)
    z_ref[...] = jnp.where(gz == 0, falling[2][rows - across :, :], rising[2][:across, :])
    kept = (
        kept
        + jnp.concatenate([rising[2][across:, :], blank], axis=0)
        + jnp.concatenate([blank, falling[2][: rows - across, :]], axis=0)
    )
    return kept


def first_kernel(place_ref, received_ref, courant_ref, sign_ref, kept_ref, *faces):
    rows, lanes = kept_ref.shape
    depth = faces[0].shape[0]
    adjoint = landing(received_ref, depth, rows, lanes)
    kept_ref[...] = spread_step(place_ref, adjoint, courant_ref, sign_ref, depth, faces)


def join(place_ref, kept_ref, xe_ref, xo_ref, ye_ref, yo_ref, z_ref, sizes):
    rows, lanes = kept_ref.shape
    depth = xe_ref.shape[0]
    across = rows // depth
    gx, gy, gz = place_ref[0], place_ref[1], place_ref[2]
    even = (gx % 2) == 0
    xe, xo = xe_ref[...], xo_ref[...]
    above = jnp.where(gx == sizes[0] - 1, 0.0, jnp.where(even, xe, xo))
    below = jnp.where(gx == 0, 0.0, jnp.where(even, xo, xe))
    row_x = iota((depth, across, lanes), 1)
    adjoint = kept_ref[...] + jnp.where(
        row_x == across - 1,
        above[:, None, :],
        jnp.where(row_x == 0, below[:, None, :], 0.0),
    ).reshape(rows, lanes)
    even = (gy % 2) == 0
    ye, yo = ye_ref[...], yo_ref[...]
    above = jnp.where(gy == sizes[1] - 1, 0.0, jnp.where(even, ye, yo))
    below = jnp.where(gy == 0, 0.0, jnp.where(even, yo, ye))
    row_y = iota((lanes, rows), 0)
    adjoint = adjoint + jnp.transpose(
        jnp.where(row_y == lanes - 1, above, jnp.where(row_y == 0, below, 0.0))
    )
    z = z_ref[...]
    blank = jnp.zeros((rows - across, lanes), F32)
    adjoint = adjoint + jnp.where(
        gz == 0,
        jnp.concatenate([blank, z], axis=0),
        jnp.concatenate([z, blank], axis=0),
    )
    return adjoint


def middle_kernel(
    sizes, has_gradient, place_ref, kept_ref, xe, xo, ye, yo, z, courant_ref, sign_ref, tracer_ref, *rest
):
    gradient_in = None
    if has_gradient:
        gradient_in, *rest = rest
    kept_out, gradient_ref, *faces = rest
    adjoint = join(place_ref, kept_ref, xe, xo, ye, yo, z, sizes)
    kept_out[...] = spread_step(place_ref, adjoint, courant_ref, sign_ref, xe.shape[0], faces)
    gradient = adjoint * tracer_ref[0]
    gradient_ref[...] = gradient + gradient_in[...] if has_gradient else gradient


def last_kernel(
    sizes, place_ref, kept_ref, xe, xo, ye, yo, z, tracer_ref, gradient_in, adjoint_ref, lines_ref, work_ref
):
    rows = kept_ref.shape[0]
    depth = xe.shape[0]
    across = rows // depth
    adjoint = join(place_ref, kept_ref, xe, xo, ye, yo, z, sizes)
    adjoint_ref[...] = adjoint
    work_ref[...] = gradient_in[...] + adjoint * tracer_ref[0]
    for x in range(across):
        lines_ref[x * depth : (x + 1) * depth, :] = work_ref[pl.ds(x, depth, stride=across), :]


def smooth_y_kernel(depth, length, rows_each, lines_ref, out_ref):
    rows, lanes = lines_ref.shape
    lines = lines_ref[...]
    share = 2 * depth
    groups = lanes // rows_each
    scale = 1.0 / math.sqrt(length)
    order = iota((lanes, lanes), 0)
    y_out = (order % groups) * rows_each + order // groups
    table = jnp.exp(-jnp.abs(y_out - iota((lanes, lanes), 1)).astype(F32) / length) * scale
    side = iota((8, lanes), 0)
    y_in = iota((8, lanes), 1)
    carry_table = jnp.exp(-jnp.where(side == 0, lanes - 1 - y_in, y_in).astype(F32) / length) * scale
    both = dot3(jnp.concatenate([table, carry_table], axis=0), lines, ((1,), (1,)))
    result, carry = both[:lanes], both[lanes:]
    place = iota((8, rows), 1)
    decay = math.exp(-lanes / length)
    right = carry
    left = carry
    step = share
    factor = decay
    while step < rows:
        right = right + factor * jnp.where(place >= step, pltpu.roll(right, step, 1), 0.0)
        left = left + factor * jnp.where(place < rows - step, pltpu.roll(left, rows - step, 1), 0.0)
        step, factor = 2 * step, factor * factor
    right = jnp.where(place >= share, pltpu.roll(right, share, 1), 0.0)[0:1, :]
    left = jnp.where(place < rows - share, pltpu.roll(left, rows - share, 1), 0.0)[1:2, :]
    row = iota((lanes, 1), 0)
    y_row = ((row % groups) * rows_each + row // groups).astype(F32)
    result = (
        result + jnp.exp(-(y_row + 1.0) / length) * right + jnp.exp(-(lanes - y_row) / length) * left
    )
    per_tile = lanes // depth
    quarter = iota((groups, lanes), 1) // depth
    for tile in range(rows // lanes):
        pieces = [
            result[r * groups : (r + 1) * groups, tile * lanes : (tile + 1) * lanes]
            for r in range(rows_each)
        ]
        for u in range(per_tile):
            line = tile * per_tile + u
            block, xx = line // 2, line % 2
            chunk = jnp.zeros((groups, lanes), F32)
            for r in range(rows_each):
                turn = ((r - u) * depth) % lanes
                piece = pltpu.roll(pieces[r], turn, 1) if turn else pieces[r]
                chunk = jnp.where(quarter == r, piece, chunk)
            out_ref[pl.ds(block * 2 * groups + xx, groups, stride=2), :] = chunk


def smooth_xz_kernel(depth, length_x, length_z, rows_each, data_ref, out_ref):
    rows, lanes = data_ref.shape
    full_x = out_ref.shape[1]
    sources = rows // 4
    part = [jnp.zeros((lanes, full_x), F32) for _ in range(2)]
    for xx in range(2):
        x_in = 2 * iota((sources, full_x), 0) + xx
        table = jnp.exp(-jnp.abs(x_in - iota((sources, full_x), 1)).astype(F32) / length_x)
        table = table * (1.0 / math.sqrt(length_x))
        for g in range(2):
            block = data_ref[pl.ds(2 * g + xx, sources, stride=4), :]
            part[g] = part[g] + dot3(block, table, ((0,), (0,)))
    full_z = 2 * depth
    total = None
    for g in range(2):
        r_out, z_out = iota((rows_each * full_z, lanes), 0) // full_z, iota((rows_each * full_z, lanes), 0) % full_z
        r_in, z_in = iota((rows_each * full_z, lanes), 1) // depth, iota((rows_each * full_z, lanes), 1) % depth
        table = jnp.exp(-jnp.abs(z_out - z_in - g * depth).astype(F32) / length_z) * (1.0 / math.sqrt(length_z))
        table = jnp.where(r_out == r_in, table, 0.0)
        term = dot3(table, part[g], ((1,), (0,)))
        total = term if total is None else total + term
    out_ref[...] = total


def pair_swaps(count):
    even = [(i, i ^ 1) for i in range(count)]
    odd = [(i, (i + 1) % count) for i in range(1, count, 2)]
    odd = odd + [(target, source) for source, target in odd]
    return even, odd


def exchange(faces):
    xe, xo, ye, yo, z = faces
    x_even, x_odd = pair_swaps(lax.axis_size("gx"))
    y_even, y_odd = pair_swaps(lax.axis_size("gy"))
    return (
        lax.ppermute(xe, "gx", x_even),
        lax.ppermute(xo, "gx", x_odd),
        lax.ppermute(ye, "gy", y_even),
        lax.ppermute(yo, "gy", y_odd),
        lax.ppermute(z, "gz", [(0, 1), (1, 0)]),
    )


def per_device(well_sources, well_owner, well_cell, flow_sign, courant, tracer):
    steps, brick_z, brick_x, brick_y = flow_sign.shape
    wells = well_sources.shape[0]
    rows = brick_z * brick_x
    sizes = (lax.axis_size("gx"), lax.axis_size("gy"), lax.axis_size("gz"))
    devices = sizes[0] * sizes[1] * sizes[2]
    place = jnp.stack([lax.axis_index("gx"), lax.axis_index("gy"), lax.axis_index("gz")])
    axes = ("gx", "gy", "gz")
    smem = pl.BlockSpec(memory_space=pltpu.SMEM)
    vmem = pl.BlockSpec(memory_space=pltpu.VMEM)

    def shape(*dims):
        return jax.ShapeDtypeStruct(dims, F32)

    def step_spec(step):
        return pl.BlockSpec((1, rows, brick_y), lambda i, step=step: (step, 0, 0))

    def whole(*dims):
        return pl.BlockSpec(dims, lambda i: (0,) * len(dims))

    outgoing = pl.pallas_call(
        dispatch_kernel,
        in_specs=[smem, vmem, vmem, vmem],
        out_specs=vmem,
        out_shape=shape(devices, 128),
        name="dispatch",
    )(place, well_sources, well_owner.reshape(1, wells), well_cell.reshape(1, wells))
    received = lax.all_to_all(outgoing, axes, split_axis=0, concat_axis=0, tiled=True)

    flow = flow_sign.reshape(steps, rows, brick_y)
    speed = courant.reshape(3, rows, brick_y)
    trace = tracer.reshape(steps, rows, brick_y)
    face_shapes = [
        shape(brick_z, brick_y),
        shape(brick_z, brick_y),
        shape(1, rows),
        shape(1, rows),
        shape(brick_x, brick_y),
    ]
    face_specs = [whole(*f.shape) for f in face_shapes]
    field = whole(rows, brick_y)
    speed_spec = whole(3, rows, brick_y)
    kept, *faces = pl.pallas_call(
        first_kernel,
        grid=(1,),
        in_specs=[smem, whole(devices, 128), speed_spec, step_spec(steps - 1)],
        out_specs=[field] + face_specs,
        out_shape=[shape(rows, brick_y)] + face_shapes,
        name="first",
    )(place, received, speed, flow)
    gradient = []
    for step in reversed(range(1, steps)):
        arrived = exchange(faces)
        kept, grown, *faces = pl.pallas_call(
            functools.partial(middle_kernel, sizes, bool(gradient)),
            grid=(1,),
            in_specs=[smem, field] + face_specs + [speed_spec, step_spec(step - 1), step_spec(step)]
            + [field] * len(gradient),
            out_specs=[field, field] + face_specs,
            out_shape=[shape(rows, brick_y)] * 2 + face_shapes,
            name=f"step{step}",
        )(place, kept, *arrived, speed, flow, trace, *gradient)
        gradient = [grown]
    arrived = exchange(faces)
    adjoint, lines = pl.pallas_call(
        functools.partial(last_kernel, sizes),
        grid=(1,),
        in_specs=[smem, field] + face_specs + [step_spec(0), field],
        out_specs=[field, field],
        out_shape=[shape(rows, brick_y)] * 2,
        scratch_shapes=[pltpu.VMEM((rows, brick_y), F32)],
        name="step0",
    )(place, kept, *arrived, trace, *gradient)

    y_lines = lax.all_to_all(
        lines.reshape(sizes[1], rows // sizes[1], brick_y), "gy", split_axis=0, concat_axis=0, tiled=True
    ).reshape(rows, brick_y)
    rows_each = sizes[1] * brick_y // devices
    smooth = pl.pallas_call(
        functools.partial(smooth_y_kernel, brick_z, 2.0 * brick_y, rows_each),
        in_specs=[vmem],
        out_specs=vmem,
        out_shape=shape(rows, brick_y),
        name="smooth_y",
    )(y_lines)
    planes = lax.all_to_all(
        smooth.reshape(devices, 2, 128), axes, split_axis=0, concat_axis=0, tiled=True
    ).reshape(rows, brick_y)
    full_x, full_z = sizes[0] * brick_x, sizes[2] * brick_z
    smoothed = pl.pallas_call(
        functools.partial(smooth_xz_kernel, brick_z, 2.0 * brick_x, 2.0 * brick_z, rows_each),
        in_specs=[vmem],
        out_specs=vmem,
        out_shape=shape(rows_each * full_z, full_x),
        name="smooth_xz",
    )(planes)
    return (
        adjoint.reshape(brick_z, brick_x, brick_y),
        smoothed.reshape(rows_each, full_z, full_x),
    )


def solution(mesh):
    return jax.shard_map(
        per_device,
        mesh=mesh,
        in_specs=(
            P(("gx", "gy"), "gz"),
            P(("gx", "gy"), None),
            P(("gx", "gy")),
            P(None, "gz", "gx", "gy"),
            P(None, "gz", "gx", "gy"),
            P(None, "gz", "gx", "gy"),
        ),
        out_specs=(P("gz", "gx", "gy"), P(("gx", "gy", "gz"), None, None)),
        check_vma=False,
    )
```

time: 620 us -> 115 us (0.19)
  waiting for transfers between devices: 328 us -> 10.3 us
  other arithmetic: 109 us -> 0.59 us
  starting transfers between devices: 92.9 us -> 14.1 us
  blocking collectives: 5.63 us -> 68.5 us
  local copies, waits for them, and re-layouts: 61 us -> 3.2 us
  Pallas kernels: 0 us -> 17 us
  between operations: 15.4 us -> 0.83 us
  matrix products: 6.64 us -> 0 us
    unnamed x3 -> x0, waiting for transfers between devices: 173 us -> none
    all_gather x1 -> x0, waiting for transfers between devices: 107 us -> none  [per_device(): lax.all_gather(well_sources, ('gx', 'gy'), axis=0, tiled=True)]
    scatter-add x1 -> x0, other arithmetic: 67 us -> none  [per_device(): landed = jnp.zeros((brick_z, columns), jnp.float32).at[:, target].add(jnp...]
    all_to_all x1 -> x3, blocking collectives: 5.63 us -> 68.5 us  [the longest x1 29.3 us: per_device(): lax.all_to_all(outgoing, axes, split_axis=0, concat_axis=0, tiled=True)]
    ppermute x24 -> x15, starting transfers between devices: 68 us -> 14.1 us  [the longest x3 6.57 us: exchange(): lax.ppermute(xo, 'gx', x_odd)]
    all_to_all x2 -> x0, waiting for transfers between devices: 25.3 us -> none  [the longest x1 13.1 us: per_device(): lax.all_to_all(smooth_y, ('gx', 'gy'), split_axis=0, concat_axis=1, tiled...]
    all_to_all x2 -> x0, starting transfers between devices: 24.8 us -> none  [the longest x1 14.9 us: per_device(): lax.all_to_all(smooth_y, ('gx', 'gy'), split_axis=0, concat_axis=1, tiled...]
    concatenate x5 -> x0, other arithmetic: 20.4 us -> none  [with_halo(): block = jnp.concatenate([low, block, high], axis=dim)]
  transfers between devices with their start and end apart: 28 -> 15, of which waited for: 14 -> 6; matrix products, arithmetic and copies ran while one was open for 11% -> 0% of each run, Pallas kernels for 0% -> 0%
where the time goes in v1:
time: 115 us
  blocking collectives  68.5 us (60%)
  Pallas kernels  17 us (15%)
  starting transfers between devices  14.1 us (12%)
  waiting for transfers between devices  10.3 us (9%)
  local copies, waits for them, and re-layouts  3.2 us (3%)
    all_to_all x1, blocking collectives, per_device(): lax.all_to_all(outgoing, axes, split_axis=0, concat_axis=0, tiled=True)  29.3 us
    all_to_all x1, blocking collectives, per_device(): lax.all_to_all(smooth.reshape(devices, 2, 128), axes, split_axis=0, conca...  24.9 us
    all_to_all x1, blocking collectives, per_device(): lax.all_to_all(lines.reshape(sizes[1], rows // sizes[1], brick_y), 'gy',...  14.3 us
    ppermute x3, starting transfers between devices, exchange(): lax.ppermute(xo, 'gx', x_odd)  6.57 us
    ppermute x3, waiting for transfers between devices, exchange(): lax.ppermute(ye, 'gy', y_even)  5.26 us
    pallas_call x2, Pallas kernels, per_device(): pl.pallas_call(functools.partial(middle_kernel, sizes, bool(gradient)), g...  5.18 us
    ppermute x3, waiting for transfers between devices, exchange(): lax.ppermute(yo, 'gy', y_odd)  5 us
    ppermute x3, starting transfers between devices, exchange(): lax.ppermute(z, 'gz', [(0, 1), (1, 0)])  4.7 us
  transfers between devices with their start and end apart: 15, of which 6 were waited for; matrix products, arithmetic and copies ran while one was open for 0% of the time, Pallas kernels for 0%

profile of v1, /device:TPU:1, one launch (start us, length us, event | category | flops | bytes accessed | tf_op | source)
XLA Modules:
  0.0 114.5 jit_solution(10298796878435881376)
XLA Ops:
  0.6 0.0 copy-start.6
  0.6 0.7 copy-done.6
  1.3 0.7 copy.9.sources_ref
  2.1 0.6 pad_add_fusion.place_ref
  2.7 1.9 %dispatch.1 = f32[256,128]{1,0:T(8,128)} custom-call(s32[3]{0:T(128)} %pad_add_fusion.place_ref, f32[96,32]{1,0:T(8,128)} %copy.9.sources_ref, s32[1,96]{1,0:T(1,128)} %bitcast.34, s32[1,96]{1,0:T(1,128)} %bitcast.35), custom_call_target="tpu_custom_call" | custom-call | tf_op jit(solution)/shard_map/dispatch/pallas_call | solution.py:308
  4.6 29.3 %all_to_all.21 = f32[256,1,128]{2,1,0:T(1,128)} all-to-all(f32[256,1,128]{2,1,0:T(1,128)} %bitcast.31), channel_id=1, replica_groups=mesh['gx'=16,'gy'=8,'gz'=2] {'gx','gy','gz'}, dimensions={0} | all-to-all | bytes 262144 | tf_op jit(solution)/shard_map/all_to_all | solution.py:315
  33.9 2.9 %first.1 = (f32[512,128]{1,0:T(8,128)}, f32[32,128]{1,0:T(8,128)}, f32[32,128]{1,0:T(8,128)}, f32[1,512]{1,0:T(1,128)}, f32[1,512]{1,0:T(1,128)}, /*index=5*/f32[16,128]{1,0:T(8,128)}) custom-call(s32[3]{0:T(128)} %pad_add_fusion.place_ref, f32[256,128]{1,0:T(8,128)} %bitcast.30, f32[3,512,128]{2,1,0:T(8,128)} %bitcast.18, s32[3,512,128]{2,1,0:T(8,128)} %bitcast.21), custom_call_target="tpu_custom_call" | custom-call | tf_op jit(solution)/shard_map/first/pallas_call | solution.py:330
  36.8 0.0 collective-permute-start
  36.9 0.0 copy-start.21
  36.9 0.7 collective-permute-start.1
  37.5 1.3 %collective-permute-start.4 = (f32[16,128]{1,0:T(8,128)}, f32[16,128]{1,0:T(8,128)S(1)}, u32[]{:S(2)}, u32[]{:S(2)}) collective-permute-start(f32[16,128]{1,0:T(8,128)} %get-tuple-element.29), channel_id=1, source_target_pairs={{0,1},{1,0},{2,3},{3,2},{4,5},{5,4},{6,7},{7,6},{8,9},{9,8},{10,11... | collective-permute-start | bytes 24584 | tf_op jit(solution)/shard_map/ppermute | solution.py:284
  38.9 0.0 copy-done.21
  38.9 0.7 collective-permute-start.2
  39.6 0.0 copy-done.20
  39.6 0.9 collective-permute-start.3
  40.6 0.7 collective-permute-done.2.ye
  41.3 1.9 %collective-permute-done.3.yo = f32[1,512]{1,0:T(1,128)S(1)} collective-permute-done((f32[1,512]{1,0:T(1,128)S(1)}, f32[1,512]{1,0:T(1,128)S(1)}, u32[]{:S(2)}, u32[]{:S(2)}) %collective-permute-start.3) | collective-permute-done | bytes 2080 | tf_op jit(solution)/shard_map/ppermute | solution.py:283
  43.3 0.0 collective-permute-done.4.z
  43.3 0.0 collective-permute-done.xe
  43.3 0.0 copy-start.1
  43.3 0.0 collective-permute-done.1.xo
  43.3 0.0 copy-start.3
  43.3 0.5 copy-done.15
  43.9 0.0 copy-done.8
  43.9 0.0 copy-done.1
  43.9 0.0 copy-done.3
  43.9 2.5 %step2.1 = (f32[512,128]{1,0:T(8,128)}, f32[512,128]{1,0:T(8,128)}, f32[32,128]{1,0:T(8,128)}, f32[32,128]{1,0:T(8,128)}, f32[1,512]{1,0:T(1,128)}, /*index=5*/f32[1,512]{1,0:T(1,128)}, f32[16,128]{1,0:T(8,128)}) custom-call(s32[3]{0:T(128)} %pad_add_fusion.place_ref, f32[512,128]{1,0:T(8,128)} %get-tuple-element.24.kept_ref, f32[32,128]{1,0:T(8,128)} %copy-done.1, ...), custom_call_target="tpu_custom_call" | custom-call | tf_op jit(solution)/shard_map/step2/pallas_call | solution.py:341
  46.4 0.4 collective-permute-start.5
  46.8 3.8 %collective-permute-start.6 = (f32[32,128]{1,0:T(8,128)}, f32[32,128]{1,0:T(8,128)S(1)}, u32[]{:S(2)}, u32[]{:S(2)}) collective-permute-start(f32[32,128]{1,0:T(8,128)} %get-tuple-element.32), channel_id=1, source_target_pairs={{16,32},{48,64},{80,96},{112,128},{144,160},{176,192},{208,224},{2... | collective-permute-start | bytes 49160 | tf_op jit(solution)/shard_map/ppermute | solution.py:281
  50.7 1.8 %collective-permute-start.9 = (f32[16,128]{1,0:T(8,128)}, f32[16,128]{1,0:T(8,128)S(1)}, u32[]{:S(2)}, u32[]{:S(2)}) collective-permute-start(f32[16,128]{1,0:T(8,128)} %get-tuple-element.35), channel_id=1, source_target_pairs={{0,1},{1,0},{2,3},{3,2},{4,5},{5,4},{6,7},{7,6},{8,9},{9,8},{10,11... | collective-permute-start | bytes 24584 | tf_op jit(solution)/shard_map/ppermute | solution.py:284
  52.5 0.0 collective-permute-start.7
  52.5 0.1 collective-permute-start.8
  52.6 2.6 %collective-permute-done.7.ye = f32[1,512]{1,0:T(1,128)S(1)} collective-permute-done((f32[1,512]{1,0:T(1,128)S(1)}, f32[1,512]{1,0:T(1,128)S(1)}, u32[]{:S(2)}, u32[]{:S(2)}) %collective-permute-start.7) | collective-permute-done | bytes 2080 | tf_op jit(solution)/shard_map/ppermute | solution.py:282
  55.2 1.0 collective-permute-done.8.yo
  56.2 0.0 collective-permute-done.9.z
  56.2 0.0 collective-permute-done.5.xe
  56.2 0.0 copy-start
  56.2 0.0 collective-permute-done.6.xo
  56.3 0.5 copy-done.11
  56.8 0.0 copy-done.7
  56.8 0.0 copy-done
  56.8 0.0 copy-done.2
  56.9 2.6 %step1.1 = (f32[512,128]{1,0:T(8,128)}, f32[512,128]{1,0:T(8,128)}, f32[32,128]{1,0:T(8,128)}, f32[32,128]{1,0:T(8,128)}, f32[1,512]{1,0:T(1,128)}, /*index=5*/f32[1,512]{1,0:T(1,128)}, f32[16,128]{1,0:T(8,128)}) custom-call(s32[3]{0:T(128)} %pad_add_fusion.place_ref, f32[512,128]{1,0:T(8,128)} %get-tuple-element.30.kept_ref, f32[32,128]{1,0:T(8,128)} %copy-done, ...), custom_call_target="tpu_custom_call" | custom-call | tf_op jit(solution)/shard_map/step1/pallas_call | solution.py:341
  59.5 0.1 collective-permute-start.10
  59.6 2.1 %collective-permute-start.11 = (f32[32,128]{1,0:T(8,128)}, f32[32,128]{1,0:T(8,128)S(1)}, u32[]{:S(2)}, u32[]{:S(2)}) collective-permute-start(f32[32,128]{1,0:T(8,128)} %get-tuple-element.39), channel_id=1, source_target_pairs={{16,32},{48,64},{80,96},{112,128},{144,160},{176,192},{208,224},{2... | collective-permute-start | bytes 49160 | tf_op jit(solution)/shard_map/ppermute | solution.py:281
  61.7 1.6 %collective-permute-start.14 = (f32[16,128]{1,0:T(8,128)}, f32[16,128]{1,0:T(8,128)S(1)}, u32[]{:S(2)}, u32[]{:S(2)}) collective-permute-start(f32[16,128]{1,0:T(8,128)} %get-tuple-element.42), channel_id=1, source_target_pairs={{0,1},{1,0},{2,3},{3,2},{4,5},{5,4},{6,7},{7,6},{8,9},{9,8},{10,11... | collective-permute-start | bytes 24584 | tf_op jit(solution)/shard_map/ppermute | solution.py:284
  63.2 0.5 collective-permute-start.12
  63.8 0.0 collective-permute-start.13
  63.8 1.9 %collective-permute-done.12.ye = f32[1,512]{1,0:T(1,128)S(1)} collective-permute-done((f32[1,512]{1,0:T(1,128)S(1)}, f32[1,512]{1,0:T(1,128)S(1)}, u32[]{:S(2)}, u32[]{:S(2)}) %collective-permute-start.12) | collective-permute-done | bytes 2080 | tf_op jit(solution)/shard_map/ppermute | solution.py:282
  65.7 2.0 %collective-permute-done.13.yo = f32[1,512]{1,0:T(1,128)S(1)} collective-permute-done((f32[1,512]{1,0:T(1,128)S(1)}, f32[1,512]{1,0:T(1,128)S(1)}, u32[]{:S(2)}, u32[]{:S(2)}) %collective-permute-start.13) | collective-permute-done | bytes 2080 | tf_op jit(solution)/shard_map/ppermute | solution.py:283
  67.7 0.0 collective-permute-done.14.z
  67.7 0.0 collective-permute-done.10.xe
  67.7 0.0 collective-permute-done.11.xo
  67.8 0.0 copy-start.5
  67.8 0.0 copy-done.12
  67.8 0.5 copy-done.13
  68.3 0.0 copy-done.9
  68.3 0.0 copy-done.4
  68.3 0.0 copy-done.5
  68.4 2.2 %step0.1 = (f32[512,128]{1,0:T(8,128)}, f32[512,128]{1,0:T(8,128)}) custom-call(s32[3]{0:T(128)} %pad_add_fusion.place_ref, f32[512,128]{1,0:T(8,128)} %get-tuple-element.37.kept_ref, f32[32,128]{1,0:T(8,128)} %copy-done.4, f32[32,128]{1,0:T(8,128)} %copy-done.5, f32[1,512]{1,0:T(1,128)} %copy-done.12, f32[1,512]{1,0:T(1,128)} %copy-done.13, ...), custom_call_target="tpu_custom_call" | custom-call | tf_op jit(solution)/shard_map/step0/pallas_call | solution.py:352
  70.5 14.3 %all_to_all.22 = f32[8,64,128]{2,1,0:T(8,128)} all-to-all(f32[8,64,128]{2,1,0:T(8,128)} %bitcast.32), channel_id=1, replica_groups=mesh['gx'=16,'gy'=8,'gz'=2] {'gy'}, dimensions={0} | all-to-all | bytes 524288 | tf_op jit(solution)/shard_map/all_to_all | solution.py:362
  84.8 2.4 %smooth_y.1 = f32[512,128]{1,0:T(8,128)} custom-call(f32[512,128]{1,0:T(8,128)} %bitcast.27), custom_call_target="tpu_custom_call" | custom-call | tf_op jit(solution)/shard_map/smooth_y/pallas_call | solution.py:366
  87.2 24.9 %all_to_all.23 = f32[256,2,128]{2,1,0:T(2,128)} all-to-all(f32[256,2,128]{2,1,0:T(2,128)} %bitcast.28), channel_id=1, replica_groups=mesh['gx'=16,'gy'=8,'gz'=2] {'gx','gy','gz'}, dimensions={0} | all-to-all | bytes 524288 | tf_op jit(solution)/shard_map/all_to_all | solution.py:373
  112.1 2.4 %smooth_xz.1 = f32[256,256]{1,0:T(8,128)} custom-call(f32[512,128]{1,0:T(8,128)} %bitcast.29), custom_call_target="tpu_custom_call" | custom-call | tf_op jit(solution)/shard_map/smooth_xz/pallas_call | solution.py:377
  (22 shorter events, 0.0 us)
Async XLA Ops:
  0.6 0.7 copy-start.6
  36.8 6.4 %collective-permute-start = (f32[32,128]{1,0:T(8,128)}, f32[32,128]{1,0:T(8,128)S(1)}, u32[]{:S(2)}, u32[]{:S(2)}) collective-permute-start(f32[32,128]{1,0:T(8,128)} %get-tuple-element.25), channel_id=1, source_target_pairs={{0,16},{16,0},{32,48},{48,32},{64,80},{80,64},{96,112},{112,96},{1... | collective-permute-start | bytes 49160 | tf_op jit(solution)/shard_map/ppermute | solution.py:280
  36.9 2.0 %copy-start.21 = (f32[1,512]{1,0:T(1,128)S(1)}, f32[1,512]{1,0:T(1,128)}, u32[]{:S(2)}) copy-start(f32[1,512]{1,0:T(1,128)} %get-tuple-element.27) | copy-start | bytes 6148
  36.9 6.4 %collective-permute-start.1 = (f32[32,128]{1,0:T(8,128)}, f32[32,128]{1,0:T(8,128)S(1)}, u32[]{:S(2)}, u32[]{:S(2)}) collective-permute-start(f32[32,128]{1,0:T(8,128)} %get-tuple-element.26), channel_id=1, source_target_pairs={{16,32},{48,64},{80,96},{112,128},{144,160},{176,192},{208,224},{2... | collective-permute-start | bytes 49160 | tf_op jit(solution)/shard_map/ppermute | solution.py:281
  37.5 2.1 %copy-start.20 = (f32[1,512]{1,0:T(1,128)S(1)}, f32[1,512]{1,0:T(1,128)}, u32[]{:S(2)}) copy-start(f32[1,512]{1,0:T(1,128)} %get-tuple-element.28) | copy-start | bytes 6148
  37.5 5.7 %collective-permute-start.4 = (f32[16,128]{1,0:T(8,128)}, f32[16,128]{1,0:T(8,128)S(1)}, u32[]{:S(2)}, u32[]{:S(2)}) collective-permute-start(f32[16,128]{1,0:T(8,128)} %get-tuple-element.29), channel_id=1, source_target_pairs={{0,1},{1,0},{2,3},{3,2},{4,5},{5,4},{6,7},{7,6},{8,9},{9,8},{10,11... | collective-permute-start | bytes 24584 | tf_op jit(solution)/shard_map/ppermute | solution.py:284
  38.9 2.4 %collective-permute-start.2 = (f32[1,512]{1,0:T(1,128)S(1)}, f32[1,512]{1,0:T(1,128)S(1)}, u32[]{:S(2)}, u32[]{:S(2)}) collective-permute-start(f32[1,512]{1,0:T(1,128)S(1)} %copy-done.21), channel_id=1, source_target_pairs={{0,2},{2,0},{4,6},{6,4},{8,10},{10,8},{12,14},{14,12},{1,3},{3,1},... | collective-permute-start | bytes 6152 | tf_op jit(solution)/shard_map/ppermute | solution.py:282
  39.6 3.6 %collective-permute-start.3 = (f32[1,512]{1,0:T(1,128)S(1)}, f32[1,512]{1,0:T(1,128)S(1)}, u32[]{:S(2)}, u32[]{:S(2)}) collective-permute-start(f32[1,512]{1,0:T(1,128)S(1)} %copy-done.20), channel_id=1, source_target_pairs={{2,4},{6,8},{10,12},{14,0},{4,2},{8,6},{12,10},{0,14},{3,5},{7,9},... | collective-permute-start | bytes 6152 | tf_op jit(solution)/shard_map/ppermute | solution.py:283
  41.3 2.0 %copy-start.14 = (f32[1,512]{1,0:T(1,128)}, f32[1,512]{1,0:T(1,128)S(1)}, u32[]{:S(2)}) copy-start(f32[1,512]{1,0:T(1,128)S(1)} %collective-permute-done.2.ye) | copy-start | bytes 6148
  43.3 0.6 copy-start.15
  43.3 0.6 copy-start.8
  43.3 0.6 copy-start.1
  43.3 0.6 copy-start.3
  46.4 9.8 %collective-permute-start.5 = (f32[32,128]{1,0:T(8,128)}, f32[32,128]{1,0:T(8,128)S(1)}, u32[]{:S(2)}, u32[]{:S(2)}) collective-permute-start(f32[32,128]{1,0:T(8,128)} %get-tuple-element.31), channel_id=1, source_target_pairs={{0,16},{16,0},{32,48},{48,32},{64,80},{80,64},{96,112},{112,96},{1... | collective-permute-start | bytes 49160 | tf_op jit(solution)/shard_map/ppermute | solution.py:280
  46.8 5.6 %copy-start.19 = (f32[1,512]{1,0:T(1,128)S(1)}, f32[1,512]{1,0:T(1,128)}, u32[]{:S(2)}) copy-start(f32[1,512]{1,0:T(1,128)} %get-tuple-element.33) | copy-start | bytes 6148
  46.8 9.4 %collective-permute-start.6 = (f32[32,128]{1,0:T(8,128)}, f32[32,128]{1,0:T(8,128)S(1)}, u32[]{:S(2)}, u32[]{:S(2)}) collective-permute-start(f32[32,128]{1,0:T(8,128)} %get-tuple-element.32), channel_id=1, source_target_pairs={{16,32},{48,64},{80,96},{112,128},{144,160},{176,192},{208,224},{2... | collective-permute-start | bytes 49160 | tf_op jit(solution)/shard_map/ppermute | solution.py:281
  50.7 1.8 %copy-start.17 = (f32[1,512]{1,0:T(1,128)S(1)}, f32[1,512]{1,0:T(1,128)}, u32[]{:S(2)}) copy-start(f32[1,512]{1,0:T(1,128)} %get-tuple-element.34) | copy-start | bytes 6148
  50.7 5.5 %collective-permute-start.9 = (f32[16,128]{1,0:T(8,128)}, f32[16,128]{1,0:T(8,128)S(1)}, u32[]{:S(2)}, u32[]{:S(2)}) collective-permute-start(f32[16,128]{1,0:T(8,128)} %get-tuple-element.35), channel_id=1, source_target_pairs={{0,1},{1,0},{2,3},{3,2},{4,5},{5,4},{6,7},{7,6},{8,9},{9,8},{10,11... | collective-permute-start | bytes 24584 | tf_op jit(solution)/shard_map/ppermute | solution.py:284
  52.5 2.7 %collective-permute-start.7 = (f32[1,512]{1,0:T(1,128)S(1)}, f32[1,512]{1,0:T(1,128)S(1)}, u32[]{:S(2)}, u32[]{:S(2)}) collective-permute-start(f32[1,512]{1,0:T(1,128)S(1)} %copy-done.19), channel_id=1, source_target_pairs={{0,2},{2,0},{4,6},{6,4},{8,10},{10,8},{12,14},{14,12},{1,3},{3,1},... | collective-permute-start | bytes 6152 | tf_op jit(solution)/shard_map/ppermute | solution.py:282
  52.5 3.7 %collective-permute-start.8 = (f32[1,512]{1,0:T(1,128)S(1)}, f32[1,512]{1,0:T(1,128)S(1)}, u32[]{:S(2)}, u32[]{:S(2)}) collective-permute-start(f32[1,512]{1,0:T(1,128)S(1)} %copy-done.17), channel_id=1, source_target_pairs={{2,4},{6,8},{10,12},{14,0},{4,2},{8,6},{12,10},{0,14},{3,5},{7,9},... | collective-permute-start | bytes 6152 | tf_op jit(solution)/shard_map/ppermute | solution.py:283
  55.2 1.1 copy-start.10
  56.2 0.6 copy-start.11
  56.2 0.6 copy-start.7
  56.2 0.6 copy-start
  56.3 0.6 copy-start.2
  59.5 8.2 %collective-permute-start.10 = (f32[32,128]{1,0:T(8,128)}, f32[32,128]{1,0:T(8,128)S(1)}, u32[]{:S(2)}, u32[]{:S(2)}) collective-permute-start(f32[32,128]{1,0:T(8,128)} %get-tuple-element.38), channel_id=1, source_target_pairs={{0,16},{16,0},{32,48},{48,32},{64,80},{80,64},{96,112},{112,96},{1... | collective-permute-start | bytes 49160 | tf_op jit(solution)/shard_map/ppermute | solution.py:280
  59.6 3.6 %copy-start.18 = (f32[1,512]{1,0:T(1,128)S(1)}, f32[1,512]{1,0:T(1,128)}, u32[]{:S(2)}) copy-start(f32[1,512]{1,0:T(1,128)} %get-tuple-element.40) | copy-start | bytes 6148
  59.6 8.1 %collective-permute-start.11 = (f32[32,128]{1,0:T(8,128)}, f32[32,128]{1,0:T(8,128)S(1)}, u32[]{:S(2)}, u32[]{:S(2)}) collective-permute-start(f32[32,128]{1,0:T(8,128)} %get-tuple-element.39), channel_id=1, source_target_pairs={{16,32},{48,64},{80,96},{112,128},{144,160},{176,192},{208,224},{2... | collective-permute-start | bytes 49160 | tf_op jit(solution)/shard_map/ppermute | solution.py:281
  61.7 2.1 %copy-start.16 = (f32[1,512]{1,0:T(1,128)S(1)}, f32[1,512]{1,0:T(1,128)}, u32[]{:S(2)}) copy-start(f32[1,512]{1,0:T(1,128)} %get-tuple-element.41) | copy-start | bytes 6148
  61.7 6.0 %collective-permute-start.14 = (f32[16,128]{1,0:T(8,128)}, f32[16,128]{1,0:T(8,128)S(1)}, u32[]{:S(2)}, u32[]{:S(2)}) collective-permute-start(f32[16,128]{1,0:T(8,128)} %get-tuple-element.42), channel_id=1, source_target_pairs={{0,1},{1,0},{2,3},{3,2},{4,5},{5,4},{6,7},{7,6},{8,9},{9,8},{10,11... | collective-permute-start | bytes 24584 | tf_op jit(solution)/shard_map/ppermute | solution.py:284
  63.2 2.4 %collective-permute-start.12 = (f32[1,512]{1,0:T(1,128)S(1)}, f32[1,512]{1,0:T(1,128)S(1)}, u32[]{:S(2)}, u32[]{:S(2)}) collective-permute-start(f32[1,512]{1,0:T(1,128)S(1)} %copy-done.18), channel_id=1, source_target_pairs={{0,2},{2,0},{4,6},{6,4},{8,10},{10,8},{12,14},{14,12},{1,3},{3,1},... | collective-permute-start | bytes 6152 | tf_op jit(solution)/shard_map/ppermute | solution.py:282
  63.8 3.9 %collective-permute-start.13 = (f32[1,512]{1,0:T(1,128)S(1)}, f32[1,512]{1,0:T(1,128)S(1)}, u32[]{:S(2)}, u32[]{:S(2)}) collective-permute-start(f32[1,512]{1,0:T(1,128)S(1)} %copy-done.16), channel_id=1, source_target_pairs={{2,4},{6,8},{10,12},{14,0},{4,2},{8,6},{12,10},{0,14},{3,5},{7,9},... | collective-permute-start | bytes 6152 | tf_op jit(solution)/shard_map/ppermute | solution.py:283
  65.7 2.1 %copy-start.12 = (f32[1,512]{1,0:T(1,128)}, f32[1,512]{1,0:T(1,128)S(1)}, u32[]{:S(2)}) copy-start(f32[1,512]{1,0:T(1,128)S(1)} %collective-permute-done.12.ye) | copy-start | bytes 6148
  67.7 0.6 copy-start.13
  67.7 0.6 copy-start.9
  67.7 0.6 copy-start.4
  67.8 0.6 copy-start.5

commit v2 on v1

v2 whole, which is shorter than its diff:
```python
import functools
import math

import jax
import jax.numpy as jnp
from jax import lax
from jax.experimental import pallas as pl
from jax.experimental.pallas import tpu as pltpu
from jax.sharding import PartitionSpec as P

F32 = jnp.float32
BF16 = jnp.bfloat16
CAP = 2


def iota(shape, dim):
    return lax.broadcasted_iota(jnp.int32, shape, dim)


def thirds(value):
    high = value.astype(BF16)
    left = value - high.astype(F32)
    middle = left.astype(BF16)
    low = (left - middle.astype(F32)).astype(BF16)
    return high, middle, low


def halves(value):
    high = value.astype(BF16)
    return high, (value - high.astype(F32)).astype(BF16)


def dot(left, right, dims):
    return lax.dot_general(left, right, (dims, ((), ())), preferred_element_type=F32)


def dot3(left, right, dims):
    lh, ll = halves(left)
    rh, rl = halves(right)
    return dot(lh, rh, dims) + (dot(lh, rl, dims) + dot(ll, rh, dims))


def fetch(copies, sems):
    started = [pltpu.make_async_copy(source, target, sems.at[i]) for i, (source, target) in enumerate(copies)]
    for copy in started:
        copy.start()
    return started


def dispatch_kernel(sources_hbm, owner_hbm, cell_hbm, out_ref, sources_ref, owner_ref, cell_ref, sems):
    for copy in fetch([(sources_hbm, sources_ref), (owner_hbm, owner_ref), (cell_hbm, cell_ref)], sems):
        copy.wait()
    depth, wells = sources_ref.shape
    chunks, lanes = out_ref.shape
    owner = owner_ref[...]
    owner_row = owner.astype(F32)
    owner_col = jnp.transpose(jnp.broadcast_to(owner_row, (8, wells)))[:, :1]
    earlier = iota((wells, wells), 0) < iota((wells, wells), 1)
    same = (owner_col == owner_row) & earlier
    rank = jnp.sum(same.astype(F32), axis=0, keepdims=True)
    target = CAP * owner_row + rank
    chosen = jnp.where(iota((chunks, wells), 0).astype(F32) == target, 1.0, 0.0).astype(BF16)
    cell = jnp.broadcast_to(cell_ref[...].astype(F32), (lanes - depth, wells))
    total = jnp.zeros((chunks, lanes), F32)
    for piece in thirds(jnp.concatenate([sources_ref[...], cell], axis=0)):
        total = total + dot(chosen, piece, ((1,), (1,)))
    out_ref[...] = total


def landing(received_ref, depth, rows, lanes):
    wells, width = received_ref.shape
    across = rows // depth
    received = received_ref[...]
    cell = received[:, depth : depth + 1].astype(jnp.int32)
    spread = jnp.where(iota((width, rows), 0) == iota((width, rows), 1) // across, 1.0, 0.0).astype(BF16)
    at_x = iota((wells, rows), 1) % across == cell // lanes
    at_y = jnp.where(iota((wells, lanes), 1) == cell % lanes, 1.0, 0.0).astype(BF16)
    landed = jnp.zeros((rows, lanes), F32)
    for piece in reversed(thirds(received)):
        wide = jnp.where(at_x, dot(piece, spread, ((1,), (0,))), 0.0).astype(BF16)
        landed = landed + dot(wide, at_y, ((0,), (0,)))
    return landed


def put_faces(adjoint, step, courant_ref, sign_ref, depth, faces):
    rows, lanes = adjoint.shape
    across = rows // depth
    xe_ref, xo_ref, ye_ref, yo_ref, z_ref = faces
    sign = sign_ref[step]
    lane = iota((rows, lanes), 1)
    flow = courant_ref[1] * adjoint
    raised = (sign & 2) != 0
    ends = jnp.transpose(jnp.where(raised == (lane == 0), flow, 0.0))
    low, high = ends[0:1, :], ends[lanes - 1 : lanes, :]
    even = (lax.axis_index("gy") % 2) == 0
    ye_ref[...] = jnp.where(even, high, low)
    yo_ref[...] = jnp.where(even, low, high)
    shape = (depth, across, lanes)
    flow = (courant_ref[0] * adjoint).reshape(shape)
    raised = (sign & 1).reshape(shape)
    low = jnp.where(raised[:, 0, :] != 0, flow[:, 0, :], 0.0)
    high = jnp.where(raised[:, across - 1, :] != 0, 0.0, flow[:, across - 1, :])
    even = (lax.axis_index("gx") % 2) == 0
    xe_ref[...] = jnp.where(even, high, low)
    xo_ref[...] = jnp.where(even, low, high)
    flow = courant_ref[2]
    low = jnp.where((sign[:across] & 4) != 0, flow[:across] * adjoint[:across], 0.0)
    high = jnp.where((sign[rows - across :] & 4) != 0, 0.0, flow[rows - across :] * adjoint[rows - across :])
    z_ref[...] = jnp.where(lax.axis_index("gz") == 0, high, low)


def inner_kernel(step, depth, tracer_step, adjoint_ref, courant_ref, sign_ref, *rest):
    gradient_in, tracer_ref, gradient_ref = None, None, None
    if tracer_step is not None:
        tracer_ref, *rest = rest
        if len(rest) == 3:
            gradient_in, *rest = rest
        gradient_ref, *rest = rest
    (kept_ref,) = rest
    adjoint = adjoint_ref[...]
    rows, lanes = adjoint.shape
    across = rows // depth
    sign = sign_ref[step]
    row_x = iota((rows, lanes), 0) % across
    lane = iota((rows, lanes), 1)
    flow = [courant_ref[axis] * adjoint for axis in range(3)]
    rising = [jnp.where((sign & (1 << axis)) != 0, flow[axis], 0.0) for axis in range(3)]
    falling = [flow[axis] - rising[axis] for axis in range(3)]
    kept = (1.0 - (courant_ref[0] + courant_ref[1] + courant_ref[2])) * adjoint
    up = jnp.where(row_x == across - 1, 0.0, pltpu.roll(rising[0], rows - 1, 0))
    down = jnp.where(row_x == 0, 0.0, pltpu.roll(falling[0], 1, 0))
    kept = kept + up + down
    up = jnp.where(lane == lanes - 1, 0.0, pltpu.roll(rising[1], lanes - 1, 1))
    down = jnp.where(lane == 0, 0.0, pltpu.roll(falling[1], 1, 1))
    kept = kept + up + down
    blank = jnp.zeros((across, lanes), F32)
    kept_ref[...] = (
        kept
        + jnp.concatenate([rising[2][across:, :], blank], axis=0)
        + jnp.concatenate([blank, falling[2][: rows - across, :]], axis=0)
    )
    if tracer_step is not None:
        gradient = adjoint * tracer_ref[tracer_step]
        gradient_ref[...] = gradient if gradient_in is None else gradient_in[...] + gradient


def first_kernel(step, received_ref, courant_hbm, sign_hbm, *rest):
    adjoint_ref, *faces, courant_ref, sign_ref, sems = rest
    rows, lanes = adjoint_ref.shape
    depth = faces[0].shape[0]
    across = rows // depth
    last = rows - across
    copies = fetch(
        [
            (courant_hbm.at[1], courant_ref.at[1]),
            (sign_hbm.at[step], sign_ref.at[0]),
            (courant_hbm.at[0], courant_ref.at[0]),
            (courant_hbm.at[2, 0:across], courant_ref.at[2, 0:across]),
            (courant_hbm.at[2, last:rows], courant_ref.at[2, last:rows]),
        ],
        sems,
    )
    adjoint = landing(received_ref, depth, rows, lanes)
    adjoint_ref[...] = adjoint
    for copy in copies:
        copy.wait()
    put_faces(adjoint, 0, courant_ref, sign_ref, depth, faces)


def join(sizes, kept_ref, xe_ref, xo_ref, ye_ref, yo_ref, z_ref):
    rows, lanes = kept_ref.shape
    depth = xe_ref.shape[0]
    across = rows // depth
    gx, gy, gz = lax.axis_index("gx"), lax.axis_index("gy"), lax.axis_index("gz")
    even = (gx % 2) == 0
    xe, xo = xe_ref[...], xo_ref[...]
    above = jnp.where(gx == sizes[0] - 1, 0.0, jnp.where(even, xe, xo))
    below = jnp.where(gx == 0, 0.0, jnp.where(even, xo, xe))
    row_x = iota((depth, across, lanes), 1)
    adjoint = kept_ref[...] + jnp.where(
        row_x == across - 1,
        above[:, None, :],
        jnp.where(row_x == 0, below[:, None, :], 0.0),
    ).reshape(rows, lanes)
    even = (gy % 2) == 0
    ye, yo = ye_ref[...], yo_ref[...]
    above = jnp.where(gy == sizes[1] - 1, 0.0, jnp.where(even, ye, yo))
    below = jnp.where(gy == 0, 0.0, jnp.where(even, yo, ye))
    row_y = iota((lanes, rows), 0)
    adjoint = adjoint + jnp.transpose(
        jnp.where(row_y == lanes - 1, above, jnp.where(row_y == 0, below, 0.0))
    )
    z = z_ref[...]
    blank = jnp.zeros((rows - across, lanes), F32)
    return adjoint + jnp.where(
        gz == 0,
        jnp.concatenate([blank, z], axis=0),
        jnp.concatenate([z, blank], axis=0),
    )


def middle_kernel(sizes, step, kept_ref, xe, xo, ye, yo, z, courant_ref, sign_ref, adjoint_ref, *faces):
    adjoint = join(sizes, kept_ref, xe, xo, ye, yo, z)
    adjoint_ref[...] = adjoint
    put_faces(adjoint, step, courant_ref, sign_ref, xe.shape[0], faces)


def last_kernel(
    sizes, kept_ref, xe, xo, ye, yo, z, tracer_ref, gradient_in, adjoint_ref, lines_ref, work_ref
):
    rows = kept_ref.shape[0]
    depth = xe.shape[0]
    across = rows // depth
    adjoint = join(sizes, kept_ref, xe, xo, ye, yo, z)
    adjoint_ref[...] = adjoint
    work_ref[...] = gradient_in[...] + adjoint * tracer_ref[0]
    for x in range(across):
        lines_ref[x * depth : (x + 1) * depth, :] = work_ref[pl.ds(x, depth, stride=across), :]


def smooth_y_kernel(depth, length, rows_each, lines_ref, out_ref):
    rows, lanes = lines_ref.shape
    lines = lines_ref[...]
    share = 2 * depth
    groups = lanes // rows_each
    scale = 1.0 / math.sqrt(length)
    order = iota((lanes, lanes), 0)
    y_out = (order % groups) * rows_each + order // groups
    table = jnp.exp(-jnp.abs(y_out - iota((lanes, lanes), 1)).astype(F32) / length) * scale
    side = iota((8, lanes), 0)
    y_in = iota((8, lanes), 1)
    carry_table = jnp.exp(-jnp.where(side == 0, lanes - 1 - y_in, y_in).astype(F32) / length) * scale
    both = dot3(jnp.concatenate([table, carry_table], axis=0), lines, ((1,), (1,)))
    result, carry = both[:lanes], both[lanes:]
    place = iota((8, rows), 1)
    decay = math.exp(-lanes / length)
    right = carry
    left = carry
    step = share
    factor = decay
    while step < rows:
        right = right + factor * jnp.where(place >= step, pltpu.roll(right, step, 1), 0.0)
        left = left + factor * jnp.where(place < rows - step, pltpu.roll(left, rows - step, 1), 0.0)
        step, factor = 2 * step, factor * factor
    right = jnp.where(place >= share, pltpu.roll(right, share, 1), 0.0)[0:1, :]
    left = jnp.where(place < rows - share, pltpu.roll(left, rows - share, 1), 0.0)[1:2, :]
    row = iota((lanes, 1), 0)
    y_row = ((row % groups) * rows_each + row // groups).astype(F32)
    result = (
        result + jnp.exp(-(y_row + 1.0) / length) * right + jnp.exp(-(lanes - y_row) / length) * left
    )
    per_tile = lanes // depth
    quarter = iota((groups, lanes), 1) // depth
    for tile in range(rows // lanes):
        pieces = [
            result[r * groups : (r + 1) * groups, tile * lanes : (tile + 1) * lanes]
            for r in range(rows_each)
        ]
        for u in range(per_tile):
            line = tile * per_tile + u
            block, xx = line // 2, line % 2
            chunk = jnp.zeros((groups, lanes), F32)
            for r in range(rows_each):
                turn = ((r - u) * depth) % lanes
                piece = pltpu.roll(pieces[r], turn, 1) if turn else pieces[r]
                chunk = jnp.where(quarter == r, piece, chunk)
            out_ref[pl.ds(block * 2 * groups + xx, groups, stride=2), :] = chunk


def smooth_xz_kernel(depth, length_x, length_z, rows_each, data_ref, out_hbm, work_ref, sems):
    rows, lanes = data_ref.shape
    full_x = work_ref.shape[1]
    sources = rows // 4
    part = [jnp.zeros((lanes, full_x), F32) for _ in range(2)]
    for xx in range(2):
        x_in = 2 * iota((sources, full_x), 0) + xx
        table = jnp.exp(-jnp.abs(x_in - iota((sources, full_x), 1)).astype(F32) / length_x)
        table = table * (1.0 / math.sqrt(length_x))
        for g in range(2):
            block = data_ref[pl.ds(2 * g + xx, sources, stride=4), :]
            part[g] = part[g] + dot3(block, table, ((0,), (0,)))
    full_z = 2 * depth
    z_out, z_in = iota((full_z, full_z), 0), iota((full_z, full_z), 1)
    table = jnp.exp(-jnp.abs(z_out - z_in).astype(F32) / length_z) * (1.0 / math.sqrt(length_z))
    copies = []
    for r in range(rows_each):
        column = jnp.concatenate([part[g][r * depth : (r + 1) * depth] for g in range(2)], axis=0)
        here = slice(r * full_z, (r + 1) * full_z)
        work_ref[here, :] = dot3(table, column, ((1,), (0,)))
        copy = pltpu.make_async_copy(work_ref.at[here], out_hbm.at[here], sems.at[r])
        copy.start()
        copies.append(copy)
    for copy in copies:
        copy.wait()


def pair_swaps(count):
    even = [(i, i ^ 1) for i in range(count)]
    odd = [(i, (i + 1) % count) for i in range(1, count, 2)]
    odd = odd + [(target, source) for source, target in odd]
    return even, odd


def exchange(faces):
    xe, xo, ye, yo, z = faces
    x_even, x_odd = pair_swaps(lax.axis_size("gx"))
    y_even, y_odd = pair_swaps(lax.axis_size("gy"))
    return (
        lax.ppermute(xe, "gx", x_even),
        lax.ppermute(xo, "gx", x_odd),
        lax.ppermute(ye, "gy", y_even),
        lax.ppermute(yo, "gy", y_odd),
        lax.ppermute(z, "gz", [(0, 1), (1, 0)]),
    )


def local(kernel, name, inputs, outputs, scratch=(), far=0, far_out=False):
    vmem = pl.BlockSpec(memory_space=pltpu.VMEM)
    hbm = pl.BlockSpec(memory_space=pl.ANY)
    near = len(inputs) - far
    return pl.pallas_call(
        kernel,
        in_specs=[vmem] * near + [hbm] * far,
        out_specs=[hbm if far_out else vmem] * len(outputs),
        out_shape=[(pltpu.HBM if far_out else pltpu.VMEM)(dims, F32) for dims in outputs],
        scratch_shapes=scratch,
        compiler_params=pltpu.CompilerParams(vmem_limit_bytes=8 << 20),
        name=name,
    )(
        *[pltpu.with_memory_space_constraint(values, pltpu.VMEM) for values in inputs[:near]],
        *[pltpu.with_memory_space_constraint(values, pltpu.HBM) for values in inputs[near:]],
    )


def per_device(well_sources, well_owner, well_cell, flow_sign, courant, tracer):
    steps, brick_z, brick_x, brick_y = flow_sign.shape
    wells = well_sources.shape[0]
    rows = brick_z * brick_x
    sizes = (lax.axis_size("gx"), lax.axis_size("gy"), lax.axis_size("gz"))
    devices = sizes[0] * sizes[1] * sizes[2]
    owners = sizes[0] * sizes[1]
    axes = ("gx", "gy", "gz")
    (outgoing,) = local(
        dispatch_kernel,
        "dispatch",
        [well_sources.T, well_owner.reshape(1, wells), well_cell.reshape(1, wells)],
        [(CAP * owners, 128)],
        [
            pltpu.VMEM((brick_z, wells), F32),
            pltpu.VMEM((1, wells), jnp.int32),
            pltpu.VMEM((1, wells), jnp.int32),
            pltpu.SemaphoreType.DMA((3,)),
        ],
        far=3,
    )
    received = lax.all_to_all(
        outgoing.reshape(owners, CAP, 128), ("gx", "gy"), split_axis=0, concat_axis=0, tiled=True
    ).reshape(CAP * owners, 128)

    flow = flow_sign.reshape(steps, rows, brick_y)
    speed = courant.reshape(3, rows, brick_y)
    trace = tracer.reshape(steps, rows, brick_y)
    field = (rows, brick_y)
    face_shapes = [(brick_z, brick_y)] * 2 + [(1, rows)] * 2 + [(brick_x, brick_y)]
    gradient = []
    adjoint, *faces = local(
        functools.partial(first_kernel, steps - 1),
        "first",
        [received, speed, flow],
        [field] + face_shapes,
        [
            pltpu.VMEM((3, *field), F32),
            pltpu.VMEM((1, *field), jnp.int32),
            pltpu.SemaphoreType.DMA((5,)),
        ],
        far=2,
    )
    for step in reversed(range(steps)):
        arrived = exchange(faces)
        if step == steps - 1:
            inputs, outputs, tracer_step = [], [], None
        else:
            inputs, outputs, tracer_step = [trace] + gradient, [field], step + 1
        *gradient, kept = local(
            functools.partial(inner_kernel, step, brick_z, tracer_step),
            f"inner{step}",
            [adjoint, speed, flow] + inputs,
            outputs + [field],
        )
        if step:
            adjoint, *faces = local(
                functools.partial(middle_kernel, sizes, step - 1),
                f"join{step}",
                [kept, *arrived, speed, flow],
                [field] + face_shapes,
            )
    adjoint, lines = local(
        functools.partial(last_kernel, sizes),
        "join0",
        [kept, *arrived, trace, *gradient],
        [field, field],
        [pltpu.VMEM(field, F32)],
    )
    y_lines = lax.all_to_all(
        lines.reshape(sizes[1], rows // sizes[1], brick_y), "gy", split_axis=0, concat_axis=0, tiled=True
    ).reshape(rows, brick_y)
    rows_each = sizes[1] * brick_y // devices
    (smooth,) = local(
        functools.partial(smooth_y_kernel, brick_z, 2.0 * brick_y, rows_each), "smooth_y", [y_lines], [field]
    )
    planes = lax.all_to_all(
        smooth.reshape(devices, 2, 128), axes, split_axis=0, concat_axis=0, tiled=True
    ).reshape(rows, brick_y)
    full_x, full_z = sizes[0] * brick_x, sizes[2] * brick_z
    (smoothed,) = local(
        functools.partial(smooth_xz_kernel, brick_z, 2.0 * brick_x, 2.0 * brick_z, rows_each),
        "smooth_xz",
        [planes],
        [(rows_each * full_z, full_x)],
        [pltpu.VMEM((rows_each * full_z, full_x), F32), pltpu.SemaphoreType.DMA((rows_each,))],
        far_out=True,
    )
    return (
        adjoint.reshape(brick_z, brick_x, brick_y),
        smoothed.reshape(rows_each, full_z, full_x),
    )


def solution(mesh):
    return jax.shard_map(
        per_device,
        mesh=mesh,
        in_specs=(
            P(("gx", "gy"), "gz"),
            P(("gx", "gy"), None),
            P(("gx", "gy")),
            P(None, "gz", "gx", "gy"),
            P(None, "gz", "gx", "gy"),
            P(None, "gz", "gx", "gy"),
        ),
        out_specs=(P("gz", "gx", "gy"), P(("gx", "gy", "gz"), None, None)),
        check_vma=False,
    )
```

time: 115 us -> 95.8 us (0.83)
  blocking collectives: 68.5 us -> 40.1 us
  waiting for transfers between devices: 10.3 us -> 24.7 us
  Pallas kernels: 17 us -> 7.07 us
  starting transfers between devices: 14.1 us -> 22 us
  local copies, waits for them, and re-layouts: 3.2 us -> 0.72 us
    all_to_all x2 -> x1, blocking collectives: 54.2 us -> 27.5 us  [per_device(): lax.all_to_all(outgoing.reshape(owners, CAP, 128), ('gx', 'gy'), split_ax...]
    all_to_all x0 -> x1, waiting for transfers between devices: none -> 15.3 us  [per_device(): lax.all_to_all(smooth.reshape(devices, 2, 128), axes, split_axis=0, conca...]
    pallas_call x7 -> x10, Pallas kernels: 17 us -> 7.07 us  [local(): pl.pallas_call(kernel, in_specs=[vmem] * near + [hbm] * far, out_specs=[h...]
    all_to_all x0 -> x1, starting transfers between devices: none -> 7.75 us  [per_device(): lax.all_to_all(smooth.reshape(devices, 2, 128), axes, split_axis=0, conca...]
    unnamed x45 -> x7, local copies, waits for them, and re-layouts: 3.2 us -> 0.72 us
    all_to_all x1, blocking collectives: 14.3 us -> 12.6 us  [per_device(): lax.all_to_all(lines.reshape(sizes[1], rows // sizes[1], brick_y), 'gy',...]
  transfers between devices with their start and end apart: 15 -> 16, of which waited for: 6 -> 7; matrix products, arithmetic and copies ran while one was open for 0% -> 1% of each run, Pallas kernels for 0% -> 1%
where the time goes in v2:
time: 95.8 us; the launch traced here: 95.5 us
  blocking collectives  40.1 us (42%)
  waiting for transfers between devices  24.7 us (26%)
  starting transfers between devices  22 us (23%)
  Pallas kernels  7.07 us (7%)
    all_to_all x1, blocking collectives, per_device(): lax.all_to_all(outgoing.reshape(owners, CAP, 128), ('gx', 'gy'), split_ax...  27.5 us
    all_to_all x1, waiting for transfers between devices, per_device(): lax.all_to_all(smooth.reshape(devices, 2, 128), axes, split_axis=0, conca...  15.3 us
    all_to_all x1, blocking collectives, per_device(): lax.all_to_all(lines.reshape(sizes[1], rows // sizes[1], brick_y), 'gy',...  12.6 us
    all_to_all x1, starting transfers between devices, per_device(): lax.all_to_all(smooth.reshape(devices, 2, 128), axes, split_axis=0, conca...  7.75 us
    pallas_call x10, Pallas kernels, local(): pl.pallas_call(kernel, in_specs=[vmem] * near + [hbm] * far, out_specs=[h...  7.07 us
    ppermute x3, starting transfers between devices, exchange(): lax.ppermute(xo, 'gx', x_odd)  6.34 us
    ppermute x3, starting transfers between devices, exchange(): lax.ppermute(z, 'gz', [(0, 1), (1, 0)])  5.79 us
    ppermute x3, waiting for transfers between devices, exchange(): lax.ppermute(ye, 'gy', y_even)  4.76 us
  transfers between devices with their start and end apart: 16, of which 7 were waited for; matrix products, arithmetic and copies ran while one was open for 1% of the time, Pallas kernels for 1%

profile of v2, /device:TPU:1, one launch (start us, length us, event | category | flops | bytes accessed | tf_op | source)
XLA Modules:
  0.0 95.5 jit_solution(4335981937524681921)
XLA Ops:
  0.6 1.1 %dispatch.1 = f32[256,128]{1,0:T(8,128)S(1)} custom-call(f32[32,96]{1,0:T(8,128)} %bitcast.36, s32[1,96]{1,0:T(1,128)} %bitcast.37, s32[1,96]{1,0:T(1,128)} %bitcast.38), custom_call_target="tpu_custom_call" | custom-call | tf_op jit(solution)/shard_map/dispatch/pallas_call | solution.py:321
  1.7 27.5 %all_to_all.15 = f32[128,2,128]{2,1,0:T(2,128)S(1)} all-to-all(f32[128,2,128]{2,1,0:T(2,128)S(1)} %bitcast.32), channel_id=1, replica_groups=mesh['gx'=16,'gy'=8,'gz'=2] {'gx','gy'}, dimensions={0} | all-to-all | bytes 262144 | tf_op jit(solution)/shard_map/all_to_all | solution.py:356
  29.3 0.0 copy-start
  29.3 0.0 copy-start.1
  29.3 1.5 %first.1 = (f32[512,128]{1,0:T(8,128)S(1)}, f32[32,128]{1,0:T(8,128)S(1)}, f32[32,128]{1,0:T(8,128)S(1)}, f32[1,512]{1,0:T(1,128)S(1)}, f32[1,512]{1,0:T(1,128)S(1)}, /*index=5*/f32[16,128]{1,0:T(8,128)S(1)}) custom-call(f32[256,128]{1,0:T(8,128)S(1)} %bitcast.33, f32[3,512,128]{2,1,0:T(8,128)} %bitcast.15, s32[3,512,128]{2,1,0:T(8,128)} %bitcast.21), custom_call_target="tpu_custom_call" | custom-call | tf_op jit(solution)/shard_map/first/pallas_call | solution.py:321
  30.7 0.1 collective-permute-start
  30.8 1.3 %collective-permute-start.1 = (f32[32,128]{1,0:T(8,128)S(1)}, f32[32,128]{1,0:T(8,128)S(1)}, u32[]{:S(2)}, u32[]{:S(2)}) collective-permute-start(f32[32,128]{1,0:T(8,128)S(1)} %get-tuple-element.28), channel_id=1, source_target_pairs={{16,32},{48,64},{80,96},{112,128},{144,160},{176,192},{208,224},{2... | collective-permute-start | bytes 49160 | tf_op jit(solution)/shard_map/ppermute | solution.py:310
  32.1 2.7 %collective-permute-start.4 = (f32[16,128]{1,0:T(8,128)S(1)}, f32[16,128]{1,0:T(8,128)S(1)}, u32[]{:S(2)}, u32[]{:S(2)}) collective-permute-start(f32[16,128]{1,0:T(8,128)S(1)} %get-tuple-element.31), channel_id=1, source_target_pairs={{0,1},{1,0},{2,3},{3,2},{4,5},{5,4},{6,7},{7,6},{8,9},{9,8},{10,11... | collective-permute-start | bytes 24584 | tf_op jit(solution)/shard_map/ppermute | solution.py:313
  34.8 0.4 collective-permute-start.2
  35.2 0.0 collective-permute-start.3
  35.2 0.0 copy-done
  35.2 0.0 copy-done.1
  35.2 0.3 inner2.1.kept_ref
  35.6 0.0 copy-start.2
  35.6 1.6 %collective-permute-done.2.ye = f32[1,512]{1,0:T(1,128)S(1)} collective-permute-done((f32[1,512]{1,0:T(1,128)S(1)}, f32[1,512]{1,0:T(1,128)S(1)}, u32[]{:S(2)}, u32[]{:S(2)}) %collective-permute-start.2) | collective-permute-done | bytes 2080 | tf_op jit(solution)/shard_map/ppermute | solution.py:311
  37.2 1.9 %collective-permute-done.3.yo = f32[1,512]{1,0:T(1,128)S(1)} collective-permute-done((f32[1,512]{1,0:T(1,128)S(1)}, f32[1,512]{1,0:T(1,128)S(1)}, u32[]{:S(2)}, u32[]{:S(2)}) %collective-permute-start.3) | collective-permute-done | bytes 2080 | tf_op jit(solution)/shard_map/ppermute | solution.py:312
  39.1 0.0 collective-permute-done.4.z
  39.1 0.0 collective-permute-done.xe
  39.1 0.0 collective-permute-done.1.xo
  39.1 0.3 join2.1
  39.4 0.1 collective-permute-start.5
  39.5 3.0 %collective-permute-start.6 = (f32[32,128]{1,0:T(8,128)S(1)}, f32[32,128]{1,0:T(8,128)S(1)}, u32[]{:S(2)}, u32[]{:S(2)}) collective-permute-start(f32[32,128]{1,0:T(8,128)S(1)} %get-tuple-element.35), channel_id=1, source_target_pairs={{16,32},{48,64},{80,96},{112,128},{144,160},{176,192},{208,224},{2... | collective-permute-start | bytes 49160 | tf_op jit(solution)/shard_map/ppermute | solution.py:310
  42.6 1.7 %collective-permute-start.9 = (f32[16,128]{1,0:T(8,128)S(1)}, f32[16,128]{1,0:T(8,128)S(1)}, u32[]{:S(2)}, u32[]{:S(2)}) collective-permute-start(f32[16,128]{1,0:T(8,128)S(1)} %get-tuple-element.38), channel_id=1, source_target_pairs={{0,1},{1,0},{2,3},{3,2},{4,5},{5,4},{6,7},{7,6},{8,9},{9,8},{10,11... | collective-permute-start | bytes 24584 | tf_op jit(solution)/shard_map/ppermute | solution.py:313
  44.3 0.0 collective-permute-start.7
  44.3 0.6 collective-permute-start.8
  44.9 0.0 copy-done.2
  44.9 0.3 inner1.1
  45.2 1.8 %collective-permute-done.7.ye = f32[1,512]{1,0:T(1,128)S(1)} collective-permute-done((f32[1,512]{1,0:T(1,128)S(1)}, f32[1,512]{1,0:T(1,128)S(1)}, u32[]{:S(2)}, u32[]{:S(2)}) %collective-permute-start.7) | collective-permute-done | bytes 2080 | tf_op jit(solution)/shard_map/ppermute | solution.py:311
  47.0 0.9 collective-permute-done.8.yo
  47.9 0.0 collective-permute-done.9.z
  47.9 0.0 collective-permute-done.5.xe
  47.9 0.0 collective-permute-done.6.xo
  47.9 0.3 join1.1
  48.2 0.1 collective-permute-start.10
  48.3 2.1 %collective-permute-start.11 = (f32[32,128]{1,0:T(8,128)S(1)}, f32[32,128]{1,0:T(8,128)S(1)}, u32[]{:S(2)}, u32[]{:S(2)}) collective-permute-start(f32[32,128]{1,0:T(8,128)S(1)} %get-tuple-element.43), channel_id=1, source_target_pairs={{16,32},{48,64},{80,96},{112,128},{144,160},{176,192},{208,224},{2... | collective-permute-start | bytes 49160 | tf_op jit(solution)/shard_map/ppermute | solution.py:310
  50.4 1.4 %collective-permute-start.14 = (f32[16,128]{1,0:T(8,128)S(1)}, f32[16,128]{1,0:T(8,128)S(1)}, u32[]{:S(2)}, u32[]{:S(2)}) collective-permute-start(f32[16,128]{1,0:T(8,128)S(1)} %get-tuple-element.46), channel_id=1, source_target_pairs={{0,1},{1,0},{2,3},{3,2},{4,5},{5,4},{6,7},{7,6},{8,9},{9,8},{10,11... | collective-permute-start | bytes 24584 | tf_op jit(solution)/shard_map/ppermute | solution.py:313
  51.8 0.3 collective-permute-start.12
  52.1 0.5 collective-permute-start.13
  52.6 0.3 inner0.1
  52.9 1.3 %collective-permute-done.12.ye = f32[1,512]{1,0:T(1,128)S(1)} collective-permute-done((f32[1,512]{1,0:T(1,128)S(1)}, f32[1,512]{1,0:T(1,128)S(1)}, u32[]{:S(2)}, u32[]{:S(2)}) %collective-permute-start.12) | collective-permute-done | bytes 2080 | tf_op jit(solution)/shard_map/ppermute | solution.py:311
  54.2 1.8 %collective-permute-done.13.yo = f32[1,512]{1,0:T(1,128)S(1)} collective-permute-done((f32[1,512]{1,0:T(1,128)S(1)}, f32[1,512]{1,0:T(1,128)S(1)}, u32[]{:S(2)}, u32[]{:S(2)}) %collective-permute-start.13) | collective-permute-done | bytes 2080 | tf_op jit(solution)/shard_map/ppermute | solution.py:312
  56.0 0.0 collective-permute-done.14.z
  56.0 0.0 collective-permute-done.10.xe
  56.0 0.0 collective-permute-done.11.xo
  56.0 0.2 join0.1
  56.3 12.6 %all_to_all.16 = f32[8,64,128]{2,1,0:T(8,128)S(1)} all-to-all(f32[8,64,128]{2,1,0:T(8,128)S(1)} %bitcast.34), channel_id=1, replica_groups=mesh['gx'=16,'gy'=8,'gz'=2] {'gy'}, dimensions={0} | all-to-all | bytes 524288 | tf_op jit(solution)/shard_map/all_to_all | solution.py:404
  68.8 1.4 %smooth_y.1 = f32[512,128]{1,0:T(8,128)} custom-call(f32[512,128]{1,0:T(8,128)S(1)} %bitcast.31), custom_call_target="tpu_custom_call" | custom-call | tf_op jit(solution)/shard_map/smooth_y/pallas_call | solution.py:321
  70.2 7.8 %all-to-all-start.2 = ((f32[256,2,128]{2,1,0:T(2,128)}), f32[256,2,128]{2,1,0:T(2,128)S(1)}, u32[]{:S(2)}, u32[]{:S(2)}) async-start(f32[256,2,128]{2,1,0:T(2,128)} %bitcast.11), calls=%async_computation.2 | async-start | bytes 524288 | tf_op jit(solution)/shard_map/all_to_all | solution.py:411
  78.0 0.7 copy.8
  78.7 15.3 %all-to-all-done.2 = f32[256,2,128]{2,1,0:T(2,128)S(1)} async-done(((f32[256,2,128]{2,1,0:T(2,128)}), f32[256,2,128]{2,1,0:T(2,128)S(1)}, u32[]{:S(2)}, u32[]{:S(2)}) %all-to-all-start.2) | async-done | bytes 262176 | tf_op jit(solution)/shard_map/all_to_all | solution.py:411
  94.0 1.3 %smooth_xz.1 = f32[256,256]{1,0:T(8,128)} custom-call(f32[512,128]{1,0:T(8,128)S(1)} %bitcast.30), custom_call_target="tpu_custom_call" | custom-call | tf_op jit(solution)/shard_map/smooth_xz/pallas_call | solution.py:321
Async XLA Ops:
  29.3 6.0 %copy-start = (f32[3,32,16,128]{3,2,1,0:T(8,128)S(1)}, f32[3,32,16,128]{3,2,1,0:T(8,128)}, u32[]{:S(2)}) copy-start(f32[3,32,16,128]{3,2,1,0:T(8,128)} %param.10) | copy-start | bytes 2359300
  29.3 6.0 %copy-start.1 = (s32[3,32,16,128]{3,2,1,0:T(8,128)S(1)}, s32[3,32,16,128]{3,2,1,0:T(8,128)}, u32[]{:S(2)}) copy-start(s32[3,32,16,128]{3,2,1,0:T(8,128)} %param.9) | copy-start | bytes 2359300
  30.7 8.4 %collective-permute-start = (f32[32,128]{1,0:T(8,128)S(1)}, f32[32,128]{1,0:T(8,128)S(1)}, u32[]{:S(2)}, u32[]{:S(2)}) collective-permute-start(f32[32,128]{1,0:T(8,128)S(1)} %get-tuple-element.27), channel_id=1, source_target_pairs={{0,16},{16,0},{32,48},{48,32},{64,80},{80,64},{96,112},{112,96},{1... | collective-permute-start | bytes 49160 | tf_op jit(solution)/shard_map/ppermute | solution.py:309
  30.8 8.3 %collective-permute-start.1 = (f32[32,128]{1,0:T(8,128)S(1)}, f32[32,128]{1,0:T(8,128)S(1)}, u32[]{:S(2)}, u32[]{:S(2)}) collective-permute-start(f32[32,128]{1,0:T(8,128)S(1)} %get-tuple-element.28), channel_id=1, source_target_pairs={{16,32},{48,64},{80,96},{112,128},{144,160},{176,192},{208,224},{2... | collective-permute-start | bytes 49160 | tf_op jit(solution)/shard_map/ppermute | solution.py:310
  32.1 7.0 %collective-permute-start.4 = (f32[16,128]{1,0:T(8,128)S(1)}, f32[16,128]{1,0:T(8,128)S(1)}, u32[]{:S(2)}, u32[]{:S(2)}) collective-permute-start(f32[16,128]{1,0:T(8,128)S(1)} %get-tuple-element.31), channel_id=1, source_target_pairs={{0,1},{1,0},{2,3},{3,2},{4,5},{5,4},{6,7},{7,6},{8,9},{9,8},{10,11... | collective-permute-start | bytes 24584 | tf_op jit(solution)/shard_map/ppermute | solution.py:313
  34.8 2.4 %collective-permute-start.2 = (f32[1,512]{1,0:T(1,128)S(1)}, f32[1,512]{1,0:T(1,128)S(1)}, u32[]{:S(2)}, u32[]{:S(2)}) collective-permute-start(f32[1,512]{1,0:T(1,128)S(1)} %get-tuple-element.29), channel_id=1, source_target_pairs={{0,2},{2,0},{4,6},{6,4},{8,10},{10,8},{12,14},{14,12},{1,3},{3,1},... | collective-permute-start | bytes 6152 | tf_op jit(solution)/shard_map/ppermute | solution.py:311
  35.2 3.9 %collective-permute-start.3 = (f32[1,512]{1,0:T(1,128)S(1)}, f32[1,512]{1,0:T(1,128)S(1)}, u32[]{:S(2)}, u32[]{:S(2)}) collective-permute-start(f32[1,512]{1,0:T(1,128)S(1)} %get-tuple-element.30), channel_id=1, source_target_pairs={{2,4},{6,8},{10,12},{14,0},{4,2},{8,6},{12,10},{0,14},{3,5},{7,9},... | collective-permute-start | bytes 6152 | tf_op jit(solution)/shard_map/ppermute | solution.py:312
  35.6 9.4 %copy-start.2 = (f32[3,32,16,128]{3,2,1,0:T(8,128)S(1)}, f32[3,32,16,128]{3,2,1,0:T(8,128)}, u32[]{:S(2)}) copy-start(f32[3,32,16,128]{3,2,1,0:T(8,128)} %param.11) | copy-start | bytes 2359300
  39.4 8.5 %collective-permute-start.5 = (f32[32,128]{1,0:T(8,128)S(1)}, f32[32,128]{1,0:T(8,128)S(1)}, u32[]{:S(2)}, u32[]{:S(2)}) collective-permute-start(f32[32,128]{1,0:T(8,128)S(1)} %get-tuple-element.34), channel_id=1, source_target_pairs={{0,16},{16,0},{32,48},{48,32},{64,80},{80,64},{96,112},{112,96},{1... | collective-permute-start | bytes 49160 | tf_op jit(solution)/shard_map/ppermute | solution.py:309
  39.5 8.4 %collective-permute-start.6 = (f32[32,128]{1,0:T(8,128)S(1)}, f32[32,128]{1,0:T(8,128)S(1)}, u32[]{:S(2)}, u32[]{:S(2)}) collective-permute-start(f32[32,128]{1,0:T(8,128)S(1)} %get-tuple-element.35), channel_id=1, source_target_pairs={{16,32},{48,64},{80,96},{112,128},{144,160},{176,192},{208,224},{2... | collective-permute-start | bytes 49160 | tf_op jit(solution)/shard_map/ppermute | solution.py:310
  42.6 5.4 %collective-permute-start.9 = (f32[16,128]{1,0:T(8,128)S(1)}, f32[16,128]{1,0:T(8,128)S(1)}, u32[]{:S(2)}, u32[]{:S(2)}) collective-permute-start(f32[16,128]{1,0:T(8,128)S(1)} %get-tuple-element.38), channel_id=1, source_target_pairs={{0,1},{1,0},{2,3},{3,2},{4,5},{5,4},{6,7},{7,6},{8,9},{9,8},{10,11... | collective-permute-start | bytes 24584 | tf_op jit(solution)/shard_map/ppermute | solution.py:313
  44.3 2.7 %collective-permute-start.7 = (f32[1,512]{1,0:T(1,128)S(1)}, f32[1,512]{1,0:T(1,128)S(1)}, u32[]{:S(2)}, u32[]{:S(2)}) collective-permute-start(f32[1,512]{1,0:T(1,128)S(1)} %get-tuple-element.36), channel_id=1, source_target_pairs={{0,2},{2,0},{4,6},{6,4},{8,10},{10,8},{12,14},{14,12},{1,3},{3,1},... | collective-permute-start | bytes 6152 | tf_op jit(solution)/shard_map/ppermute | solution.py:311
  44.3 3.6 %collective-permute-start.8 = (f32[1,512]{1,0:T(1,128)S(1)}, f32[1,512]{1,0:T(1,128)S(1)}, u32[]{:S(2)}, u32[]{:S(2)}) collective-permute-start(f32[1,512]{1,0:T(1,128)S(1)} %get-tuple-element.37), channel_id=1, source_target_pairs={{2,4},{6,8},{10,12},{14,0},{4,2},{8,6},{12,10},{0,14},{3,5},{7,9},... | collective-permute-start | bytes 6152 | tf_op jit(solution)/shard_map/ppermute | solution.py:312
  48.2 7.8 %collective-permute-start.10 = (f32[32,128]{1,0:T(8,128)S(1)}, f32[32,128]{1,0:T(8,128)S(1)}, u32[]{:S(2)}, u32[]{:S(2)}) collective-permute-start(f32[32,128]{1,0:T(8,128)S(1)} %get-tuple-element.42), channel_id=1, source_target_pairs={{0,16},{16,0},{32,48},{48,32},{64,80},{80,64},{96,112},{112,96},{1... | collective-permute-start | bytes 49160 | tf_op jit(solution)/shard_map/ppermute | solution.py:309
  48.3 7.7 %collective-permute-start.11 = (f32[32,128]{1,0:T(8,128)S(1)}, f32[32,128]{1,0:T(8,128)S(1)}, u32[]{:S(2)}, u32[]{:S(2)}) collective-permute-start(f32[32,128]{1,0:T(8,128)S(1)} %get-tuple-element.43), channel_id=1, source_target_pairs={{16,32},{48,64},{80,96},{112,128},{144,160},{176,192},{208,224},{2... | collective-permute-start | bytes 49160 | tf_op jit(solution)/shard_map/ppermute | solution.py:310
  50.4 5.6 %collective-permute-start.14 = (f32[16,128]{1,0:T(8,128)S(1)}, f32[16,128]{1,0:T(8,128)S(1)}, u32[]{:S(2)}, u32[]{:S(2)}) collective-permute-start(f32[16,128]{1,0:T(8,128)S(1)} %get-tuple-element.46), channel_id=1, source_target_pairs={{0,1},{1,0},{2,3},{3,2},{4,5},{5,4},{6,7},{7,6},{8,9},{9,8},{10,11... | collective-permute-start | bytes 24584 | tf_op jit(solution)/shard_map/ppermute | solution.py:313
  51.8 2.4 %collective-permute-start.12 = (f32[1,512]{1,0:T(1,128)S(1)}, f32[1,512]{1,0:T(1,128)S(1)}, u32[]{:S(2)}, u32[]{:S(2)}) collective-permute-start(f32[1,512]{1,0:T(1,128)S(1)} %get-tuple-element.44), channel_id=1, source_target_pairs={{0,2},{2,0},{4,6},{6,4},{8,10},{10,8},{12,14},{14,12},{1,3},{3,1},... | collective-permute-start | bytes 6152 | tf_op jit(solution)/shard_map/ppermute | solution.py:311
  52.1 3.9 %collective-permute-start.13 = (f32[1,512]{1,0:T(1,128)S(1)}, f32[1,512]{1,0:T(1,128)S(1)}, u32[]{:S(2)}, u32[]{:S(2)}) collective-permute-start(f32[1,512]{1,0:T(1,128)S(1)} %get-tuple-element.45), channel_id=1, source_target_pairs={{2,4},{6,8},{10,12},{14,0},{4,2},{8,6},{12,10},{0,14},{3,5},{7,9},... | collective-permute-start | bytes 6152 | tf_op jit(solution)/shard_map/ppermute | solution.py:312
  70.2 23.8 %all-to-all-start.2 = ((f32[256,2,128]{2,1,0:T(2,128)}), f32[256,2,128]{2,1,0:T(2,128)S(1)}, u32[]{:S(2)}, u32[]{:S(2)}) async-start(f32[256,2,128]{2,1,0:T(2,128)} %bitcast.11), calls=%async_computation.2 | async-start | bytes 524288 | tf_op jit(solution)/shard_map/all_to_all | solution.py:411

commit v3 on v2

--- a/solution.py
+++ b/solution.py
@@ -206,85 +206,113 @@
 
 
 def last_kernel(
-    sizes, kept_ref, xe, xo, ye, yo, z, tracer_ref, gradient_in, adjoint_ref, lines_ref, work_ref
+    sizes, length, kept_ref, xe, xo, ye, yo, z, tracer_ref, gradient_in, adjoint_hbm, out_ref, work_ref, lines_ref, sem
 ):
-    rows = kept_ref.shape[0]
+    rows, lanes = kept_ref.shape
     depth = xe.shape[0]
     across = rows // depth
     adjoint = join(sizes, kept_ref, xe, xo, ye, yo, z)
-    adjoint_ref[...] = adjoint
-    work_ref[...] = gradient_in[...] + adjoint * tracer_ref[0]
-    for x in range(across):
-        lines_ref[x * depth : (x + 1) * depth, :] = work_ref[pl.ds(x, depth, stride=across), :]
-
-
-def smooth_y_kernel(depth, length, rows_each, lines_ref, out_ref):
-    rows, lanes = lines_ref.shape
-    lines = lines_ref[...]
-    share = 2 * depth
-    groups = lanes // rows_each
-    scale = 1.0 / math.sqrt(length)
-    order = iota((lanes, lanes), 0)
-    y_out = (order % groups) * rows_each + order // groups
-    table = jnp.exp(-jnp.abs(y_out - iota((lanes, lanes), 1)).astype(F32) / length) * scale
-    side = iota((8, lanes), 0)
-    y_in = iota((8, lanes), 1)
-    carry_table = jnp.exp(-jnp.where(side == 0, lanes - 1 - y_in, y_in).astype(F32) / length) * scale
-    both = dot3(jnp.concatenate([table, carry_table], axis=0), lines, ((1,), (1,)))
-    result, carry = both[:lanes], both[lanes:]
-    place = iota((8, rows), 1)
-    decay = math.exp(-lanes / length)
-    right = carry
-    left = carry
-    step = share
-    factor = decay
-    while step < rows:
-        right = right + factor * jnp.where(place >= step, pltpu.roll(right, step, 1), 0.0)
-        left = left + factor * jnp.where(place < rows - step, pltpu.roll(left, rows - step, 1), 0.0)
-        step, factor = 2 * step, factor * factor
-    right = jnp.where(place >= share, pltpu.roll(right, share, 1), 0.0)[0:1, :]
-    left = jnp.where(place < rows - share, pltpu.roll(left, rows - share, 1), 0.0)[1:2, :]
-    row = iota((lanes, 1), 0)
-    y_row = ((row % groups) * rows_each + row // groups).astype(F32)
-    result = (
-        result + jnp.exp(-(y_row + 1.0) / length) * right + jnp.exp(-(lanes - y_row) / length) * left
-    )
-    per_tile = lanes // depth
-    quarter = iota((groups, lanes), 1) // depth
+    work_ref[...] = adjoint
+    copy = pltpu.make_async_copy(work_ref, adjoint_hbm, sem)
+    copy.start()
+    lines_ref[...] = gradient_in[...] + adjoint * tracer_ref[0]
+    lines = jnp.concatenate(
+        [lines_ref[pl.ds(x, depth, stride=across), :] for x in range(across)], axis=0
+    )
+    rows_each = lanes // depth
+    places = lanes // (sizes[1] * rows_each)
+    group = sizes[1] * (places + 1)
+    order = iota((rows_each * group, lanes), 0)
+    r, j, e = order // group, order % group // (places + 1), order % (places + 1)
+    y_out = y_of(sizes, lanes, rows_each, e, j, r)
+    y_out = jnp.where(e < places, y_out, jnp.where(r == 0, lanes - 1, 0))
+    table = jnp.exp(-jnp.abs(y_out - iota(order.shape, 1)).astype(F32) / length) * (1.0 / math.sqrt(length))
+    result = dot3(table, lines, ((1,), (1,)))
+    quarter = iota((group, lanes), 1) // depth
     for tile in range(rows // lanes):
-        pieces = [
-            result[r * groups : (r + 1) * groups, tile * lanes : (tile + 1) * lanes]
-            for r in range(rows_each)
-        ]
-        for u in range(per_tile):
-            line = tile * per_tile + u
-            block, xx = line // 2, line % 2
-            chunk = jnp.zeros((groups, lanes), F32)
+        pieces = [result[r * group : (r + 1) * group, tile * lanes : (tile + 1) * lanes] for r in range(rows_each)]
+        for u in range(rows_each):
+            chunk = jnp.zeros((group, lanes), F32)
             for r in range(rows_each):
                 turn = ((r - u) * depth) % lanes
-                piece = pltpu.roll(pieces[r], turn, 1) if turn else pieces[r]
-                chunk = jnp.where(quarter == r, piece, chunk)
-            out_ref[pl.ds(block * 2 * groups + xx, groups, stride=2), :] = chunk
-
-
-def smooth_xz_kernel(depth, length_x, length_z, rows_each, data_ref, out_hbm, work_ref, sems):
-    rows, lanes = data_ref.shape
+                chunk = jnp.where(quarter == r, pltpu.roll(pieces[r], turn, 1) if turn else pieces[r], chunk)
+            out_ref[pl.ds(tile * rows_each + u, group, stride=across), :] = chunk
+    copy.wait()
+
+
+def y_of(sizes, lanes, rows_each, place, gy, r):
+    high, low = place // sizes[2], place % sizes[2]
+    return high * (sizes[1] * sizes[2] * rows_each) + gy * (sizes[2] * rows_each) + low * rows_each + r
+
+
+def carry_kernel(sizes, depth, across, length, lines_ref, out_ref):
+    lanes = lines_ref.shape[1]
+    bricks = sizes[1]
+    rows_each = lanes // depth
+    places = lanes // (bricks * rows_each)
+    block = (places + 1) * across
+    lane = iota((across, lanes), 1)
+
+    def spread(values, group):
+        values = jnp.where(lane // depth == group, values, 0.0)
+        if group:
+            values = pltpu.roll(values, lanes - group * depth, 1)
+        step = depth
+        while step < lanes:
+            values = values + pltpu.roll(values, step, 1)
+            step = 2 * step
+        return values
+
+    carries = [lines_ref[g * block + places * across : (g + 1) * block, :] for g in range(bricks)]
+    decay = math.exp(-lanes / length)
+    below, above = [None] * bricks, [None] * bricks
+    total = jnp.zeros((across, lanes), F32)
+    for g in range(bricks):
+        below[g] = total
+        total = decay * total + spread(carries[g], 0)
+    total = jnp.zeros((across, lanes), F32)
+    for g in reversed(range(bricks)):
+        above[g] = total
+        total = decay * total + spread(carries[g], 1)
+    first_core = lax.axis_index("gz") == 0
+    gy = lax.axis_index("gy")
+    for high in range(places // sizes[2]):
+        factors = []
+        for low in range(sizes[2]):
+            y = y_of(sizes, lanes, rows_each, high * sizes[2] + low, gy, iota((1, lanes), 1) // depth)
+            y = y.astype(F32)
+            factors.append((jnp.exp(-(y + 1.0) / length), jnp.exp(-(lanes - y) / length)))
+        for g in range(bricks):
+            values = []
+            for low in range(sizes[2]):
+                start = g * block + (high * sizes[2] + low) * across
+                here = lines_ref[start : start + across, :]
+                values.append(here + factors[low][0] * below[g] + factors[low][1] * above[g])
+            start = (g * (places // sizes[2]) + high) * sizes[2] * across
+            out_ref[start : start + across, :] = jnp.where(first_core, values[1], values[0])
+            out_ref[start + across : start + 2 * across, :] = jnp.where(first_core, values[0], values[1])
+
+
+def smooth_xz_kernel(depth, across, length_x, length_z, data_ref, other_ref, out_hbm, work_ref, sems):
+    lanes = data_ref.shape[1]
     full_x = work_ref.shape[1]
-    sources = rows // 4
-    part = [jnp.zeros((lanes, full_x), F32) for _ in range(2)]
-    for xx in range(2):
-        x_in = 2 * iota((sources, full_x), 0) + xx
-        table = jnp.exp(-jnp.abs(x_in - iota((sources, full_x), 1)).astype(F32) / length_x)
-        table = table * (1.0 / math.sqrt(length_x))
-        for g in range(2):
-            block = data_ref[pl.ds(2 * g + xx, sources, stride=4), :]
-            part[g] = part[g] + dot3(block, table, ((0,), (0,)))
+    rows_each = lanes // depth
+    gz = lax.axis_index("gz")
+    x_in, x_out = iota((full_x, full_x), 0), iota((full_x, full_x), 1)
+    table = jnp.exp(-jnp.abs(x_in - x_out).astype(F32) / length_x) * (1.0 / math.sqrt(length_x))
+    own = jnp.concatenate(
+        [data_ref[(2 * g + 1) * across : (2 * g + 2) * across, :] for g in range(full_x // across)], axis=0
+    )
+    own = dot3(own, table, ((0,), (0,)))
+    other = dot3(other_ref[...], table, ((0,), (0,)))
     full_z = 2 * depth
     z_out, z_in = iota((full_z, full_z), 0), iota((full_z, full_z), 1)
+    z_in = z_in % depth + jnp.where(z_in < depth, gz, 1 - gz) * depth
     table = jnp.exp(-jnp.abs(z_out - z_in).astype(F32) / length_z) * (1.0 / math.sqrt(length_z))
     copies = []
     for r in range(rows_each):
-        column = jnp.concatenate([part[g][r * depth : (r + 1) * depth] for g in range(2)], axis=0)
+        part = slice(r * depth, (r + 1) * depth)
+        column = jnp.concatenate([own[part], other[part]], axis=0)
         here = slice(r * full_z, (r + 1) * full_z)
         work_ref[here, :] = dot3(table, column, ((1,), (0,)))
         copy = pltpu.make_async_copy(work_ref.at[here], out_hbm.at[here], sems.at[r])
@@ -314,15 +342,16 @@
     )
 
 
-def local(kernel, name, inputs, outputs, scratch=(), far=0, far_out=False):
+def local(kernel, name, inputs, outputs, scratch=(), far=0, far_outputs=()):
     vmem = pl.BlockSpec(memory_space=pltpu.VMEM)
     hbm = pl.BlockSpec(memory_space=pl.ANY)
     near = len(inputs) - far
+    out_far = [i in far_outputs for i in range(len(outputs))]
     return pl.pallas_call(
         kernel,
         in_specs=[vmem] * near + [hbm] * far,
-        out_specs=[hbm if far_out else vmem] * len(outputs),
-        out_shape=[(pltpu.HBM if far_out else pltpu.VMEM)(dims, F32) for dims in outputs],
+        out_specs=[hbm if away else vmem for away in out_far],
+        out_shape=[(pltpu.HBM if away else pltpu.VMEM)(dims, F32) for dims, away in zip(outputs, out_far)],
         scratch_shapes=scratch,
         compiler_params=pltpu.CompilerParams(vmem_limit_bytes=8 << 20),
         name=name,
@@ -394,31 +423,35 @@
                 [kept, *arrived, speed, flow],
                 [field] + face_shapes,
             )
+    rows_each = sizes[1] * brick_y // devices
+    block = (brick_y // (sizes[1] * rows_each) + 1) * brick_x
+    length_y = 2.0 * brick_y
     adjoint, lines = local(
-        functools.partial(last_kernel, sizes),
+        functools.partial(last_kernel, sizes, length_y),
         "join0",
         [kept, *arrived, trace, *gradient],
-        [field, field],
-        [pltpu.VMEM(field, F32)],
-    )
-    y_lines = lax.all_to_all(
-        lines.reshape(sizes[1], rows // sizes[1], brick_y), "gy", split_axis=0, concat_axis=0, tiled=True
-    ).reshape(rows, brick_y)
-    rows_each = sizes[1] * brick_y // devices
-    (smooth,) = local(
-        functools.partial(smooth_y_kernel, brick_z, 2.0 * brick_y, rows_each), "smooth_y", [y_lines], [field]
+        [field, (sizes[1] * block, brick_y)],
+        [pltpu.VMEM(field, F32), pltpu.VMEM(field, F32), pltpu.SemaphoreType.DMA],
+        far_outputs=(0,),
+    )
+    lines = lax.all_to_all(
+        lines.reshape(sizes[1], block, brick_y), "gy", split_axis=0, concat_axis=0, tiled=True
+    ).reshape(sizes[1] * block, brick_y)
+    (planes,) = local(
+        functools.partial(carry_kernel, sizes, brick_z, brick_x, length_y), "carry", [lines], [field]
     )
     planes = lax.all_to_all(
-        smooth.reshape(devices, 2, 128), axes, split_axis=0, concat_axis=0, tiled=True
-    ).reshape(rows, brick_y)
+        planes.reshape(sizes[0], sizes[2] * brick_x, brick_y), "gx", split_axis=0, concat_axis=0, tiled=True
+    )
     full_x, full_z = sizes[0] * brick_x, sizes[2] * brick_z
+    other = lax.ppermute(planes[:, :brick_x], "gz", [(0, 1), (1, 0)])
     (smoothed,) = local(
-        functools.partial(smooth_xz_kernel, brick_z, 2.0 * brick_x, 2.0 * brick_z, rows_each),
+        functools.partial(smooth_xz_kernel, brick_z, brick_x, 2.0 * brick_x, 2.0 * brick_z),
         "smooth_xz",
-        [planes],
+        [planes.reshape(field), other.reshape(full_x, brick_y)],
         [(rows_each * full_z, full_x)],
         [pltpu.VMEM((rows_each * full_z, full_x), F32), pltpu.SemaphoreType.DMA((rows_each,))],
-        far_out=True,
+        far_outputs=(0,),
     )
     return (
         adjoint.reshape(brick_z, brick_x, brick_y),

time: 95.8 us -> 89.6 us (0.935)
  waiting for transfers between devices: 24.7 us -> 10.4 us
  blocking collectives: 40.1 us -> 52.1 us
  starting transfers between devices: 22 us -> 19.2 us
    all_to_all x1 -> x0, waiting for transfers between devices: 15.3 us -> none  [per_device(): lax.all_to_all(smooth.reshape(devices, 2, 128), axes, split_axis=0, conca...]
    all_to_all x1 -> x2, blocking collectives: 12.6 us -> 24.6 us  [the longest x1 13.6 us: per_device(): lax.all_to_all(lines.reshape(sizes[1], block, brick_y), 'gy', split_axis=...]
    all_to_all x1 -> x0, starting transfers between devices: 7.75 us -> none  [per_device(): lax.all_to_all(smooth.reshape(devices, 2, 128), axes, split_axis=0, conca...]
    ppermute x0 -> x1, starting transfers between devices: none -> 4.97 us  [per_device(): other = lax.ppermute(planes[:, :brick_x], 'gz', [(0, 1), (1, 0)])]
    ppermute x0 -> x1, waiting for transfers between devices: none -> 0.99 us  [per_device(): other = lax.ppermute(planes[:, :brick_x], 'gz', [(0, 1), (1, 0)])]
  transfers between devices with their start and end apart: 16 -> 16, of which waited for: 7 -> 7; matrix products, arithmetic and copies ran while one was open for 1% -> 0% of each run, Pallas kernels for 1% -> 1%
where the time goes in v3:
time: 89.6 us; the launch traced here: 89.3 us
  blocking collectives  52.1 us (58%)
  starting transfers between devices  19.2 us (21%)
  waiting for transfers between devices  10.4 us (12%)
  Pallas kernels  6.61 us (7%)
  between operations  0.91 us (1%)
    all_to_all x1, blocking collectives, per_device(): lax.all_to_all(outgoing.reshape(owners, CAP, 128), ('gx', 'gy'), split_ax...  27.5 us
    all_to_all x1, blocking collectives, per_device(): lax.all_to_all(lines.reshape(sizes[1], block, brick_y), 'gy', split_axis=...  13.6 us
    all_to_all x1, blocking collectives, per_device(): lax.all_to_all(planes.reshape(sizes[0], sizes[2] * brick_x, brick_y), 'gx...  11 us
    pallas_call x10, Pallas kernels, local(): pl.pallas_call(kernel, in_specs=[vmem] * near + [hbm] * far, out_specs=[h...  6.61 us
    ppermute x3, starting transfers between devices, exchange(): lax.ppermute(xo, 'gx', x_odd)  6.34 us
    ppermute x3, starting transfers between devices, exchange(): lax.ppermute(z, 'gz', [(0, 1), (1, 0)])  5.79 us
    ppermute x1, starting transfers between devices, per_device(): other = lax.ppermute(planes[:, :brick_x], 'gz', [(0, 1), (1, 0)])  4.97 us
    ppermute x3, waiting for transfers between devices, exchange(): lax.ppermute(ye, 'gy', y_even)  4.76 us
  transfers between devices with their start and end apart: 16, of which 7 were waited for; matrix products, arithmetic and copies ran while one was open for 0% of the time, Pallas kernels for 1%

profile of v3, /device:TPU:1, one launch (start us, length us, event | category | flops | bytes accessed | tf_op | source)
XLA Modules:
  0.0 89.3 jit_solution(7965458348777031601)
XLA Ops:
  0.6 1.1 %dispatch.1 = f32[256,128]{1,0:T(8,128)S(1)} custom-call(f32[32,96]{1,0:T(8,128)} %bitcast.38, s32[1,96]{1,0:T(1,128)} %bitcast.39, s32[1,96]{1,0:T(1,128)} %bitcast.40), custom_call_target="tpu_custom_call" | custom-call | tf_op jit(solution)/shard_map/dispatch/pallas_call | solution.py:350
  1.7 27.5 %all_to_all.15 = f32[128,2,128]{2,1,0:T(2,128)S(1)} all-to-all(f32[128,2,128]{2,1,0:T(2,128)S(1)} %bitcast.33), channel_id=1, replica_groups=mesh['gx'=16,'gy'=8,'gz'=2] {'gx','gy'}, dimensions={0} | all-to-all | bytes 262144 | tf_op jit(solution)/shard_map/all_to_all | solution.py:385
  29.3 0.0 copy-start
  29.3 0.0 copy-start.1
  29.3 1.5 %first.1 = (f32[512,128]{1,0:T(8,128)S(1)}, f32[32,128]{1,0:T(8,128)S(1)}, f32[32,128]{1,0:T(8,128)S(1)}, f32[1,512]{1,0:T(1,128)S(1)}, f32[1,512]{1,0:T(1,128)S(1)}, /*index=5*/f32[16,128]{1,0:T(8,128)S(1)}) custom-call(f32[256,128]{1,0:T(8,128)S(1)} %bitcast.34, f32[3,512,128]{2,1,0:T(8,128)} %bitcast.15, s32[3,512,128]{2,1,0:T(8,128)} %bitcast.21), custom_call_target="tpu_custom_call" | custom-call | tf_op jit(solution)/shard_map/first/pallas_call | solution.py:350
  30.7 0.1 collective-permute-start
  30.8 1.3 %collective-permute-start.1 = (f32[32,128]{1,0:T(8,128)S(1)}, f32[32,128]{1,0:T(8,128)S(1)}, u32[]{:S(2)}, u32[]{:S(2)}) collective-permute-start(f32[32,128]{1,0:T(8,128)S(1)} %get-tuple-element.28), channel_id=1, source_target_pairs={{16,32},{48,64},{80,96},{112,128},{144,160},{176,192},{208,224},{2... | collective-permute-start | bytes 49160 | tf_op jit(solution)/shard_map/ppermute | solution.py:338
  32.1 2.7 %collective-permute-start.4 = (f32[16,128]{1,0:T(8,128)S(1)}, f32[16,128]{1,0:T(8,128)S(1)}, u32[]{:S(2)}, u32[]{:S(2)}) collective-permute-start(f32[16,128]{1,0:T(8,128)S(1)} %get-tuple-element.31), channel_id=1, source_target_pairs={{0,1},{1,0},{2,3},{3,2},{4,5},{5,4},{6,7},{7,6},{8,9},{9,8},{10,11... | collective-permute-start | bytes 24584 | tf_op jit(solution)/shard_map/ppermute | solution.py:341
  34.8 0.4 collective-permute-start.2
  35.2 0.0 collective-permute-start.3
  35.2 0.0 copy-done
  35.2 0.0 copy-done.1
  35.2 0.3 inner2.1.kept_ref
  35.6 0.0 copy-start.2
  35.6 1.6 %collective-permute-done.2.ye = f32[1,512]{1,0:T(1,128)S(1)} collective-permute-done((f32[1,512]{1,0:T(1,128)S(1)}, f32[1,512]{1,0:T(1,128)S(1)}, u32[]{:S(2)}, u32[]{:S(2)}) %collective-permute-start.2) | collective-permute-done | bytes 2080 | tf_op jit(solution)/shard_map/ppermute | solution.py:339
  37.2 1.9 %collective-permute-done.3.yo = f32[1,512]{1,0:T(1,128)S(1)} collective-permute-done((f32[1,512]{1,0:T(1,128)S(1)}, f32[1,512]{1,0:T(1,128)S(1)}, u32[]{:S(2)}, u32[]{:S(2)}) %collective-permute-start.3) | collective-permute-done | bytes 2080 | tf_op jit(solution)/shard_map/ppermute | solution.py:340
  39.1 0.0 collective-permute-done.4.z
  39.1 0.0 collective-permute-done.xe
  39.1 0.0 collective-permute-done.1.xo
  39.1 0.3 join2.1
  39.4 0.1 collective-permute-start.5
  39.5 3.0 %collective-permute-start.6 = (f32[32,128]{1,0:T(8,128)S(1)}, f32[32,128]{1,0:T(8,128)S(1)}, u32[]{:S(2)}, u32[]{:S(2)}) collective-permute-start(f32[32,128]{1,0:T(8,128)S(1)} %get-tuple-element.35), channel_id=1, source_target_pairs={{16,32},{48,64},{80,96},{112,128},{144,160},{176,192},{208,224},{2... | collective-permute-start | bytes 49160 | tf_op jit(solution)/shard_map/ppermute | solution.py:338
  42.6 1.7 %collective-permute-start.9 = (f32[16,128]{1,0:T(8,128)S(1)}, f32[16,128]{1,0:T(8,128)S(1)}, u32[]{:S(2)}, u32[]{:S(2)}) collective-permute-start(f32[16,128]{1,0:T(8,128)S(1)} %get-tuple-element.38), channel_id=1, source_target_pairs={{0,1},{1,0},{2,3},{3,2},{4,5},{5,4},{6,7},{7,6},{8,9},{9,8},{10,11... | collective-permute-start | bytes 24584 | tf_op jit(solution)/shard_map/ppermute | solution.py:341
  44.3 0.0 collective-permute-start.7
  44.3 0.6 collective-permute-start.8
  44.9 0.0 copy-done.2
  44.9 0.3 inner1.1
  45.2 1.8 %collective-permute-done.7.ye = f32[1,512]{1,0:T(1,128)S(1)} collective-permute-done((f32[1,512]{1,0:T(1,128)S(1)}, f32[1,512]{1,0:T(1,128)S(1)}, u32[]{:S(2)}, u32[]{:S(2)}) %collective-permute-start.7) | collective-permute-done | bytes 2080 | tf_op jit(solution)/shard_map/ppermute | solution.py:339
  47.0 0.9 %collective-permute-done.8.yo = f32[1,512]{1,0:T(1,128)S(1)} collective-permute-done((f32[1,512]{1,0:T(1,128)S(1)}, f32[1,512]{1,0:T(1,128)S(1)}, u32[]{:S(2)}, u32[]{:S(2)}) %collective-permute-start.8) | collective-permute-done | bytes 2080 | tf_op jit(solution)/shard_map/ppermute | solution.py:340
  47.9 0.0 collective-permute-done.9.z
  47.9 0.0 collective-permute-done.5.xe
  47.9 0.0 collective-permute-done.6.xo
  47.9 0.3 join1.1
  48.2 0.1 collective-permute-start.10
  48.3 2.1 %collective-permute-start.11 = (f32[32,128]{1,0:T(8,128)S(1)}, f32[32,128]{1,0:T(8,128)S(1)}, u32[]{:S(2)}, u32[]{:S(2)}) collective-permute-start(f32[32,128]{1,0:T(8,128)S(1)} %get-tuple-element.43), channel_id=1, source_target_pairs={{16,32},{48,64},{80,96},{112,128},{144,160},{176,192},{208,224},{2... | collective-permute-start | bytes 49160 | tf_op jit(solution)/shard_map/ppermute | solution.py:338
  50.4 1.4 %collective-permute-start.14 = (f32[16,128]{1,0:T(8,128)S(1)}, f32[16,128]{1,0:T(8,128)S(1)}, u32[]{:S(2)}, u32[]{:S(2)}) collective-permute-start(f32[16,128]{1,0:T(8,128)S(1)} %get-tuple-element.46), channel_id=1, source_target_pairs={{0,1},{1,0},{2,3},{3,2},{4,5},{5,4},{6,7},{7,6},{8,9},{9,8},{10,11... | collective-permute-start | bytes 24584 | tf_op jit(solution)/shard_map/ppermute | solution.py:341
  51.8 0.3 collective-permute-start.12
  52.1 0.5 collective-permute-start.13
  52.6 0.3 inner0.1
  52.9 1.3 %collective-permute-done.12.ye = f32[1,512]{1,0:T(1,128)S(1)} collective-permute-done((f32[1,512]{1,0:T(1,128)S(1)}, f32[1,512]{1,0:T(1,128)S(1)}, u32[]{:S(2)}, u32[]{:S(2)}) %collective-permute-start.12) | collective-permute-done | bytes 2080 | tf_op jit(solution)/shard_map/ppermute | solution.py:339
  54.2 1.8 %collective-permute-done.13.yo = f32[1,512]{1,0:T(1,128)S(1)} collective-permute-done((f32[1,512]{1,0:T(1,128)S(1)}, f32[1,512]{1,0:T(1,128)S(1)}, u32[]{:S(2)}, u32[]{:S(2)}) %collective-permute-start.13) | collective-permute-done | bytes 2080 | tf_op jit(solution)/shard_map/ppermute | solution.py:340
  56.0 0.0 collective-permute-done.14.z
  56.0 0.0 collective-permute-done.10.xe
  56.0 0.0 collective-permute-done.11.xo
  56.0 1.0 %join0.1 = (f32[512,128]{1,0:T(8,128)}, f32[640,128]{1,0:T(8,128)S(1)}) custom-call(f32[512,128]{1,0:T(8,128)S(1)} %get-tuple-element.41.kept_ref, f32[32,128]{1,0:T(8,128)S(1)} %collective-permute-done.10.xe, f32[32,128]{1,0:T(8,128)S(1)} %collective-permute-done.11.xo, f32[1,512]{1,0:T(1,128)S(1)} %collective-permute-done.12.ye, ...), custom_call_target="tpu_custom_call" | custom-call | tf_op jit(solution)/shard_map/join0/pallas_call | solution.py:350
  57.0 13.6 %all_to_all.16 = f32[8,80,128]{2,1,0:T(8,128)S(1)} all-to-all(f32[8,80,128]{2,1,0:T(8,128)S(1)} %bitcast.35), channel_id=1, replica_groups=mesh['gx'=16,'gy'=8,'gz'=2] {'gy'}, dimensions={0} | all-to-all | bytes 655360 | tf_op jit(solution)/shard_map/all_to_all | solution.py:437
  70.6 0.2 carry.1
  70.9 11.0 %all_to_all.17 = f32[16,32,128]{2,1,0:T(8,128)S(1)} all-to-all(f32[16,32,128]{2,1,0:T(8,128)S(1)} %bitcast.32), channel_id=1, replica_groups=mesh['gx'=16,'gy'=8,'gz'=2] {'gx'}, dimensions={0} | all-to-all | bytes 524288 | tf_op jit(solution)/shard_map/all_to_all | solution.py:443
  81.9 5.0 %collective-permute-start.15 = (f32[16,16,128]{2,1,0:T(8,128)S(1)}, f32[16,16,128]{2,1,0:T(8,128)S(1)}, u32[]{:S(2)}, u32[]{:S(2)}) collective-permute-start(f32[16,16,128]{2,1,0:T(8,128)S(1)} %slice.4), channel_id=1, source_target_pairs={{0,1},{1,0},{2,3},{3,2},{4,5},{5,4},{6,7},{7,6},{8,9},{9,8},{10,11... | collective-permute-start | bytes 393224 | tf_op jit(solution)/shard_map/ppermute | solution.py:447
  86.9 1.0 %collective-permute-done.15 = f32[16,16,128]{2,1,0:T(8,128)S(1)} collective-permute-done((f32[16,16,128]{2,1,0:T(8,128)S(1)}, f32[16,16,128]{2,1,0:T(8,128)S(1)}, u32[]{:S(2)}, u32[]{:S(2)}) %collective-permute-start.15) | collective-permute-done | bytes 131104 | tf_op jit(solution)/shard_map/ppermute | solution.py:447
  87.9 1.3 %smooth_xz.1 = f32[256,256]{1,0:T(8,128)} custom-call(f32[512,128]{1,0:T(8,128)S(1)} %bitcast.30, f32[256,128]{1,0:T(8,128)S(1)} %bitcast.36), custom_call_target="tpu_custom_call" | custom-call | tf_op jit(solution)/shard_map/smooth_xz/pallas_call | solution.py:350
  (1 shorter events, 0.0 us)
Async XLA Ops:
  29.3 6.0 %copy-start = (f32[3,32,16,128]{3,2,1,0:T(8,128)S(1)}, f32[3,32,16,128]{3,2,1,0:T(8,128)}, u32[]{:S(2)}) copy-start(f32[3,32,16,128]{3,2,1,0:T(8,128)} %param.10) | copy-start | bytes 2359300
  29.3 6.0 %copy-start.1 = (s32[3,32,16,128]{3,2,1,0:T(8,128)S(1)}, s32[3,32,16,128]{3,2,1,0:T(8,128)}, u32[]{:S(2)}) copy-start(s32[3,32,16,128]{3,2,1,0:T(8,128)} %param.9) | copy-start | bytes 2359300
  30.7 8.4 %collective-permute-start = (f32[32,128]{1,0:T(8,128)S(1)}, f32[32,128]{1,0:T(8,128)S(1)}, u32[]{:S(2)}, u32[]{:S(2)}) collective-permute-start(f32[32,128]{1,0:T(8,128)S(1)} %get-tuple-element.27), channel_id=1, source_target_pairs={{0,16},{16,0},{32,48},{48,32},{64,80},{80,64},{96,112},{112,96},{1... | collective-permute-start | bytes 49160 | tf_op jit(solution)/shard_map/ppermute | solution.py:337
  30.8 8.3 %collective-permute-start.1 = (f32[32,128]{1,0:T(8,128)S(1)}, f32[32,128]{1,0:T(8,128)S(1)}, u32[]{:S(2)}, u32[]{:S(2)}) collective-permute-start(f32[32,128]{1,0:T(8,128)S(1)} %get-tuple-element.28), channel_id=1, source_target_pairs={{16,32},{48,64},{80,96},{112,128},{144,160},{176,192},{208,224},{2... | collective-permute-start | bytes 49160 | tf_op jit(solution)/shard_map/ppermute | solution.py:338
  32.1 7.0 %collective-permute-start.4 = (f32[16,128]{1,0:T(8,128)S(1)}, f32[16,128]{1,0:T(8,128)S(1)}, u32[]{:S(2)}, u32[]{:S(2)}) collective-permute-start(f32[16,128]{1,0:T(8,128)S(1)} %get-tuple-element.31), channel_id=1, source_target_pairs={{0,1},{1,0},{2,3},{3,2},{4,5},{5,4},{6,7},{7,6},{8,9},{9,8},{10,11... | collective-permute-start | bytes 24584 | tf_op jit(solution)/shard_map/ppermute | solution.py:341
  34.8 2.4 %collective-permute-start.2 = (f32[1,512]{1,0:T(1,128)S(1)}, f32[1,512]{1,0:T(1,128)S(1)}, u32[]{:S(2)}, u32[]{:S(2)}) collective-permute-start(f32[1,512]{1,0:T(1,128)S(1)} %get-tuple-element.29), channel_id=1, source_target_pairs={{0,2},{2,0},{4,6},{6,4},{8,10},{10,8},{12,14},{14,12},{1,3},{3,1},... | collective-permute-start | bytes 6152 | tf_op jit(solution)/shard_map/ppermute | solution.py:339
  35.2 3.9 %collective-permute-start.3 = (f32[1,512]{1,0:T(1,128)S(1)}, f32[1,512]{1,0:T(1,128)S(1)}, u32[]{:S(2)}, u32[]{:S(2)}) collective-permute-start(f32[1,512]{1,0:T(1,128)S(1)} %get-tuple-element.30), channel_id=1, source_target_pairs={{2,4},{6,8},{10,12},{14,0},{4,2},{8,6},{12,10},{0,14},{3,5},{7,9},... | collective-permute-start | bytes 6152 | tf_op jit(solution)/shard_map/ppermute | solution.py:340
  35.6 9.4 %copy-start.2 = (f32[3,32,16,128]{3,2,1,0:T(8,128)S(1)}, f32[3,32,16,128]{3,2,1,0:T(8,128)}, u32[]{:S(2)}) copy-start(f32[3,32,16,128]{3,2,1,0:T(8,128)} %param.11) | copy-start | bytes 2359300
  39.4 8.5 %collective-permute-start.5 = (f32[32,128]{1,0:T(8,128)S(1)}, f32[32,128]{1,0:T(8,128)S(1)}, u32[]{:S(2)}, u32[]{:S(2)}) collective-permute-start(f32[32,128]{1,0:T(8,128)S(1)} %get-tuple-element.34), channel_id=1, source_target_pairs={{0,16},{16,0},{32,48},{48,32},{64,80},{80,64},{96,112},{112,96},{1... | collective-permute-start | bytes 49160 | tf_op jit(solution)/shard_map/ppermute | solution.py:337
  39.5 8.4 %collective-permute-start.6 = (f32[32,128]{1,0:T(8,128)S(1)}, f32[32,128]{1,0:T(8,128)S(1)}, u32[]{:S(2)}, u32[]{:S(2)}) collective-permute-start(f32[32,128]{1,0:T(8,128)S(1)} %get-tuple-element.35), channel_id=1, source_target_pairs={{16,32},{48,64},{80,96},{112,128},{144,160},{176,192},{208,224},{2... | collective-permute-start | bytes 49160 | tf_op jit(solution)/shard_map/ppermute | solution.py:338
  42.6 5.4 %collective-permute-start.9 = (f32[16,128]{1,0:T(8,128)S(1)}, f32[16,128]{1,0:T(8,128)S(1)}, u32[]{:S(2)}, u32[]{:S(2)}) collective-permute-start(f32[16,128]{1,0:T(8,128)S(1)} %get-tuple-element.38), channel_id=1, source_target_pairs={{0,1},{1,0},{2,3},{3,2},{4,5},{5,4},{6,7},{7,6},{8,9},{9,8},{10,11... | collective-permute-start | bytes 24584 | tf_op jit(solution)/shard_map/ppermute | solution.py:341
  44.3 2.7 %collective-permute-start.7 = (f32[1,512]{1,0:T(1,128)S(1)}, f32[1,512]{1,0:T(1,128)S(1)}, u32[]{:S(2)}, u32[]{:S(2)}) collective-permute-start(f32[1,512]{1,0:T(1,128)S(1)} %get-tuple-element.36), channel_id=1, source_target_pairs={{0,2},{2,0},{4,6},{6,4},{8,10},{10,8},{12,14},{14,12},{1,3},{3,1},... | collective-permute-start | bytes 6152 | tf_op jit(solution)/shard_map/ppermute | solution.py:339
  44.3 3.6 %collective-permute-start.8 = (f32[1,512]{1,0:T(1,128)S(1)}, f32[1,512]{1,0:T(1,128)S(1)}, u32[]{:S(2)}, u32[]{:S(2)}) collective-permute-start(f32[1,512]{1,0:T(1,128)S(1)} %get-tuple-element.37), channel_id=1, source_target_pairs={{2,4},{6,8},{10,12},{14,0},{4,2},{8,6},{12,10},{0,14},{3,5},{7,9},... | collective-permute-start | bytes 6152 | tf_op jit(solution)/shard_map/ppermute | solution.py:340
  48.2 7.8 %collective-permute-start.10 = (f32[32,128]{1,0:T(8,128)S(1)}, f32[32,128]{1,0:T(8,128)S(1)}, u32[]{:S(2)}, u32[]{:S(2)}) collective-permute-start(f32[32,128]{1,0:T(8,128)S(1)} %get-tuple-element.42), channel_id=1, source_target_pairs={{0,16},{16,0},{32,48},{48,32},{64,80},{80,64},{96,112},{112,96},{1... | collective-permute-start | bytes 49160 | tf_op jit(solution)/shard_map/ppermute | solution.py:337
  48.3 7.7 %collective-permute-start.11 = (f32[32,128]{1,0:T(8,128)S(1)}, f32[32,128]{1,0:T(8,128)S(1)}, u32[]{:S(2)}, u32[]{:S(2)}) collective-permute-start(f32[32,128]{1,0:T(8,128)S(1)} %get-tuple-element.43), channel_id=1, source_target_pairs={{16,32},{48,64},{80,96},{112,128},{144,160},{176,192},{208,224},{2... | collective-permute-start | bytes 49160 | tf_op jit(solution)/shard_map/ppermute | solution.py:338
  50.4 5.6 %collective-permute-start.14 = (f32[16,128]{1,0:T(8,128)S(1)}, f32[16,128]{1,0:T(8,128)S(1)}, u32[]{:S(2)}, u32[]{:S(2)}) collective-permute-start(f32[16,128]{1,0:T(8,128)S(1)} %get-tuple-element.46), channel_id=1, source_target_pairs={{0,1},{1,0},{2,3},{3,2},{4,5},{5,4},{6,7},{7,6},{8,9},{9,8},{10,11... | collective-permute-start | bytes 24584 | tf_op jit(solution)/shard_map/ppermute | solution.py:341
  51.8 2.4 %collective-permute-start.12 = (f32[1,512]{1,0:T(1,128)S(1)}, f32[1,512]{1,0:T(1,128)S(1)}, u32[]{:S(2)}, u32[]{:S(2)}) collective-permute-start(f32[1,512]{1,0:T(1,128)S(1)} %get-tuple-element.44), channel_id=1, source_target_pairs={{0,2},{2,0},{4,6},{6,4},{8,10},{10,8},{12,14},{14,12},{1,3},{3,1},... | collective-permute-start | bytes 6152 | tf_op jit(solution)/shard_map/ppermute | solution.py:339
  52.1 3.9 %collective-permute-start.13 = (f32[1,512]{1,0:T(1,128)S(1)}, f32[1,512]{1,0:T(1,128)S(1)}, u32[]{:S(2)}, u32[]{:S(2)}) collective-permute-start(f32[1,512]{1,0:T(1,128)S(1)} %get-tuple-element.45), channel_id=1, source_target_pairs={{2,4},{6,8},{10,12},{14,0},{4,2},{8,6},{12,10},{0,14},{3,5},{7,9},... | collective-permute-start | bytes 6152 | tf_op jit(solution)/shard_map/ppermute | solution.py:340
  81.9 6.0 %collective-permute-start.15 = (f32[16,16,128]{2,1,0:T(8,128)S(1)}, f32[16,16,128]{2,1,0:T(8,128)S(1)}, u32[]{:S(2)}, u32[]{:S(2)}) collective-permute-start(f32[16,16,128]{2,1,0:T(8,128)S(1)} %slice.4), channel_id=1, source_target_pairs={{0,1},{1,0},{2,3},{3,2},{4,5},{5,4},{6,7},{7,6},{8,9},{9,8},{10,11... | collective-permute-start | bytes 393224 | tf_op jit(solution)/shard_map/ppermute | solution.py:447

commit v4 on v3

v4 whole, which is shorter than its diff:
```python
import functools
import math

import jax
import jax.numpy as jnp
from jax import lax
from jax.experimental import pallas as pl
from jax.experimental.pallas import tpu as pltpu
from jax.sharding import PartitionSpec as P

F32 = jnp.float32
BF16 = jnp.bfloat16
CAP = 2


def iota(shape, dim):
    return lax.broadcasted_iota(jnp.int32, shape, dim)


def thirds(value):
    high = value.astype(BF16)
    left = value - high.astype(F32)
    middle = left.astype(BF16)
    low = (left - middle.astype(F32)).astype(BF16)
    return high, middle, low


def halves(value):
    high = value.astype(BF16)
    return high, (value - high.astype(F32)).astype(BF16)


def dot(left, right, dims):
    return lax.dot_general(left, right, (dims, ((), ())), preferred_element_type=F32)


def dot3(left, right, dims):
    lh, ll = halves(left)
    rh, rl = halves(right)
    return dot(lh, rh, dims) + (dot(lh, rl, dims) + dot(ll, rh, dims))


def fetch(copies, sems):
    started = [pltpu.make_async_copy(source, target, sems.at[i]) for i, (source, target) in enumerate(copies)]
    for copy in started:
        copy.start()
    return started


HALO = 3
PAD = 8
GROUP = 40


def open_kernel(sources_hbm, owner_hbm, cell_hbm, courant_hbm, sign_hbm, *rest):
    out_ref, even_ref, odd_ref, sources_ref, owner_ref, cell_ref, bits_ref, sems = rest
    gx, gy_count = lax.axis_index("gx"), lax.axis_size("gy")
    brick_x, brick_y = courant_hbm.shape[2], courant_hbm.shape[4]
    low, high = 0, brick_x - HALO
    is_even = (gx % 2) == 0
    first, second = jnp.where(is_even, high, low), jnp.where(is_even, low, high)
    copies = fetch(
        [
            (sources_hbm, sources_ref),
            (owner_hbm, owner_ref),
            (cell_hbm, cell_ref),
            (sign_hbm.at[:, :, pl.ds(first, HALO)], bits_ref.at[0]),
            (sign_hbm.at[:, :, pl.ds(second, HALO)], bits_ref.at[1]),
            (courant_hbm.at[:, :, pl.ds(first, HALO)], even_ref.at[0:3]),
            (courant_hbm.at[:, :, pl.ds(second, HALO)], odd_ref.at[0:3]),
        ],
        sems,
    )
    for copy in copies[:3]:
        copy.wait()
    depth, wells = sources_ref.shape
    chunks, lanes = out_ref.shape
    owner = owner_ref[...]
    owner_row = owner.astype(F32)
    owner_col = jnp.transpose(jnp.broadcast_to(owner_row, (8, wells)))[:, :1]
    earlier = iota((wells, wells), 0) < iota((wells, wells), 1)
    same = (owner_col == owner_row) & earlier
    rank = jnp.sum(same.astype(F32), axis=0, keepdims=True)
    cell = cell_ref[...]
    x = cell // brick_y
    far = float(-4 * chunks)
    target = CAP * owner_row + rank
    targets = [
        target,
        jnp.where(x >= high, target + CAP * gy_count, far),
        jnp.where(x < HALO, target - CAP * gy_count, far),
    ]
    row = iota((chunks, wells), 0).astype(F32)
    chosen = jnp.concatenate([jnp.where(row == t, 1.0, 0.0) for t in targets], axis=1).astype(BF16)
    column = jnp.concatenate(
        [sources_ref[...], jnp.broadcast_to(cell.astype(F32), (GROUP - depth, wells))], axis=0
    )
    payload = []
    for group in range(3):
        parts = [jnp.zeros((group * GROUP, wells), F32)] if group else []
        parts = parts + [column, jnp.zeros((lanes - (group + 1) * GROUP, wells), F32)]
        payload.append(jnp.concatenate(parts, axis=0))
    total = jnp.zeros((chunks, lanes), F32)
    for piece in thirds(jnp.concatenate(payload, axis=1)):
        total = total + dot(chosen, piece, ((1,), (1,)))
    out_ref[...] = total
    copies[3].wait()
    even_ref[3:6] = bits_ref[0].astype(F32)
    copies[4].wait()
    odd_ref[3:6] = bits_ref[1].astype(F32)
    copies[5].wait()
    copies[6].wait()


def load_kernel(gx_count, even_ref, odd_ref, courant_hbm, sign_hbm, courant_ref, sign_ref, sems):
    depth, across, lanes = courant_hbm.shape[1:]
    inside = slice(PAD, PAD + across)
    copies = fetch(
        [(courant_hbm.at[i], courant_ref.at[i, :, inside]) for i in range(3)]
        + [(sign_hbm.at[i], sign_ref.at[i, :, inside]) for i in range(3)],
        sems,
    )
    gx = lax.axis_index("gx")
    is_even = (gx % 2) == 0
    row = iota((depth, PAD, lanes), 1)
    for i in range(6):
        below = jnp.zeros((depth, PAD, lanes), F32)
        above = jnp.zeros((depth, PAD, lanes), F32)
        for d in range(HALO):
            xe = even_ref[i, pl.ds(d, depth, stride=HALO), :]
            xo = odd_ref[i, pl.ds(d, depth, stride=HALO), :]
            upper = jnp.where(gx == gx_count - 1, 0.0, jnp.where(is_even, xe, xo))
            lower = jnp.where(gx == 0, 0.0, jnp.where(is_even, xo, xe))
            above = jnp.where(row == d, upper[:, None, :], above)
            below = jnp.where(row == PAD - HALO + d, lower[:, None, :], below)
        if i < 3:
            courant_ref[i, :, 0:PAD] = below
            courant_ref[i, :, PAD + across :] = above
        else:
            sign_ref[i - 3, :, 0:PAD] = below.astype(jnp.int32)
            sign_ref[i - 3, :, PAD + across :] = above.astype(jnp.int32)
    for copy in copies:
        copy.wait()


def landing(received_ref, depth, across, lanes):
    wells, width = received_ref.shape
    pieces = thirds(received_ref[...])
    blocks = []
    for group, size, shift in ((1, PAD, across - PAD), (0, across, 0), (2, PAD, 0)):
        start, rows = group * GROUP, depth * size
        cell = received_ref[:, start + depth : start + depth + 1].astype(jnp.int32)
        spread = jnp.where(
            iota((width, rows), 0) == start + iota((width, rows), 1) // size, 1.0, 0.0
        ).astype(BF16)
        at_x = iota((wells, rows), 1) % size + shift == cell // lanes
        at_y = jnp.where(iota((wells, lanes), 1) == cell % lanes, 1.0, 0.0).astype(BF16)
        landed = jnp.zeros((rows, lanes), F32)
        for piece in reversed(pieces):
            wide = jnp.where(at_x, dot(piece, spread, ((1,), (0,))), 0.0).astype(BF16)
            landed = landed + dot(wide, at_y, ((0,), (0,)))
        blocks.append(landed.reshape(depth, size, lanes))
    return jnp.concatenate(blocks, axis=1).reshape(-1, lanes)


def flat(ref, index):
    return ref[index].reshape(-1, ref.shape[3])


def put_faces(adjoint, step, courant_ref, sign_ref, faces):
    rows, lanes = adjoint.shape
    wide = courant_ref.shape[2]
    ye_ref, yo_ref, z_ref = faces
    sign = flat(sign_ref, step)
    lane = iota((rows, lanes), 1)
    raised = (sign & 2) != 0
    ends = jnp.transpose(jnp.where(raised == (lane == 0), flat(courant_ref, 1) * adjoint, 0.0))
    low, high = ends[0:1, :], ends[lanes - 1 : lanes, :]
    even = (lax.axis_index("gy") % 2) == 0
    ye_ref[...] = jnp.where(even, high, low)
    yo_ref[...] = jnp.where(even, low, high)
    last = courant_ref.shape[1] - 1
    low = jnp.where((sign[:wide] & 4) != 0, courant_ref[2, 0] * adjoint[:wide], 0.0)
    high = jnp.where((sign[rows - wide :] & 4) != 0, 0.0, courant_ref[2, last] * adjoint[rows - wide :])
    z_ref[...] = jnp.where(lax.axis_index("gz") == 0, high, low)


def inside_of(values, wide):
    rows, lanes = values.shape
    values = values.reshape(rows // wide, wide, lanes)
    return values[:, PAD : wide - PAD].reshape(-1, lanes)


def inner_kernel(step, tracer_step, adjoint_ref, courant_ref, sign_ref, *rest):
    gradient_in, tracer_ref, gradient_ref = None, None, None
    if tracer_step is not None:
        tracer_ref, *rest = rest
        if len(rest) == 3:
            gradient_in, *rest = rest
        gradient_ref, *rest = rest
    (kept_ref,) = rest
    adjoint = adjoint_ref[...]
    rows, lanes = adjoint.shape
    wide = courant_ref.shape[2]
    sign = flat(sign_ref, step)
    speed = [flat(courant_ref, axis) for axis in range(3)]
    row_x = iota((rows, lanes), 0) % wide
    lane = iota((rows, lanes), 1)
    flow = [speed[axis] * adjoint for axis in range(3)]
    rising = [jnp.where((sign & (1 << axis)) != 0, flow[axis], 0.0) for axis in range(3)]
    falling = [flow[axis] - rising[axis] for axis in range(3)]
    kept = (1.0 - (speed[0] + speed[1] + speed[2])) * adjoint
    up = jnp.where(row_x == wide - 1, 0.0, pltpu.roll(rising[0], rows - 1, 0))
    down = jnp.where(row_x == 0, 0.0, pltpu.roll(falling[0], 1, 0))
    kept = kept + up + down
    up = jnp.where(lane == lanes - 1, 0.0, pltpu.roll(rising[1], lanes - 1, 1))
    down = jnp.where(lane == 0, 0.0, pltpu.roll(falling[1], 1, 1))
    kept = kept + up + down
    blank = jnp.zeros((wide, lanes), F32)
    kept_ref[...] = (
        kept
        + jnp.concatenate([rising[2][wide:, :], blank], axis=0)
        + jnp.concatenate([blank, falling[2][: rows - wide, :]], axis=0)
    )
    if tracer_step is not None:
        gradient = inside_of(adjoint, wide) * tracer_ref[tracer_step]
        gradient_ref[...] = gradient if gradient_in is None else gradient_in[...] + gradient


def first_kernel(step, received_ref, courant_ref, sign_ref, adjoint_ref, *faces):
    _, depth, wide, lanes = courant_ref.shape
    adjoint = landing(received_ref, depth, wide - 2 * PAD, lanes)
    adjoint_ref[...] = adjoint
    put_faces(adjoint, step, courant_ref, sign_ref, faces)


def join(sizes, kept_ref, ye_ref, yo_ref, z_ref):
    rows, lanes = kept_ref.shape
    wide = z_ref.shape[0]
    gy, gz = lax.axis_index("gy"), lax.axis_index("gz")
    even = (gy % 2) == 0
    ye, yo = ye_ref[...], yo_ref[...]
    above = jnp.where(gy == sizes[1] - 1, 0.0, jnp.where(even, ye, yo))
    below = jnp.where(gy == 0, 0.0, jnp.where(even, yo, ye))
    row_y = iota((lanes, rows), 0)
    adjoint = kept_ref[...] + jnp.transpose(
        jnp.where(row_y == lanes - 1, above, jnp.where(row_y == 0, below, 0.0))
    )
    z = z_ref[...]
    blank = jnp.zeros((rows - wide, lanes), F32)
    return adjoint + jnp.where(
        gz == 0,
        jnp.concatenate([blank, z], axis=0),
        jnp.concatenate([z, blank], axis=0),
    )


def middle_kernel(sizes, step, kept_ref, ye, yo, z, courant_ref, sign_ref, adjoint_ref, *faces):
    adjoint = join(sizes, kept_ref, ye, yo, z)
    adjoint_ref[...] = adjoint
    put_faces(adjoint, step, courant_ref, sign_ref, faces)


def last_kernel(
    sizes, length, depth, kept_ref, ye, yo, z, tracer_ref, gradient_in, adjoint_hbm, out_ref, work_ref, lines_ref, sem
):
    rows, lanes = work_ref.shape
    across = rows // depth
    adjoint = inside_of(join(sizes, kept_ref, ye, yo, z), z.shape[0])
    work_ref[...] = adjoint
    copy = pltpu.make_async_copy(work_ref, adjoint_hbm, sem)
    copy.start()
    lines_ref[...] = gradient_in[...] + adjoint * tracer_ref[0]
    lines = jnp.concatenate(
        [lines_ref[pl.ds(x, depth, stride=across), :] for x in range(across)], axis=0
    )
    rows_each = lanes // depth
    places = lanes // (sizes[1] * rows_each)
    group = sizes[1] * (places + 1)
    order = iota((rows_each * group, lanes), 0)
    r, j, e = order // group, order % group // (places + 1), order % (places + 1)
    y_out = y_of(sizes, lanes, rows_each, e, j, r)
    y_out = jnp.where(e < places, y_out, jnp.where(r == 0, lanes - 1, 0))
    table = jnp.exp(-jnp.abs(y_out - iota(order.shape, 1)).astype(F32) / length) * (1.0 / math.sqrt(length))
    result = dot3(table, lines, ((1,), (1,)))
    quarter = iota((group, lanes), 1) // depth
    for tile in range(rows // lanes):
        pieces = [result[r * group : (r + 1) * group, tile * lanes : (tile + 1) * lanes] for r in range(rows_each)]
        for u in range(rows_each):
            chunk = jnp.zeros((group, lanes), F32)
            for r in range(rows_each):
                turn = ((r - u) * depth) % lanes
                chunk = jnp.where(quarter == r, pltpu.roll(pieces[r], turn, 1) if turn else pieces[r], chunk)
            out_ref[pl.ds(tile * rows_each + u, group, stride=across), :] = chunk
    copy.wait()


def y_of(sizes, lanes, rows_each, place, gy, r):
    high, low = place // sizes[2], place % sizes[2]
    return high * (sizes[1] * sizes[2] * rows_each) + gy * (sizes[2] * rows_each) + low * rows_each + r


def carry_kernel(sizes, depth, across, length, lines_ref, out_ref):
    lanes = lines_ref.shape[1]
    bricks = sizes[1]
    rows_each = lanes // depth
    places = lanes // (bricks * rows_each)
    block = (places + 1) * across
    lane = iota((across, lanes), 1)

    def spread(values, group):
        values = jnp.where(lane // depth == group, values, 0.0)
        if group:
            values = pltpu.roll(values, lanes - group * depth, 1)
        step = depth
        while step < lanes:
            values = values + pltpu.roll(values, step, 1)
            step = 2 * step
        return values

    carries = [lines_ref[g * block + places * across : (g + 1) * block, :] for g in range(bricks)]
    decay = math.exp(-lanes / length)
    below, above = [None] * bricks, [None] * bricks
    total = jnp.zeros((across, lanes), F32)
    for g in range(bricks):
        below[g] = total
        total = decay * total + spread(carries[g], 0)
    total = jnp.zeros((across, lanes), F32)
    for g in reversed(range(bricks)):
        above[g] = total
        total = decay * total + spread(carries[g], 1)
    first_core = lax.axis_index("gz") == 0
    gy = lax.axis_index("gy")
    for high in range(places // sizes[2]):
        factors = []
        for low in range(sizes[2]):
            y = y_of(sizes, lanes, rows_each, high * sizes[2] + low, gy, iota((1, lanes), 1) // depth)
            y = y.astype(F32)
            factors.append((jnp.exp(-(y + 1.0) / length), jnp.exp(-(lanes - y) / length)))
        for g in range(bricks):
            values = []
            for low in range(sizes[2]):
                start = g * block + (high * sizes[2] + low) * across
                here = lines_ref[start : start + across, :]
                values.append(here + factors[low][0] * below[g] + factors[low][1] * above[g])
            start = (g * (places // sizes[2]) + high) * sizes[2] * across
            out_ref[start : start + across, :] = jnp.where(first_core, values[1], values[0])
            out_ref[start + across : start + 2 * across, :] = jnp.where(first_core, values[0], values[1])


def smooth_own_kernel(across, length, data_ref, own_ref, table_ref):
    full_x = own_ref.shape[1]
    x_in, x_out = iota((full_x, full_x), 0), iota((full_x, full_x), 1)
    table = jnp.exp(-jnp.abs(x_in - x_out).astype(F32) / length) * (1.0 / math.sqrt(length))
    table_ref[...] = table
    own = jnp.concatenate(
        [data_ref[(2 * g + 1) * across : (2 * g + 2) * across, :] for g in range(full_x // across)], axis=0
    )
    own_ref[...] = dot3(own, table, ((0,), (0,)))


def smooth_xz_kernel(depth, length, own_ref, table_ref, other_ref, out_hbm, work_ref, sems):
    rows_each = own_ref.shape[0] // depth
    gz = lax.axis_index("gz")
    own = own_ref[...]
    other = dot3(other_ref[...], table_ref[...], ((0,), (0,)))
    full_z = 2 * depth
    z_out, z_in = iota((full_z, full_z), 0), iota((full_z, full_z), 1)
    z_in = z_in % depth + jnp.where(z_in < depth, gz, 1 - gz) * depth
    table = jnp.exp(-jnp.abs(z_out - z_in).astype(F32) / length) * (1.0 / math.sqrt(length))
    copies = []
    for r in range(rows_each):
        part = slice(r * depth, (r + 1) * depth)
        column = jnp.concatenate([own[part], other[part]], axis=0)
        here = slice(r * full_z, (r + 1) * full_z)
        work_ref[here, :] = dot3(table, column, ((1,), (0,)))
        copy = pltpu.make_async_copy(work_ref.at[here], out_hbm.at[here], sems.at[r])
        copy.start()
        copies.append(copy)
    for copy in copies:
        copy.wait()


def pair_swaps(count):
    even = [(i, i ^ 1) for i in range(count)]
    odd = [(i, (i + 1) % count) for i in range(1, count, 2)]
    odd = odd + [(target, source) for source, target in odd]
    return even, odd


def swap(even, odd, axis):
    pairs = pair_swaps(lax.axis_size(axis))
    return lax.ppermute(even, axis, pairs[0]), lax.ppermute(odd, axis, pairs[1])


def exchange(faces):
    ye, yo, z = faces
    return (*swap(ye, yo, "gy"), lax.ppermute(z, "gz", [(0, 1), (1, 0)]))


def local(kernel, name, inputs, outputs, scratch=(), far=0, far_outputs=()):
    vmem = pl.BlockSpec(memory_space=pltpu.VMEM)
    hbm = pl.BlockSpec(memory_space=pl.ANY)
    near = len(inputs) - far
    out_far = [i in far_outputs for i in range(len(outputs))]
    return pl.pallas_call(
        kernel,
        in_specs=[vmem] * near + [hbm] * far,
        out_specs=[hbm if away else vmem for away in out_far],
        out_shape=[
            (pltpu.HBM if away else pltpu.VMEM)(*(dims if isinstance(dims[0], tuple) else (dims, F32)))
            for dims, away in zip(outputs, out_far)
        ],
        scratch_shapes=scratch,
        compiler_params=pltpu.CompilerParams(vmem_limit_bytes=12 << 20),
        name=name,
    )(
        *[pltpu.with_memory_space_constraint(values, pltpu.VMEM) for values in inputs[:near]],
        *[pltpu.with_memory_space_constraint(values, pltpu.HBM) for values in inputs[near:]],
    )


def per_device(well_sources, well_owner, well_cell, flow_sign, courant, tracer):
    steps, brick_z, brick_x, brick_y = flow_sign.shape
    wells = well_sources.shape[0]
    rows = brick_z * brick_x
    sizes = (lax.axis_size("gx"), lax.axis_size("gy"), lax.axis_size("gz"))
    devices = sizes[0] * sizes[1] * sizes[2]
    owners = sizes[0] * sizes[1]
    axes = ("gx", "gy", "gz")
    trace = tracer.reshape(steps, rows, brick_y)
    ends = (6, brick_z, HALO, 1, brick_y)
    lined = (3, brick_z, brick_x, 1, brick_y)
    outgoing, even, odd = local(
        open_kernel,
        "open",
        [
            well_sources.T,
            well_owner.reshape(1, wells),
            well_cell.reshape(1, wells),
            courant.reshape(lined),
            flow_sign.reshape(lined),
        ],
        [(CAP * owners, 128), ends, ends],
        [
            pltpu.VMEM((brick_z, wells), F32),
            pltpu.VMEM((1, wells), jnp.int32),
            pltpu.VMEM((1, wells), jnp.int32),
            pltpu.VMEM((2, 3, brick_z, HALO, 1, brick_y), jnp.int32),
            pltpu.SemaphoreType.DMA((7,)),
        ],
        far=5,
    )
    even, odd = swap(even, odd, "gx")
    received = lax.all_to_all(
        outgoing.reshape(owners, CAP, 128), ("gx", "gy"), split_axis=0, concat_axis=0, tiled=True
    ).reshape(CAP * owners, 128)
    wide_x = brick_x + 2 * PAD
    stack = (3, brick_z, wide_x, brick_y)
    weights = local(
        functools.partial(load_kernel, sizes[0]),
        "load",
        [
            even.reshape(6, brick_z * HALO, brick_y),
            odd.reshape(6, brick_z * HALO, brick_y),
            courant,
            flow_sign,
        ],
        [stack, (stack, jnp.int32)],
        [pltpu.SemaphoreType.DMA((6,))],
        far=2,
    )

    field = (rows, brick_y)
    wide = (brick_z * wide_x, brick_y)
    face_shapes = [(1, brick_z * wide_x)] * 2 + [(wide_x, brick_y)]
    gradient = []
    adjoint, *faces = local(
        functools.partial(first_kernel, steps - 1),
        "first",
        [received, *weights],
        [wide] + face_shapes,
    )
    for step in reversed(range(steps)):
        arrived = exchange(faces)
        if step == steps - 1:
            inputs, outputs, tracer_step = [], [], None
        else:
            inputs, outputs, tracer_step = [trace] + gradient, [field], step + 1
        *gradient, kept = local(
            functools.partial(inner_kernel, step, tracer_step),
            f"inner{step}",
            [adjoint, *weights] + inputs,
            outputs + [wide],
        )
        if step:
            adjoint, *faces = local(
                functools.partial(middle_kernel, sizes, step - 1),
                f"join{step}",
                [kept, *arrived, *weights],
                [wide] + face_shapes,
            )
    rows_each = sizes[1] * brick_y // devices
    block = (brick_y // (sizes[1] * rows_each) + 1) * brick_x
    length_y = 2.0 * brick_y
    adjoint, lines = local(
        functools.partial(last_kernel, sizes, length_y, brick_z),
        "join0",
        [kept, *arrived, trace, *gradient],
        [field, (sizes[1] * block, brick_y)],
        [pltpu.VMEM(field, F32), pltpu.VMEM(field, F32), pltpu.SemaphoreType.DMA],
        far_outputs=(0,),
    )
    lines = lax.all_to_all(
        lines.reshape(sizes[1], block, brick_y), "gy", split_axis=0, concat_axis=0, tiled=True
    ).reshape(sizes[1] * block, brick_y)
    (planes,) = local(
        functools.partial(carry_kernel, sizes, brick_z, brick_x, length_y), "carry", [lines], [field]
    )
    planes = lax.all_to_all(
        planes.reshape(sizes[0], sizes[2] * brick_x, brick_y), "gx", split_axis=0, concat_axis=0, tiled=True
    )
    full_x, full_z = sizes[0] * brick_x, sizes[2] * brick_z
    other = lax.ppermute(planes[:, :brick_x], "gz", [(0, 1), (1, 0)])
    own, table = local(
        functools.partial(smooth_own_kernel, brick_x, 2.0 * brick_x),
        "smooth_own",
        [planes.reshape(field)],
        [(brick_y, full_x), (full_x, full_x)],
    )
    (smoothed,) = local(
        functools.partial(smooth_xz_kernel, brick_z, 2.0 * brick_z),
        "smooth_xz",
        [own, table, other.reshape(full_x, brick_y)],
        [(rows_each * full_z, full_x)],
        [pltpu.VMEM((rows_each * full_z, full_x), F32), pltpu.SemaphoreType.DMA((rows_each,))],
        far_outputs=(0,),
    )
    return (
        adjoint.reshape(brick_z, brick_x, brick_y),
        smoothed.reshape(rows_each, full_z, full_x),
    )


def solution(mesh):
    return jax.shard_map(
        per_device,
        mesh=mesh,
        in_specs=(
            P(("gx", "gy"), "gz"),
            P(("gx", "gy"), None),
            P(("gx", "gy")),
            P(None, "gz", "gx", "gy"),
            P(None, "gz", "gx", "gy"),
            P(None, "gz", "gx", "gy"),
        ),
        out_specs=(P("gz", "gx", "gy"), P(("gx", "gy", "gz"), None, None)),
        check_vma=False,
    )
```

time: 89.6 us -> 85 us (0.949)
  blocking collectives: 52.1 us -> 23.5 us
  starting transfers between devices: 19.2 us -> 30.7 us
  waiting for transfers between devices: 10.4 us -> 15.2 us
  Pallas kernels: 6.61 us -> 11 us
  local copies, waits for them, and re-layouts: 0.02 us -> 3.36 us
    all_to_all x1 -> x0, blocking collectives: 27.5 us -> none  [per_device(): lax.all_to_all(outgoing.reshape(owners, CAP, 128), ('gx', 'gy'), split_ax...]
    all_to_all x0 -> x1, starting transfers between devices: none -> 11.8 us  [per_device(): lax.all_to_all(outgoing.reshape(owners, CAP, 128), ('gx', 'gy'), split_ax...]
    all_to_all x0 -> x1, waiting for transfers between devices: none -> 6.64 us  [per_device(): lax.all_to_all(outgoing.reshape(owners, CAP, 128), ('gx', 'gy'), split_ax...]
    pallas_call x10 -> x12, Pallas kernels: 6.61 us -> 11 us  [local(): pl.pallas_call(kernel, in_specs=[vmem] * near + [hbm] * far, out_specs=[h...]
    unnamed x6 -> x10, local copies, waits for them, and re-layouts: 0.01 us -> 3.35 us
    ppermute x15 -> x11, waiting for transfers between devices: 9.39 us -> 7.88 us  [the longest x4 4.22 us: swap(): lax.ppermute(odd, axis, pairs[1])]
    ppermute x15 -> x11, starting transfers between devices: 14.2 us -> 13.9 us  [the longest x3 5.83 us: exchange(): return (*swap(ye, yo, 'gy'), lax.ppermute(z, 'gz', [(0, 1), (1, 0)]))]
  transfers between devices with their start and end apart: 16 -> 13, of which waited for: 7 -> 8; matrix products, arithmetic and copies ran while one was open for 0% -> 0% of each run, Pallas kernels for 1% -> 4%
where the time goes in v4:
time: 85 us; the launch traced here: 84.7 us
  starting transfers between devices  30.7 us (36%)
  blocking collectives  23.5 us (28%)
  waiting for transfers between devices  15.2 us (18%)
  Pallas kernels  11 us (13%)
  local copies, waits for them, and re-layouts  3.36 us (4%)
  between operations  0.92 us (1%)
    all_to_all x1, blocking collectives, per_device(): lax.all_to_all(lines.reshape(sizes[1], block, brick_y), 'gy', split_axis=...  13.2 us
    all_to_all x1, starting transfers between devices, per_device(): lax.all_to_all(outgoing.reshape(owners, CAP, 128), ('gx', 'gy'), split_ax...  11.8 us
    pallas_call x12, Pallas kernels, local(): pl.pallas_call(kernel, in_specs=[vmem] * near + [hbm] * far, out_specs=[h...  11 us
    all_to_all x1, blocking collectives, per_device(): lax.all_to_all(planes.reshape(sizes[0], sizes[2] * brick_x, brick_y), 'gx...  10.3 us
    all_to_all x1, waiting for transfers between devices, per_device(): lax.all_to_all(outgoing.reshape(owners, CAP, 128), ('gx', 'gy'), split_ax...  6.64 us
    ppermute x3, starting transfers between devices, exchange(): return (*swap(ye, yo, 'gy'), lax.ppermute(z, 'gz', [(0, 1), (1, 0)]))  5.83 us
    ppermute x4, starting transfers between devices, swap(): lax.ppermute(odd, axis, pairs[1])  5.31 us
    ppermute x1, starting transfers between devices, per_device(): other = lax.ppermute(planes[:, :brick_x], 'gz', [(0, 1), (1, 0)])  4.98 us
  transfers between devices with their start and end apart: 13, of which 8 were waited for; matrix products, arithmetic and copies ran while one was open for 0% of the time, Pallas kernels for 4%

profile of v4, /device:TPU:1, one launch (start us, length us, event | category | flops | bytes accessed | tf_op | source)
XLA Modules:
  0.0 84.7 jit_solution(6849520037467435495)
XLA Ops:
  0.6 2.2 %open.1 = (f32[256,128]{1,0:T(8,128)}, f32[6,32,3,1,128]{4,3,2,1,0:T(1,128)S(1)}, f32[6,32,3,1,128]{4,3,2,1,0:T(1,128)S(1)}) custom-call(f32[32,96]{1,0:T(8,128)} %bitcast.31, s32[1,96]{1,0:T(1,128)} %bitcast.32, s32[1,96]{1,0:T(1,128)} %bitcast.33, f32[3,32,16,1,128]{4,3,2,1,0:T(1,128)} %bitcast.28, s32[3,32,16,1,128]{4,3,2,1,0:T(1,128)} %bitcast.29), custom_call_target="tpu_custom_call" | custom-call | tf_op jit(solution)/shard_map/open/pallas_call | solution.py:406
  2.8 2.2 %collective-permute-start = (f32[6,32,3,1,128]{4,3,2,1,0:T(1,128)S(1)}, f32[6,32,3,1,128]{4,3,2,1,0:T(1,128)S(1)}, u32[]{:S(2)}, u32[]{:S(2)}) collective-permute-start(f32[6,32,3,1,128]{4,3,2,1,0:T(1,128)S(1)} %get-tuple-element.28), channel_id=1, source_target_pairs={{0,16},{16,0},{32,48},{48,32},{64,80},{80,64},{96,112},{112,96},{1... | collective-permute-start | bytes 884744 | tf_op jit(solution)/shard_map/ppermute | solution.py:393
  5.0 4.1 %collective-permute-start.1 = (f32[6,32,3,1,128]{4,3,2,1,0:T(1,128)S(1)}, f32[6,32,3,1,128]{4,3,2,1,0:T(1,128)S(1)}, u32[]{:S(2)}, u32[]{:S(2)}) collective-permute-start(f32[6,32,3,1,128]{4,3,2,1,0:T(1,128)S(1)} %get-tuple-element.29), channel_id=1, source_target_pairs={{16,32},{48,64},{80,96},{112,128},{144,160},{176,192},{208,224},{2... | collective-permute-start | bytes 884744 | tf_op jit(solution)/shard_map/ppermute | solution.py:393
  9.1 11.8 %all-to-all-start = ((f32[128,2,128]{2,1,0:T(2,128)}), f32[128,2,128]{2,1,0:T(2,128)S(1)}, u32[]{:S(2)}, u32[]{:S(2)}) async-start(f32[128,2,128]{2,1,0:T(2,128)} %bitcast.5), calls=%async_computation | async-start | bytes 262144 | tf_op jit(solution)/shard_map/all_to_all | solution.py:455
  20.9 0.0 collective-permute-done
  21.0 0.0 copy-start.1
  21.0 0.7 copy-done.1
  21.7 0.0 collective-permute-done.1
  21.7 0.0 copy-start.3
  21.7 0.7 copy-done.3
  22.4 0.0 copy-start.2
  22.4 1.0 %copy-done.2 = f32[6,32,3,1,128]{4,3,2,1,0:T(1,128)S(1)} copy-done((f32[6,32,3,1,128]{4,3,2,1,0:T(1,128)S(1)}, f32[6,32,3,1,128]{4,3,2,1,0:T(1,128)}, u32[]{:S(2)}) %copy-start.2) | copy-done | bytes 294936
  23.4 0.0 copy-start.4
  23.4 1.0 %copy-done.4 = f32[6,32,3,1,128]{4,3,2,1,0:T(1,128)S(1)} copy-done((f32[6,32,3,1,128]{4,3,2,1,0:T(1,128)S(1)}, f32[6,32,3,1,128]{4,3,2,1,0:T(1,128)}, u32[]{:S(2)}) %copy-start.4) | copy-done | bytes 294936
  24.3 1.4 %load.1 = (f32[3,32,32,128]{3,2,1,0:T(8,128)S(1)}, s32[3,32,32,128]{3,2,1,0:T(8,128)S(1)}) custom-call(f32[6,96,128]{2,1,0:T(8,128)S(1)} %bitcast.25, f32[6,96,128]{2,1,0:T(8,128)S(1)} %bitcast.26, f32[3,32,16,128]{3,2,1,0:T(8,128)} %courant_hbm.1, s32[3,32,16,128]{3,2,1,0:T(8,128)} %sign_hbm.1), custom_call_target="tpu_custom_call" | custom-call | tf_op jit(solution)/shard_map/load/pallas_call | solution.py:406
  25.7 6.6 %all-to-all-done = f32[128,2,128]{2,1,0:T(2,128)S(1)} async-done(((f32[128,2,128]{2,1,0:T(2,128)}), f32[128,2,128]{2,1,0:T(2,128)S(1)}, u32[]{:S(2)}, u32[]{:S(2)}) %all-to-all-start) | async-done | bytes 131104 | tf_op jit(solution)/shard_map/all_to_all | solution.py:455
  32.4 1.9 %first.1 = (f32[1024,128]{1,0:T(8,128)S(1)}, f32[1,1024]{1,0:T(1,128)S(1)}, f32[1,1024]{1,0:T(1,128)S(1)}, f32[32,128]{1,0:T(8,128)S(1)}) custom-call(f32[256,128]{1,0:T(8,128)S(1)} %bitcast.23, f32[3,32,32,128]{3,2,1,0:T(8,128)S(1)} %get-tuple-element.30.courant_ref, s32[3,32,32,128]{3,2,1,0:T(8,128)S(1)} %get-tuple-element.31.sign_ref), custom_call_target="tpu_custom_call" | custom-call | tf_op jit(solution)/shard_map/first/pallas_call | solution.py:406
  34.3 2.5 %collective-permute-start.4 = (f32[32,128]{1,0:T(8,128)S(1)}, f32[32,128]{1,0:T(8,128)S(1)}, u32[]{:S(2)}, u32[]{:S(2)}) collective-permute-start(f32[32,128]{1,0:T(8,128)S(1)} %get-tuple-element.35), channel_id=1, source_target_pairs={{0,1},{1,0},{2,3},{3,2},{4,5},{5,4},{6,7},{7,6},{8,9},{9,8},{10,11... | collective-permute-start | bytes 49160 | tf_op jit(solution)/shard_map/ppermute | solution.py:398
  36.7 0.3 collective-permute-start.2
  37.0 0.4 collective-permute-start.3
  37.4 0.6 inner2.1.kept_ref
  38.0 0.0 copy-start
  38.1 1.1 %collective-permute-done.2.ye = f32[1,1024]{1,0:T(1,128)S(1)} collective-permute-done((f32[1,1024]{1,0:T(1,128)S(1)}, f32[1,1024]{1,0:T(1,128)S(1)}, u32[]{:S(2)}, u32[]{:S(2)}) %collective-permute-start.2) | collective-permute-done | bytes 4128 | tf_op jit(solution)/shard_map/ppermute | solution.py:393
  39.2 1.5 %collective-permute-done.3.yo = f32[1,1024]{1,0:T(1,128)S(1)} collective-permute-done((f32[1,1024]{1,0:T(1,128)S(1)}, f32[1,1024]{1,0:T(1,128)S(1)}, u32[]{:S(2)}, u32[]{:S(2)}) %collective-permute-start.3) | collective-permute-done | bytes 4128 | tf_op jit(solution)/shard_map/ppermute | solution.py:393
  40.7 0.0 collective-permute-done.4.z
  40.7 0.4 join2.1
  41.1 1.6 %collective-permute-start.7 = (f32[32,128]{1,0:T(8,128)S(1)}, f32[32,128]{1,0:T(8,128)S(1)}, u32[]{:S(2)}, u32[]{:S(2)}) collective-permute-start(f32[32,128]{1,0:T(8,128)S(1)} %get-tuple-element.40), channel_id=1, source_target_pairs={{0,1},{1,0},{2,3},{3,2},{4,5},{5,4},{6,7},{7,6},{8,9},{9,8},{10,11... | collective-permute-start | bytes 49160 | tf_op jit(solution)/shard_map/ppermute | solution.py:398
  42.7 0.0 collective-permute-start.5
  42.7 0.4 collective-permute-start.6
  43.1 0.0 copy-done
  43.2 0.7 inner1.1
  43.8 1.4 %collective-permute-done.5.ye = f32[1,1024]{1,0:T(1,128)S(1)} collective-permute-done((f32[1,1024]{1,0:T(1,128)S(1)}, f32[1,1024]{1,0:T(1,128)S(1)}, u32[]{:S(2)}, u32[]{:S(2)}) %collective-permute-start.5) | collective-permute-done | bytes 4128 | tf_op jit(solution)/shard_map/ppermute | solution.py:393
  45.2 1.2 %collective-permute-done.6.yo = f32[1,1024]{1,0:T(1,128)S(1)} collective-permute-done((f32[1,1024]{1,0:T(1,128)S(1)}, f32[1,1024]{1,0:T(1,128)S(1)}, u32[]{:S(2)}, u32[]{:S(2)}) %collective-permute-start.6) | collective-permute-done | bytes 4128 | tf_op jit(solution)/shard_map/ppermute | solution.py:393
  46.4 0.0 collective-permute-done.7.z
  46.4 0.4 join1.1
  46.8 1.8 %collective-permute-start.10 = (f32[32,128]{1,0:T(8,128)S(1)}, f32[32,128]{1,0:T(8,128)S(1)}, u32[]{:S(2)}, u32[]{:S(2)}) collective-permute-start(f32[32,128]{1,0:T(8,128)S(1)} %get-tuple-element.46), channel_id=1, source_target_pairs={{0,1},{1,0},{2,3},{3,2},{4,5},{5,4},{6,7},{7,6},{8,9},{9,8},{10,11... | collective-permute-start | bytes 49160 | tf_op jit(solution)/shard_map/ppermute | solution.py:398
  48.6 0.3 collective-permute-start.8
  48.9 0.4 collective-permute-start.9
  49.3 0.6 inner0.1
  49.9 1.1 %collective-permute-done.8.ye = f32[1,1024]{1,0:T(1,128)S(1)} collective-permute-done((f32[1,1024]{1,0:T(1,128)S(1)}, f32[1,1024]{1,0:T(1,128)S(1)}, u32[]{:S(2)}, u32[]{:S(2)}) %collective-permute-start.8) | collective-permute-done | bytes 4128 | tf_op jit(solution)/shard_map/ppermute | solution.py:393
  51.0 1.5 %collective-permute-done.9.yo = f32[1,1024]{1,0:T(1,128)S(1)} collective-permute-done((f32[1,1024]{1,0:T(1,128)S(1)}, f32[1,1024]{1,0:T(1,128)S(1)}, u32[]{:S(2)}, u32[]{:S(2)}) %collective-permute-start.9) | collective-permute-done | bytes 4128 | tf_op jit(solution)/shard_map/ppermute | solution.py:393
  52.6 0.0 collective-permute-done.10.z
  52.6 1.0 %join0.1 = (f32[512,128]{1,0:T(8,128)}, f32[640,128]{1,0:T(8,128)S(1)}) custom-call(f32[1024,128]{1,0:T(8,128)S(1)} %get-tuple-element.43.kept_ref, f32[1,1024]{1,0:T(1,128)S(1)} %collective-permute-done.8.ye, f32[1,1024]{1,0:T(1,128)S(1)} %collective-permute-done.9.yo, f32[32,128]{1,0:T(8,128)S(1)} %collective-permute-done.10.z, ...), custom_call_target="tpu_custom_call" | custom-call | tf_op jit(solution)/shard_map/join0/pallas_call | solution.py:406
  53.6 13.2 %all_to_all.15 = f32[8,80,128]{2,1,0:T(8,128)S(1)} all-to-all(f32[8,80,128]{2,1,0:T(8,128)S(1)} %bitcast.24), channel_id=1, replica_groups=mesh['gx'=16,'gy'=8,'gz'=2] {'gy'}, dimensions={0} | all-to-all | bytes 655360 | tf_op jit(solution)/shard_map/all_to_all | solution.py:514
  66.7 0.2 carry.1
  67.0 10.3 %all_to_all.16 = f32[16,32,128]{2,1,0:T(8,128)S(1)} all-to-all(f32[16,32,128]{2,1,0:T(8,128)S(1)} %bitcast.22), channel_id=1, replica_groups=mesh['gx'=16,'gy'=8,'gz'=2] {'gx'}, dimensions={0} | all-to-all | bytes 524288 | tf_op jit(solution)/shard_map/all_to_all | solution.py:520
  77.3 5.0 %collective-permute-start.11 = (f32[16,16,128]{2,1,0:T(8,128)S(1)}, f32[16,16,128]{2,1,0:T(8,128)S(1)}, u32[]{:S(2)}, u32[]{:S(2)}) collective-permute-start(f32[16,16,128]{2,1,0:T(8,128)S(1)} %slice.4), channel_id=1, source_target_pairs={{0,1},{1,0},{2,3},{3,2},{4,5},{5,4},{6,7},{7,6},{8,9},{9,8},{10,11... | collective-permute-start | bytes 393224 | tf_op jit(solution)/shard_map/ppermute | solution.py:524
  82.3 0.3 smooth_own.1
  82.6 0.7 collective-permute-done.11
  83.3 1.2 %smooth_xz.1 = f32[256,256]{1,0:T(8,128)} custom-call(f32[128,256]{1,0:T(8,128)S(1)} %get-tuple-element.50.own_ref, f32[256,256]{1,0:T(8,128)S(1)} %get-tuple-element.51.table_ref, f32[256,128]{1,0:T(8,128)S(1)} %bitcast.27), custom_call_target="tpu_custom_call" | custom-call | tf_op jit(solution)/shard_map/smooth_xz/pallas_call | solution.py:406
  (1 shorter events, 0.0 us)
Async XLA Ops:
  2.8 18.1 %collective-permute-start = (f32[6,32,3,1,128]{4,3,2,1,0:T(1,128)S(1)}, f32[6,32,3,1,128]{4,3,2,1,0:T(1,128)S(1)}, u32[]{:S(2)}, u32[]{:S(2)}) collective-permute-start(f32[6,32,3,1,128]{4,3,2,1,0:T(1,128)S(1)} %get-tuple-element.28), channel_id=1, source_target_pairs={{0,16},{16,0},{32,48},{48,32},{64,80},{80,64},{96,112},{112,96},{1... | collective-permute-start | bytes 884744 | tf_op jit(solution)/shard_map/ppermute | solution.py:393
  5.0 16.6 %collective-permute-start.1 = (f32[6,32,3,1,128]{4,3,2,1,0:T(1,128)S(1)}, f32[6,32,3,1,128]{4,3,2,1,0:T(1,128)S(1)}, u32[]{:S(2)}, u32[]{:S(2)}) collective-permute-start(f32[6,32,3,1,128]{4,3,2,1,0:T(1,128)S(1)} %get-tuple-element.29), channel_id=1, source_target_pairs={{16,32},{48,64},{80,96},{112,128},{144,160},{176,192},{208,224},{2... | collective-permute-start | bytes 884744 | tf_op jit(solution)/shard_map/ppermute | solution.py:393
  9.1 23.2 %all-to-all-start = ((f32[128,2,128]{2,1,0:T(2,128)}), f32[128,2,128]{2,1,0:T(2,128)S(1)}, u32[]{:S(2)}, u32[]{:S(2)}) async-start(f32[128,2,128]{2,1,0:T(2,128)} %bitcast.5), calls=%async_computation | async-start | bytes 262144 | tf_op jit(solution)/shard_map/all_to_all | solution.py:455
  21.0 0.7 copy-start.1
  21.7 0.7 copy-start.3
  22.4 1.0 %copy-start.2 = (f32[6,32,3,1,128]{4,3,2,1,0:T(1,128)S(1)}, f32[6,32,3,1,128]{4,3,2,1,0:T(1,128)}, u32[]{:S(2)}) copy-start(f32[6,32,3,1,128]{4,3,2,1,0:T(1,128)} %copy-done.1) | copy-start | bytes 884740
  23.4 1.0 %copy-start.4 = (f32[6,32,3,1,128]{4,3,2,1,0:T(1,128)S(1)}, f32[6,32,3,1,128]{4,3,2,1,0:T(1,128)}, u32[]{:S(2)}) copy-start(f32[6,32,3,1,128]{4,3,2,1,0:T(1,128)} %copy-done.3) | copy-start | bytes 884740
  34.3 6.4 %collective-permute-start.4 = (f32[32,128]{1,0:T(8,128)S(1)}, f32[32,128]{1,0:T(8,128)S(1)}, u32[]{:S(2)}, u32[]{:S(2)}) collective-permute-start(f32[32,128]{1,0:T(8,128)S(1)} %get-tuple-element.35), channel_id=1, source_target_pairs={{0,1},{1,0},{2,3},{3,2},{4,5},{5,4},{6,7},{7,6},{8,9},{9,8},{10,11... | collective-permute-start | bytes 49160 | tf_op jit(solution)/shard_map/ppermute | solution.py:398
  36.7 2.5 %collective-permute-start.2 = (f32[1,1024]{1,0:T(1,128)S(1)}, f32[1,1024]{1,0:T(1,128)S(1)}, u32[]{:S(2)}, u32[]{:S(2)}) collective-permute-start(f32[1,1024]{1,0:T(1,128)S(1)} %get-tuple-element.33), channel_id=1, source_target_pairs={{0,2},{2,0},{4,6},{6,4},{8,10},{10,8},{12,14},{14,12},{1,3},{3,1},... | collective-permute-start | bytes 12296 | tf_op jit(solution)/shard_map/ppermute | solution.py:393
  37.0 3.7 %collective-permute-start.3 = (f32[1,1024]{1,0:T(1,128)S(1)}, f32[1,1024]{1,0:T(1,128)S(1)}, u32[]{:S(2)}, u32[]{:S(2)}) collective-permute-start(f32[1,1024]{1,0:T(1,128)S(1)} %get-tuple-element.34), channel_id=1, source_target_pairs={{2,4},{6,8},{10,12},{14,0},{4,2},{8,6},{12,10},{0,14},{3,5},{7,9},... | collective-permute-start | bytes 12296 | tf_op jit(solution)/shard_map/ppermute | solution.py:393
  38.0 5.1 %copy-start = (f32[3,32,16,128]{3,2,1,0:T(8,128)S(1)}, f32[3,32,16,128]{3,2,1,0:T(8,128)}, u32[]{:S(2)}) copy-start(f32[3,32,16,128]{3,2,1,0:T(8,128)} %param.11) | copy-start | bytes 2359300
  41.1 5.3 %collective-permute-start.7 = (f32[32,128]{1,0:T(8,128)S(1)}, f32[32,128]{1,0:T(8,128)S(1)}, u32[]{:S(2)}, u32[]{:S(2)}) collective-permute-start(f32[32,128]{1,0:T(8,128)S(1)} %get-tuple-element.40), channel_id=1, source_target_pairs={{0,1},{1,0},{2,3},{3,2},{4,5},{5,4},{6,7},{7,6},{8,9},{9,8},{10,11... | collective-permute-start | bytes 49160 | tf_op jit(solution)/shard_map/ppermute | solution.py:398
  42.7 2.5 %collective-permute-start.5 = (f32[1,1024]{1,0:T(1,128)S(1)}, f32[1,1024]{1,0:T(1,128)S(1)}, u32[]{:S(2)}, u32[]{:S(2)}) collective-permute-start(f32[1,1024]{1,0:T(1,128)S(1)} %get-tuple-element.38), channel_id=1, source_target_pairs={{0,2},{2,0},{4,6},{6,4},{8,10},{10,8},{12,14},{14,12},{1,3},{3,1},... | collective-permute-start | bytes 12296 | tf_op jit(solution)/shard_map/ppermute | solution.py:393
  42.7 3.7 %collective-permute-start.6 = (f32[1,1024]{1,0:T(1,128)S(1)}, f32[1,1024]{1,0:T(1,128)S(1)}, u32[]{:S(2)}, u32[]{:S(2)}) collective-permute-start(f32[1,1024]{1,0:T(1,128)S(1)} %get-tuple-element.39), channel_id=1, source_target_pairs={{2,4},{6,8},{10,12},{14,0},{4,2},{8,6},{12,10},{0,14},{3,5},{7,9},... | collective-permute-start | bytes 12296 | tf_op jit(solution)/shard_map/ppermute | solution.py:393
  46.8 5.7 %collective-permute-start.10 = (f32[32,128]{1,0:T(8,128)S(1)}, f32[32,128]{1,0:T(8,128)S(1)}, u32[]{:S(2)}, u32[]{:S(2)}) collective-permute-start(f32[32,128]{1,0:T(8,128)S(1)} %get-tuple-element.46), channel_id=1, source_target_pairs={{0,1},{1,0},{2,3},{3,2},{4,5},{5,4},{6,7},{7,6},{8,9},{9,8},{10,11... | collective-permute-start | bytes 49160 | tf_op jit(solution)/shard_map/ppermute | solution.py:398
  48.6 2.5 %collective-permute-start.8 = (f32[1,1024]{1,0:T(1,128)S(1)}, f32[1,1024]{1,0:T(1,128)S(1)}, u32[]{:S(2)}, u32[]{:S(2)}) collective-permute-start(f32[1,1024]{1,0:T(1,128)S(1)} %get-tuple-element.44), channel_id=1, source_target_pairs={{0,2},{2,0},{4,6},{6,4},{8,10},{10,8},{12,14},{14,12},{1,3},{3,1},... | collective-permute-start | bytes 12296 | tf_op jit(solution)/shard_map/ppermute | solution.py:393
  48.9 3.7 %collective-permute-start.9 = (f32[1,1024]{1,0:T(1,128)S(1)}, f32[1,1024]{1,0:T(1,128)S(1)}, u32[]{:S(2)}, u32[]{:S(2)}) collective-permute-start(f32[1,1024]{1,0:T(1,128)S(1)} %get-tuple-element.45), channel_id=1, source_target_pairs={{2,4},{6,8},{10,12},{14,0},{4,2},{8,6},{12,10},{0,14},{3,5},{7,9},... | collective-permute-start | bytes 12296 | tf_op jit(solution)/shard_map/ppermute | solution.py:393
  77.3 6.0 %collective-permute-start.11 = (f32[16,16,128]{2,1,0:T(8,128)S(1)}, f32[16,16,128]{2,1,0:T(8,128)S(1)}, u32[]{:S(2)}, u32[]{:S(2)}) collective-permute-start(f32[16,16,128]{2,1,0:T(8,128)S(1)} %slice.4), channel_id=1, source_target_pairs={{0,1},{1,0},{2,3},{3,2},{4,5},{5,4},{6,7},{7,6},{8,9},{9,8},{10,11... | collective-permute-start | bytes 393224 | tf_op jit(solution)/shard_map/ppermute | solution.py:524

commit v5 on v4

--- a/solution.py
+++ b/solution.py
@@ -84,25 +84,30 @@
     cell = cell_ref[...]
     x = cell // brick_y
     far = float(-4 * chunks)
+    spare = lanes - wells
     target = CAP * owner_row + rank
     targets = [
         target,
         jnp.where(x >= high, target + CAP * gy_count, far),
         jnp.where(x < HALO, target - CAP * gy_count, far),
     ]
-    row = iota((chunks, wells), 0).astype(F32)
-    chosen = jnp.concatenate([jnp.where(row == t, 1.0, 0.0) for t in targets], axis=1).astype(BF16)
+    blank = jnp.full((1, spare), far, F32)
+    row = iota((chunks, lanes), 0).astype(F32)
+    chosen = jnp.concatenate(
+        [jnp.where(row == jnp.concatenate([t, blank], axis=1), 1.0, 0.0).astype(BF16) for t in targets], axis=1
+    )
     column = jnp.concatenate(
         [sources_ref[...], jnp.broadcast_to(cell.astype(F32), (GROUP - depth, wells))], axis=0
     )
-    payload = []
-    for group in range(3):
-        parts = [jnp.zeros((group * GROUP, wells), F32)] if group else []
-        parts = parts + [column, jnp.zeros((lanes - (group + 1) * GROUP, wells), F32)]
-        payload.append(jnp.concatenate(parts, axis=0))
+    column = jnp.concatenate([column, jnp.zeros((GROUP, spare), F32)], axis=1)
     total = jnp.zeros((chunks, lanes), F32)
-    for piece in thirds(jnp.concatenate(payload, axis=1)):
-        total = total + dot(chosen, piece, ((1,), (1,)))
+    for piece in thirds(column):
+        payload = []
+        for group in range(3):
+            parts = [jnp.zeros((group * GROUP, lanes), F32)] if group else []
+            parts = parts + [piece.astype(F32), jnp.zeros((lanes - (group + 1) * GROUP, lanes), F32)]
+            payload.append(jnp.concatenate(parts, axis=0).astype(BF16))
+        total = total + dot(chosen, jnp.concatenate(payload, axis=1), ((1,), (1,)))
     out_ref[...] = total
     copies[3].wait()
     even_ref[3:6] = bits_ref[0].astype(F32)
@@ -145,7 +150,7 @@
 
 def landing(received_ref, depth, across, lanes):
     wells, width = received_ref.shape
-    pieces = thirds(received_ref[...])
+    pieces = halves(received_ref[...])
     blocks = []
     for group, size, shift in ((1, PAD, across - PAD), (0, across, 0), (2, PAD, 0)):
         start, rows = group * GROUP, depth * size

time: 85 us -> 84.1 us (0.989)
  no operation moved by 1% of the time
where the time goes in v5:
time: 84.1 us; the launch traced here: 83.8 us
  starting transfers between devices  30.6 us (36%)
  blocking collectives  23.5 us (28%)
  waiting for transfers between devices  15.2 us (18%)
  Pallas kernels  10.3 us (12%)
  local copies, waits for them, and re-layouts  3.36 us (4%)
  between operations  0.92 us (1%)
    all_to_all x1, blocking collectives, per_device(): lax.all_to_all(lines.reshape(sizes[1], block, brick_y), 'gy', split_axis=...  13.2 us
    all_to_all x1, starting transfers between devices, per_device(): lax.all_to_all(outgoing.reshape(owners, CAP, 128), ('gx', 'gy'), split_ax...  11.8 us
    all_to_all x1, blocking collectives, per_device(): lax.all_to_all(planes.reshape(sizes[0], sizes[2] * brick_x, brick_y), 'gx...  10.4 us
    pallas_call x12, Pallas kernels, local(): pl.pallas_call(kernel, in_specs=[vmem] * near + [hbm] * far, out_specs=[h...  10.3 us
    all_to_all x1, waiting for transfers between devices, per_device(): lax.all_to_all(outgoing.reshape(owners, CAP, 128), ('gx', 'gy'), split_ax...  6.64 us
    ppermute x3, starting transfers between devices, exchange(): return (*swap(ye, yo, 'gy'), lax.ppermute(z, 'gz', [(0, 1), (1, 0)]))  5.68 us
    ppermute x4, starting transfers between devices, swap(): lax.ppermute(odd, axis, pairs[1])  5.34 us
    ppermute x1, starting transfers between devices, per_device(): other = lax.ppermute(planes[:, :brick_x], 'gz', [(0, 1), (1, 0)])  4.98 us
  transfers between devices with their start and end apart: 13, of which 8 were waited for; matrix products, arithmetic and copies ran while one was open for 0% of the time, Pallas kernels for 4%

profile of v5, /device:TPU:1, one launch (start us, length us, event | category | flops | bytes accessed | tf_op | source)
XLA Modules:
  0.0 83.8 jit_solution(8715003785278354381)
XLA Ops:
  0.6 2.1 %open.1 = (f32[256,128]{1,0:T(8,128)}, f32[6,32,3,1,128]{4,3,2,1,0:T(1,128)S(1)}, f32[6,32,3,1,128]{4,3,2,1,0:T(1,128)S(1)}) custom-call(f32[32,96]{1,0:T(8,128)} %bitcast.31, s32[1,96]{1,0:T(1,128)} %bitcast.32, s32[1,96]{1,0:T(1,128)} %bitcast.33, f32[3,32,16,1,128]{4,3,2,1,0:T(1,128)} %bitcast.28, s32[3,32,16,1,128]{4,3,2,1,0:T(1,128)} %bitcast.29), custom_call_target="tpu_custom_call" | custom-call | tf_op jit(solution)/shard_map/open/pallas_call | solution.py:411
  2.8 2.2 %collective-permute-start = (f32[6,32,3,1,128]{4,3,2,1,0:T(1,128)S(1)}, f32[6,32,3,1,128]{4,3,2,1,0:T(1,128)S(1)}, u32[]{:S(2)}, u32[]{:S(2)}) collective-permute-start(f32[6,32,3,1,128]{4,3,2,1,0:T(1,128)S(1)} %get-tuple-element.28), channel_id=1, source_target_pairs={{0,16},{16,0},{32,48},{48,32},{64,80},{80,64},{96,112},{112,96},{1... | collective-permute-start | bytes 884744 | tf_op jit(solution)/shard_map/ppermute | solution.py:398
  5.0 4.1 %collective-permute-start.1 = (f32[6,32,3,1,128]{4,3,2,1,0:T(1,128)S(1)}, f32[6,32,3,1,128]{4,3,2,1,0:T(1,128)S(1)}, u32[]{:S(2)}, u32[]{:S(2)}) collective-permute-start(f32[6,32,3,1,128]{4,3,2,1,0:T(1,128)S(1)} %get-tuple-element.29), channel_id=1, source_target_pairs={{16,32},{48,64},{80,96},{112,128},{144,160},{176,192},{208,224},{2... | collective-permute-start | bytes 884744 | tf_op jit(solution)/shard_map/ppermute | solution.py:398
  9.1 11.8 %all-to-all-start = ((f32[128,2,128]{2,1,0:T(2,128)}), f32[128,2,128]{2,1,0:T(2,128)S(1)}, u32[]{:S(2)}, u32[]{:S(2)}) async-start(f32[128,2,128]{2,1,0:T(2,128)} %bitcast.5), calls=%async_computation | async-start | bytes 262144 | tf_op jit(solution)/shard_map/all_to_all | solution.py:460
  20.9 0.0 collective-permute-done
  20.9 0.0 copy-start.1
  20.9 0.7 copy-done.1
  21.6 0.0 collective-permute-done.1
  21.6 0.0 copy-start.3
  21.6 0.7 copy-done.3
  22.3 0.0 copy-start.2
  22.3 1.0 %copy-done.2 = f32[6,32,3,1,128]{4,3,2,1,0:T(1,128)S(1)} copy-done((f32[6,32,3,1,128]{4,3,2,1,0:T(1,128)S(1)}, f32[6,32,3,1,128]{4,3,2,1,0:T(1,128)}, u32[]{:S(2)}) %copy-start.2) | copy-done | bytes 294936
  23.3 0.0 copy-start.4
  23.3 1.0 %copy-done.4 = f32[6,32,3,1,128]{4,3,2,1,0:T(1,128)S(1)} copy-done((f32[6,32,3,1,128]{4,3,2,1,0:T(1,128)S(1)}, f32[6,32,3,1,128]{4,3,2,1,0:T(1,128)}, u32[]{:S(2)}) %copy-start.4) | copy-done | bytes 294936
  24.2 1.4 %load.1 = (f32[3,32,32,128]{3,2,1,0:T(8,128)S(1)}, s32[3,32,32,128]{3,2,1,0:T(8,128)S(1)}) custom-call(f32[6,96,128]{2,1,0:T(8,128)S(1)} %bitcast.25, f32[6,96,128]{2,1,0:T(8,128)S(1)} %bitcast.26, f32[3,32,16,128]{3,2,1,0:T(8,128)} %courant_hbm.1, s32[3,32,16,128]{3,2,1,0:T(8,128)} %sign_hbm.1), custom_call_target="tpu_custom_call" | custom-call | tf_op jit(solution)/shard_map/load/pallas_call | solution.py:411
  25.7 6.6 %all-to-all-done = f32[128,2,128]{2,1,0:T(2,128)S(1)} async-done(((f32[128,2,128]{2,1,0:T(2,128)}), f32[128,2,128]{2,1,0:T(2,128)S(1)}, u32[]{:S(2)}, u32[]{:S(2)}) %all-to-all-start) | async-done | bytes 131104 | tf_op jit(solution)/shard_map/all_to_all | solution.py:460
  32.3 1.3 %first.1 = (f32[1024,128]{1,0:T(8,128)S(1)}, f32[1,1024]{1,0:T(1,128)S(1)}, f32[1,1024]{1,0:T(1,128)S(1)}, f32[32,128]{1,0:T(8,128)S(1)}) custom-call(f32[256,128]{1,0:T(8,128)S(1)} %bitcast.23, f32[3,32,32,128]{3,2,1,0:T(8,128)S(1)} %get-tuple-element.30.courant_ref, s32[3,32,32,128]{3,2,1,0:T(8,128)S(1)} %get-tuple-element.31.sign_ref), custom_call_target="tpu_custom_call" | custom-call | tf_op jit(solution)/shard_map/first/pallas_call | solution.py:411
  33.6 2.5 %collective-permute-start.4 = (f32[32,128]{1,0:T(8,128)S(1)}, f32[32,128]{1,0:T(8,128)S(1)}, u32[]{:S(2)}, u32[]{:S(2)}) collective-permute-start(f32[32,128]{1,0:T(8,128)S(1)} %get-tuple-element.35), channel_id=1, source_target_pairs={{0,1},{1,0},{2,3},{3,2},{4,5},{5,4},{6,7},{7,6},{8,9},{9,8},{10,11... | collective-permute-start | bytes 49160 | tf_op jit(solution)/shard_map/ppermute | solution.py:403
  36.0 0.3 collective-permute-start.2
  36.3 0.4 collective-permute-start.3
  36.7 0.6 inner2.1.kept_ref
  37.3 0.0 copy-start
  37.4 1.1 %collective-permute-done.2.ye = f32[1,1024]{1,0:T(1,128)S(1)} collective-permute-done((f32[1,1024]{1,0:T(1,128)S(1)}, f32[1,1024]{1,0:T(1,128)S(1)}, u32[]{:S(2)}, u32[]{:S(2)}) %collective-permute-start.2) | collective-permute-done | bytes 4128 | tf_op jit(solution)/shard_map/ppermute | solution.py:398
  38.5 1.5 %collective-permute-done.3.yo = f32[1,1024]{1,0:T(1,128)S(1)} collective-permute-done((f32[1,1024]{1,0:T(1,128)S(1)}, f32[1,1024]{1,0:T(1,128)S(1)}, u32[]{:S(2)}, u32[]{:S(2)}) %collective-permute-start.3) | collective-permute-done | bytes 4128 | tf_op jit(solution)/shard_map/ppermute | solution.py:398
  40.0 0.0 collective-permute-done.4.z
  40.0 0.4 join2.1
  40.4 1.6 %collective-permute-start.7 = (f32[32,128]{1,0:T(8,128)S(1)}, f32[32,128]{1,0:T(8,128)S(1)}, u32[]{:S(2)}, u32[]{:S(2)}) collective-permute-start(f32[32,128]{1,0:T(8,128)S(1)} %get-tuple-element.40), channel_id=1, source_target_pairs={{0,1},{1,0},{2,3},{3,2},{4,5},{5,4},{6,7},{7,6},{8,9},{9,8},{10,11... | collective-permute-start | bytes 49160 | tf_op jit(solution)/shard_map/ppermute | solution.py:403
  42.0 0.0 collective-permute-start.5
  42.0 0.4 collective-permute-start.6
  42.5 0.0 copy-done
  42.5 0.7 inner1.1
  43.1 1.4 %collective-permute-done.5.ye = f32[1,1024]{1,0:T(1,128)S(1)} collective-permute-done((f32[1,1024]{1,0:T(1,128)S(1)}, f32[1,1024]{1,0:T(1,128)S(1)}, u32[]{:S(2)}, u32[]{:S(2)}) %collective-permute-start.5) | collective-permute-done | bytes 4128 | tf_op jit(solution)/shard_map/ppermute | solution.py:398
  44.5 1.2 %collective-permute-done.6.yo = f32[1,1024]{1,0:T(1,128)S(1)} collective-permute-done((f32[1,1024]{1,0:T(1,128)S(1)}, f32[1,1024]{1,0:T(1,128)S(1)}, u32[]{:S(2)}, u32[]{:S(2)}) %collective-permute-start.6) | collective-permute-done | bytes 4128 | tf_op jit(solution)/shard_map/ppermute | solution.py:398
  45.7 0.0 collective-permute-done.7.z
  45.7 0.4 join1.1
  46.1 1.6 %collective-permute-start.10 = (f32[32,128]{1,0:T(8,128)S(1)}, f32[32,128]{1,0:T(8,128)S(1)}, u32[]{:S(2)}, u32[]{:S(2)}) collective-permute-start(f32[32,128]{1,0:T(8,128)S(1)} %get-tuple-element.46), channel_id=1, source_target_pairs={{0,1},{1,0},{2,3},{3,2},{4,5},{5,4},{6,7},{7,6},{8,9},{9,8},{10,11... | collective-permute-start | bytes 49160 | tf_op jit(solution)/shard_map/ppermute | solution.py:403
  47.7 0.3 collective-permute-start.8
  48.0 0.4 collective-permute-start.9
  48.4 0.6 inner0.1
  49.0 1.1 %collective-permute-done.8.ye = f32[1,1024]{1,0:T(1,128)S(1)} collective-permute-done((f32[1,1024]{1,0:T(1,128)S(1)}, f32[1,1024]{1,0:T(1,128)S(1)}, u32[]{:S(2)}, u32[]{:S(2)}) %collective-permute-start.8) | collective-permute-done | bytes 4128 | tf_op jit(solution)/shard_map/ppermute | solution.py:398
  50.2 1.5 %collective-permute-done.9.yo = f32[1,1024]{1,0:T(1,128)S(1)} collective-permute-done((f32[1,1024]{1,0:T(1,128)S(1)}, f32[1,1024]{1,0:T(1,128)S(1)}, u32[]{:S(2)}, u32[]{:S(2)}) %collective-permute-start.9) | collective-permute-done | bytes 4128 | tf_op jit(solution)/shard_map/ppermute | solution.py:398
  51.7 0.0 collective-permute-done.10.z
  51.7 1.0 %join0.1 = (f32[512,128]{1,0:T(8,128)}, f32[640,128]{1,0:T(8,128)S(1)}) custom-call(f32[1024,128]{1,0:T(8,128)S(1)} %get-tuple-element.43.kept_ref, f32[1,1024]{1,0:T(1,128)S(1)} %collective-permute-done.8.ye, f32[1,1024]{1,0:T(1,128)S(1)} %collective-permute-done.9.yo, f32[32,128]{1,0:T(8,128)S(1)} %collective-permute-done.10.z, ...), custom_call_target="tpu_custom_call" | custom-call | tf_op jit(solution)/shard_map/join0/pallas_call | solution.py:411
  52.7 13.2 %all_to_all.15 = f32[8,80,128]{2,1,0:T(8,128)S(1)} all-to-all(f32[8,80,128]{2,1,0:T(8,128)S(1)} %bitcast.24), channel_id=1, replica_groups=mesh['gx'=16,'gy'=8,'gz'=2] {'gy'}, dimensions={0} | all-to-all | bytes 655360 | tf_op jit(solution)/shard_map/all_to_all | solution.py:519
  65.8 0.2 carry.1
  66.1 10.4 %all_to_all.16 = f32[16,32,128]{2,1,0:T(8,128)S(1)} all-to-all(f32[16,32,128]{2,1,0:T(8,128)S(1)} %bitcast.22), channel_id=1, replica_groups=mesh['gx'=16,'gy'=8,'gz'=2] {'gx'}, dimensions={0} | all-to-all | bytes 524288 | tf_op jit(solution)/shard_map/all_to_all | solution.py:525
  76.5 5.0 %collective-permute-start.11 = (f32[16,16,128]{2,1,0:T(8,128)S(1)}, f32[16,16,128]{2,1,0:T(8,128)S(1)}, u32[]{:S(2)}, u32[]{:S(2)}) collective-permute-start(f32[16,16,128]{2,1,0:T(8,128)S(1)} %slice.4), channel_id=1, source_target_pairs={{0,1},{1,0},{2,3},{3,2},{4,5},{5,4},{6,7},{7,6},{8,9},{9,8},{10,11... | collective-permute-start | bytes 393224 | tf_op jit(solution)/shard_map/ppermute | solution.py:529
  81.4 0.3 smooth_own.1
  81.7 0.7 collective-permute-done.11
  82.4 1.2 %smooth_xz.1 = f32[256,256]{1,0:T(8,128)} custom-call(f32[128,256]{1,0:T(8,128)S(1)} %get-tuple-element.50.own_ref, f32[256,256]{1,0:T(8,128)S(1)} %get-tuple-element.51.table_ref, f32[256,128]{1,0:T(8,128)S(1)} %bitcast.27), custom_call_target="tpu_custom_call" | custom-call | tf_op jit(solution)/shard_map/smooth_xz/pallas_call | solution.py:411
  (1 shorter events, 0.0 us)
Async XLA Ops:
  2.8 18.1 %collective-permute-start = (f32[6,32,3,1,128]{4,3,2,1,0:T(1,128)S(1)}, f32[6,32,3,1,128]{4,3,2,1,0:T(1,128)S(1)}, u32[]{:S(2)}, u32[]{:S(2)}) collective-permute-start(f32[6,32,3,1,128]{4,3,2,1,0:T(1,128)S(1)} %get-tuple-element.28), channel_id=1, source_target_pairs={{0,16},{16,0},{32,48},{48,32},{64,80},{80,64},{96,112},{112,96},{1... | collective-permute-start | bytes 884744 | tf_op jit(solution)/shard_map/ppermute | solution.py:398
  5.0 16.6 %collective-permute-start.1 = (f32[6,32,3,1,128]{4,3,2,1,0:T(1,128)S(1)}, f32[6,32,3,1,128]{4,3,2,1,0:T(1,128)S(1)}, u32[]{:S(2)}, u32[]{:S(2)}) collective-permute-start(f32[6,32,3,1,128]{4,3,2,1,0:T(1,128)S(1)} %get-tuple-element.29), channel_id=1, source_target_pairs={{16,32},{48,64},{80,96},{112,128},{144,160},{176,192},{208,224},{2... | collective-permute-start | bytes 884744 | tf_op jit(solution)/shard_map/ppermute | solution.py:398
  9.1 23.2 %all-to-all-start = ((f32[128,2,128]{2,1,0:T(2,128)}), f32[128,2,128]{2,1,0:T(2,128)S(1)}, u32[]{:S(2)}, u32[]{:S(2)}) async-start(f32[128,2,128]{2,1,0:T(2,128)} %bitcast.5), calls=%async_computation | async-start | bytes 262144 | tf_op jit(solution)/shard_map/all_to_all | solution.py:460
  20.9 0.7 copy-start.1
  21.6 0.7 copy-start.3
  22.3 1.0 %copy-start.2 = (f32[6,32,3,1,128]{4,3,2,1,0:T(1,128)S(1)}, f32[6,32,3,1,128]{4,3,2,1,0:T(1,128)}, u32[]{:S(2)}) copy-start(f32[6,32,3,1,128]{4,3,2,1,0:T(1,128)} %copy-done.1) | copy-start | bytes 884740
  23.3 1.0 %copy-start.4 = (f32[6,32,3,1,128]{4,3,2,1,0:T(1,128)S(1)}, f32[6,32,3,1,128]{4,3,2,1,0:T(1,128)}, u32[]{:S(2)}) copy-start(f32[6,32,3,1,128]{4,3,2,1,0:T(1,128)} %copy-done.3) | copy-start | bytes 884740
  33.6 6.4 %collective-permute-start.4 = (f32[32,128]{1,0:T(8,128)S(1)}, f32[32,128]{1,0:T(8,128)S(1)}, u32[]{:S(2)}, u32[]{:S(2)}) collective-permute-start(f32[32,128]{1,0:T(8,128)S(1)} %get-tuple-element.35), channel_id=1, source_target_pairs={{0,1},{1,0},{2,3},{3,2},{4,5},{5,4},{6,7},{7,6},{8,9},{9,8},{10,11... | collective-permute-start | bytes 49160 | tf_op jit(solution)/shard_map/ppermute | solution.py:403
  36.0 2.5 %collective-permute-start.2 = (f32[1,1024]{1,0:T(1,128)S(1)}, f32[1,1024]{1,0:T(1,128)S(1)}, u32[]{:S(2)}, u32[]{:S(2)}) collective-permute-start(f32[1,1024]{1,0:T(1,128)S(1)} %get-tuple-element.33), channel_id=1, source_target_pairs={{0,2},{2,0},{4,6},{6,4},{8,10},{10,8},{12,14},{14,12},{1,3},{3,1},... | collective-permute-start | bytes 12296 | tf_op jit(solution)/shard_map/ppermute | solution.py:398
  36.3 3.7 %collective-permute-start.3 = (f32[1,1024]{1,0:T(1,128)S(1)}, f32[1,1024]{1,0:T(1,128)S(1)}, u32[]{:S(2)}, u32[]{:S(2)}) collective-permute-start(f32[1,1024]{1,0:T(1,128)S(1)} %get-tuple-element.34), channel_id=1, source_target_pairs={{2,4},{6,8},{10,12},{14,0},{4,2},{8,6},{12,10},{0,14},{3,5},{7,9},... | collective-permute-start | bytes 12296 | tf_op jit(solution)/shard_map/ppermute | solution.py:398
  37.3 5.1 %copy-start = (f32[3,32,16,128]{3,2,1,0:T(8,128)S(1)}, f32[3,32,16,128]{3,2,1,0:T(8,128)}, u32[]{:S(2)}) copy-start(f32[3,32,16,128]{3,2,1,0:T(8,128)} %param.11) | copy-start | bytes 2359300
  40.4 5.3 %collective-permute-start.7 = (f32[32,128]{1,0:T(8,128)S(1)}, f32[32,128]{1,0:T(8,128)S(1)}, u32[]{:S(2)}, u32[]{:S(2)}) collective-permute-start(f32[32,128]{1,0:T(8,128)S(1)} %get-tuple-element.40), channel_id=1, source_target_pairs={{0,1},{1,0},{2,3},{3,2},{4,5},{5,4},{6,7},{7,6},{8,9},{9,8},{10,11... | collective-permute-start | bytes 49160 | tf_op jit(solution)/shard_map/ppermute | solution.py:403
  42.0 2.5 %collective-permute-start.5 = (f32[1,1024]{1,0:T(1,128)S(1)}, f32[1,1024]{1,0:T(1,128)S(1)}, u32[]{:S(2)}, u32[]{:S(2)}) collective-permute-start(f32[1,1024]{1,0:T(1,128)S(1)} %get-tuple-element.38), channel_id=1, source_target_pairs={{0,2},{2,0},{4,6},{6,4},{8,10},{10,8},{12,14},{14,12},{1,3},{3,1},... | collective-permute-start | bytes 12296 | tf_op jit(solution)/shard_map/ppermute | solution.py:398
  42.0 3.7 %collective-permute-start.6 = (f32[1,1024]{1,0:T(1,128)S(1)}, f32[1,1024]{1,0:T(1,128)S(1)}, u32[]{:S(2)}, u32[]{:S(2)}) collective-permute-start(f32[1,1024]{1,0:T(1,128)S(1)} %get-tuple-element.39), channel_id=1, source_target_pairs={{2,4},{6,8},{10,12},{14,0},{4,2},{8,6},{12,10},{0,14},{3,5},{7,9},... | collective-permute-start | bytes 12296 | tf_op jit(solution)/shard_map/ppermute | solution.py:398
  46.1 5.5 %collective-permute-start.10 = (f32[32,128]{1,0:T(8,128)S(1)}, f32[32,128]{1,0:T(8,128)S(1)}, u32[]{:S(2)}, u32[]{:S(2)}) collective-permute-start(f32[32,128]{1,0:T(8,128)S(1)} %get-tuple-element.46), channel_id=1, source_target_pairs={{0,1},{1,0},{2,3},{3,2},{4,5},{5,4},{6,7},{7,6},{8,9},{9,8},{10,11... | collective-permute-start | bytes 49160 | tf_op jit(solution)/shard_map/ppermute | solution.py:403
  47.7 2.5 %collective-permute-start.8 = (f32[1,1024]{1,0:T(1,128)S(1)}, f32[1,1024]{1,0:T(1,128)S(1)}, u32[]{:S(2)}, u32[]{:S(2)}) collective-permute-start(f32[1,1024]{1,0:T(1,128)S(1)} %get-tuple-element.44), channel_id=1, source_target_pairs={{0,2},{2,0},{4,6},{6,4},{8,10},{10,8},{12,14},{14,12},{1,3},{3,1},... | collective-permute-start | bytes 12296 | tf_op jit(solution)/shard_map/ppermute | solution.py:398
  48.0 3.7 %collective-permute-start.9 = (f32[1,1024]{1,0:T(1,128)S(1)}, f32[1,1024]{1,0:T(1,128)S(1)}, u32[]{:S(2)}, u32[]{:S(2)}) collective-permute-start(f32[1,1024]{1,0:T(1,128)S(1)} %get-tuple-element.45), channel_id=1, source_target_pairs={{2,4},{6,8},{10,12},{14,0},{4,2},{8,6},{12,10},{0,14},{3,5},{7,9},... | collective-permute-start | bytes 12296 | tf_op jit(solution)/shard_map/ppermute | solution.py:398
  76.5 6.0 %collective-permute-start.11 = (f32[16,16,128]{2,1,0:T(8,128)S(1)}, f32[16,16,128]{2,1,0:T(8,128)S(1)}, u32[]{:S(2)}, u32[]{:S(2)}) collective-permute-start(f32[16,16,128]{2,1,0:T(8,128)S(1)} %slice.4), channel_id=1, source_target_pairs={{0,1},{1,0},{2,3},{3,2},{4,5},{5,4},{6,7},{7,6},{8,9},{9,8},{10,11... | collective-permute-start | bytes 393224 | tf_op jit(solution)/shard_map/ppermute | solution.py:529

commit v6 on v5

--- a/solution.py
+++ b/solution.py
@@ -284,7 +284,7 @@
     group = sizes[1] * (places + 1)
     order = iota((rows_each * group, lanes), 0)
     r, j, e = order // group, order % group // (places + 1), order % (places + 1)
-    y_out = y_of(sizes, lanes, rows_each, e, j, r)
+    y_out = y_of(sizes, rows_each, e, j, r)
     y_out = jnp.where(e < places, y_out, jnp.where(r == 0, lanes - 1, 0))
     table = jnp.exp(-jnp.abs(y_out - iota(order.shape, 1)).astype(F32) / length) * (1.0 / math.sqrt(length))
     result = dot3(table, lines, ((1,), (1,)))
@@ -300,7 +300,7 @@
     copy.wait()
 
 
-def y_of(sizes, lanes, rows_each, place, gy, r):
+def y_of(sizes, rows_each, place, gy, r):
     high, low = place // sizes[2], place % sizes[2]
     return high * (sizes[1] * sizes[2] * rows_each) + gy * (sizes[2] * rows_each) + low * rows_each + r
 
@@ -339,7 +339,7 @@
     for high in range(places // sizes[2]):
         factors = []
         for low in range(sizes[2]):
-            y = y_of(sizes, lanes, rows_each, high * sizes[2] + low, gy, iota((1, lanes), 1) // depth)
+            y = y_of(sizes, rows_each, high * sizes[2] + low, gy, iota((1, lanes), 1) // depth)
             y = y.astype(F32)
             factors.append((jnp.exp(-(y + 1.0) / length), jnp.exp(-(lanes - y) / length)))
         for g in range(bricks):
@@ -395,15 +395,19 @@
 
 def swap(even, odd, axis):
     pairs = pair_swaps(lax.axis_size(axis))
-    return lax.ppermute(even, axis, pairs[0]), lax.ppermute(odd, axis, pairs[1])
+    even = lax.ppermute(even, axis, pairs[0])
+    odd = lax.ppermute(odd, axis, pairs[1])
+    return even, odd
 
 
 def exchange(faces):
     ye, yo, z = faces
-    return (*swap(ye, yo, "gy"), lax.ppermute(z, "gz", [(0, 1), (1, 0)]))
-
-
-def local(kernel, name, inputs, outputs, scratch=(), far=0, far_outputs=()):
+    ye, yo = swap(ye, yo, "gy")
+    z = lax.ppermute(z, "gz", [(0, 1), (1, 0)])
+    return ye, yo, z
+
+
+def local(kernel, inputs, outputs, scratch=(), far=0, far_outputs=()):
     vmem = pl.BlockSpec(memory_space=pltpu.VMEM)
     hbm = pl.BlockSpec(memory_space=pl.ANY)
     near = len(inputs) - far
@@ -418,7 +422,6 @@
         ],
         scratch_shapes=scratch,
         compiler_params=pltpu.CompilerParams(vmem_limit_bytes=12 << 20),
-        name=name,
     )(
         *[pltpu.with_memory_space_constraint(values, pltpu.VMEM) for values in inputs[:near]],
         *[pltpu.with_memory_space_constraint(values, pltpu.HBM) for values in inputs[near:]],
@@ -432,13 +435,11 @@
     sizes = (lax.axis_size("gx"), lax.axis_size("gy"), lax.axis_size("gz"))
     devices = sizes[0] * sizes[1] * sizes[2]
     owners = sizes[0] * sizes[1]
-    axes = ("gx", "gy", "gz")
     trace = tracer.reshape(steps, rows, brick_y)
     ends = (6, brick_z, HALO, 1, brick_y)
     lined = (3, brick_z, brick_x, 1, brick_y)
     outgoing, even, odd = local(
         open_kernel,
-        "open",
         [
             well_sources.T,
             well_owner.reshape(1, wells),
@@ -464,7 +465,6 @@
     stack = (3, brick_z, wide_x, brick_y)
     weights = local(
         functools.partial(load_kernel, sizes[0]),
-        "load",
         [
             even.reshape(6, brick_z * HALO, brick_y),
             odd.reshape(6, brick_z * HALO, brick_y),
@@ -480,12 +480,7 @@
     wide = (brick_z * wide_x, brick_y)
     face_shapes = [(1, brick_z * wide_x)] * 2 + [(wide_x, brick_y)]
     gradient = []
-    adjoint, *faces = local(
-        functools.partial(first_kernel, steps - 1),
-        "first",
-        [received, *weights],
-        [wide] + face_shapes,
-    )
+    adjoint, *faces = local(functools.partial(first_kernel, steps - 1), [received, *weights], [wide] + face_shapes)
     for step in reversed(range(steps)):
         arrived = exchange(faces)
         if step == steps - 1:
@@ -493,24 +488,17 @@
         else:
             inputs, outputs, tracer_step = [trace] + gradient, [field], step + 1
         *gradient, kept = local(
-            functools.partial(inner_kernel, step, tracer_step),
-            f"inner{step}",
-            [adjoint, *weights] + inputs,
-            outputs + [wide],
+            functools.partial(inner_kernel, step, tracer_step), [adjoint, *weights] + inputs, outputs + [wide]
         )
         if step:
             adjoint, *faces = local(
-                functools.partial(middle_kernel, sizes, step - 1),
-                f"join{step}",
-                [kept, *arrived, *weights],
-                [wide] + face_shapes,
+                functools.partial(middle_kernel, sizes, step - 1), [kept, *arrived, *weights], [wide] + face_shapes
             )
     rows_each = sizes[1] * brick_y // devices
     block = (brick_y // (sizes[1] * rows_each) + 1) * brick_x
     length_y = 2.0 * brick_y
     adjoint, lines = local(
         functools.partial(last_kernel, sizes, length_y, brick_z),
-        "join0",
         [kept, *arrived, trace, *gradient],
         [field, (sizes[1] * block, brick_y)],
         [pltpu.VMEM(field, F32), pltpu.VMEM(field, F32), pltpu.SemaphoreType.DMA],
@@ -519,9 +507,7 @@
     lines = lax.all_to_all(
         lines.reshape(sizes[1], block, brick_y), "gy", split_axis=0, concat_axis=0, tiled=True
     ).reshape(sizes[1] * block, brick_y)
-    (planes,) = local(
-        functools.partial(carry_kernel, sizes, brick_z, brick_x, length_y), "carry", [lines], [field]
-    )
+    (planes,) = local(functools.partial(carry_kernel, sizes, brick_z, brick_x, length_y), [lines], [field])
     planes = lax.all_to_all(
         planes.reshape(sizes[0], sizes[2] * brick_x, brick_y), "gx", split_axis=0, concat_axis=0, tiled=True
     )
@@ -529,13 +515,11 @@
     other = lax.ppermute(planes[:, :brick_x], "gz", [(0, 1), (1, 0)])
     own, table = local(
         functools.partial(smooth_own_kernel, brick_x, 2.0 * brick_x),
-        "smooth_own",
         [planes.reshape(field)],
         [(brick_y, full_x), (full_x, full_x)],
     )
     (smoothed,) = local(
         functools.partial(smooth_xz_kernel, brick_z, 2.0 * brick_z),
-        "smooth_xz",
         [own, table, other.reshape(full_x, brick_y)],
         [(rows_each * full_z, full_x)],
         [pltpu.VMEM((rows_each * full_z, full_x), F32), pltpu.SemaphoreType.DMA((rows_each,))],

time: 84.1 us -> 84.1 us (level)
  no operation moved by 1% of the time
where the time goes in v6:
time: 84.1 us; the launch traced here: 83.8 us
  starting transfers between devices  30.6 us (36%)
  blocking collectives  23.5 us (28%)
  waiting for transfers between devices  15.2 us (18%)
  Pallas kernels  10.3 us (12%)
  local copies, waits for them, and re-layouts  3.36 us (4%)
  between operations  0.92 us (1%)
    all_to_all x1, blocking collectives, per_device(): lax.all_to_all(lines.reshape(sizes[1], block, brick_y), 'gy', split_axis=...  13.2 us
    all_to_all x1, starting transfers between devices, per_device(): lax.all_to_all(outgoing.reshape(owners, CAP, 128), ('gx', 'gy'), split_ax...  11.8 us
    all_to_all x1, blocking collectives, per_device(): lax.all_to_all(planes.reshape(sizes[0], sizes[2] * brick_x, brick_y), 'gx...  10.4 us
    pallas_call x12, Pallas kernels, local(): pl.pallas_call(kernel, in_specs=[vmem] * near + [hbm] * far, out_specs=[h...  10.3 us
    all_to_all x1, waiting for transfers between devices, per_device(): lax.all_to_all(outgoing.reshape(owners, CAP, 128), ('gx', 'gy'), split_ax...  6.64 us
    ppermute x3, starting transfers between devices, exchange(): z = lax.ppermute(z, 'gz', [(0, 1), (1, 0)])  5.68 us
    ppermute x4, starting transfers between devices, swap(): odd = lax.ppermute(odd, axis, pairs[1])  5.34 us
    ppermute x1, starting transfers between devices, per_device(): other = lax.ppermute(planes[:, :brick_x], 'gz', [(0, 1), (1, 0)])  4.98 us
  transfers between devices with their start and end apart: 13, of which 8 were waited for; matrix products, arithmetic and copies ran while one was open for 0% of the time, Pallas kernels for 4%

profile of v6, /device:TPU:1, one launch (start us, length us, event | category | flops | bytes accessed | tf_op | source)
XLA Modules:
  0.0 83.8 jit_solution(8715003785278354381)
XLA Ops:
  0.6 2.1 %shard_map.77 = (f32[256,128]{1,0:T(8,128)}, f32[6,32,3,1,128]{4,3,2,1,0:T(1,128)S(1)}, f32[6,32,3,1,128]{4,3,2,1,0:T(1,128)S(1)}) custom-call(f32[32,96]{1,0:T(8,128)} %bitcast.31, s32[1,96]{1,0:T(1,128)} %bitcast.32, s32[1,96]{1,0:T(1,128)} %bitcast.33, f32[3,32,16,1,128]{4,3,2,1,0:T(1,128)} %bitcast.28, s32[3,32,16,1,128]{4,3,2,1,0:T(1,128)} %bitcast.29), custom_call_target="tpu_custom_call" | custom-call | tf_op jit(solution)/shard_map/pallas_call | solution.py:415
  2.8 2.2 %collective-permute-start = (f32[6,32,3,1,128]{4,3,2,1,0:T(1,128)S(1)}, f32[6,32,3,1,128]{4,3,2,1,0:T(1,128)S(1)}, u32[]{:S(2)}, u32[]{:S(2)}) collective-permute-start(f32[6,32,3,1,128]{4,3,2,1,0:T(1,128)S(1)} %get-tuple-element.28), channel_id=1, source_target_pairs={{0,16},{16,0},{32,48},{48,32},{64,80},{80,64},{96,112},{112,96},{1... | collective-permute-start | bytes 884744 | tf_op jit(solution)/shard_map/ppermute | solution.py:398
  5.0 4.1 %collective-permute-start.1 = (f32[6,32,3,1,128]{4,3,2,1,0:T(1,128)S(1)}, f32[6,32,3,1,128]{4,3,2,1,0:T(1,128)S(1)}, u32[]{:S(2)}, u32[]{:S(2)}) collective-permute-start(f32[6,32,3,1,128]{4,3,2,1,0:T(1,128)S(1)} %get-tuple-element.29), channel_id=1, source_target_pairs={{16,32},{48,64},{80,96},{112,128},{144,160},{176,192},{208,224},{2... | collective-permute-start | bytes 884744 | tf_op jit(solution)/shard_map/ppermute | solution.py:399
  9.1 11.8 %all-to-all-start = ((f32[128,2,128]{2,1,0:T(2,128)}), f32[128,2,128]{2,1,0:T(2,128)S(1)}, u32[]{:S(2)}, u32[]{:S(2)}) async-start(f32[128,2,128]{2,1,0:T(2,128)} %bitcast.5), calls=%async_computation | async-start | bytes 262144 | tf_op jit(solution)/shard_map/all_to_all | solution.py:461
  20.9 0.0 collective-permute-done
  20.9 0.0 copy-start.1
  20.9 0.7 copy-done.1
  21.6 0.0 collective-permute-done.1
  21.6 0.0 copy-start.3
  21.6 0.7 copy-done.3
  22.3 0.0 copy-start.2
  22.3 1.0 %copy-done.2 = f32[6,32,3,1,128]{4,3,2,1,0:T(1,128)S(1)} copy-done((f32[6,32,3,1,128]{4,3,2,1,0:T(1,128)S(1)}, f32[6,32,3,1,128]{4,3,2,1,0:T(1,128)}, u32[]{:S(2)}) %copy-start.2) | copy-done | bytes 294936
  23.3 0.0 copy-start.4
  23.3 1.0 %copy-done.4 = f32[6,32,3,1,128]{4,3,2,1,0:T(1,128)S(1)} copy-done((f32[6,32,3,1,128]{4,3,2,1,0:T(1,128)S(1)}, f32[6,32,3,1,128]{4,3,2,1,0:T(1,128)}, u32[]{:S(2)}) %copy-start.4) | copy-done | bytes 294936
  24.2 1.4 %shard_map.78 = (f32[3,32,32,128]{3,2,1,0:T(8,128)S(1)}, s32[3,32,32,128]{3,2,1,0:T(8,128)S(1)}) custom-call(f32[6,96,128]{2,1,0:T(8,128)S(1)} %bitcast.25, f32[6,96,128]{2,1,0:T(8,128)S(1)} %bitcast.26, f32[3,32,16,128]{3,2,1,0:T(8,128)} %courant_hbm.1, s32[3,32,16,128]{3,2,1,0:T(8,128)} %sign_hbm.1), custom_call_target="tpu_custom_call" | custom-call | tf_op jit(solution)/shard_map/pallas_call | solution.py:415
  25.7 6.6 %all-to-all-done = f32[128,2,128]{2,1,0:T(2,128)S(1)} async-done(((f32[128,2,128]{2,1,0:T(2,128)}), f32[128,2,128]{2,1,0:T(2,128)S(1)}, u32[]{:S(2)}, u32[]{:S(2)}) %all-to-all-start) | async-done | bytes 131104 | tf_op jit(solution)/shard_map/all_to_all | solution.py:461
  32.3 1.3 %shard_map.79 = (f32[1024,128]{1,0:T(8,128)S(1)}, f32[1,1024]{1,0:T(1,128)S(1)}, f32[1,1024]{1,0:T(1,128)S(1)}, f32[32,128]{1,0:T(8,128)S(1)}) custom-call(f32[256,128]{1,0:T(8,128)S(1)} %bitcast.23, f32[3,32,32,128]{3,2,1,0:T(8,128)S(1)} %get-tuple-element.30.courant_ref, s32[3,32,32,128]{3,2,1,0:T(8,128)S(1)} %get-tuple-element.31.sign_ref), custom_call_target="tpu_custom_call" | custom-call | tf_op jit(solution)/shard_map/pallas_call | solution.py:415
  33.6 2.5 %collective-permute-start.4 = (f32[32,128]{1,0:T(8,128)S(1)}, f32[32,128]{1,0:T(8,128)S(1)}, u32[]{:S(2)}, u32[]{:S(2)}) collective-permute-start(f32[32,128]{1,0:T(8,128)S(1)} %get-tuple-element.35), channel_id=1, source_target_pairs={{0,1},{1,0},{2,3},{3,2},{4,5},{5,4},{6,7},{7,6},{8,9},{9,8},{10,11... | collective-permute-start | bytes 49160 | tf_op jit(solution)/shard_map/ppermute | solution.py:406
  36.0 0.3 collective-permute-start.2
  36.3 0.4 collective-permute-start.3
  36.7 0.6 shard_map.80.kept_ref
  37.3 0.0 copy-start
  37.4 1.1 %collective-permute-done.2.ye = f32[1,1024]{1,0:T(1,128)S(1)} collective-permute-done((f32[1,1024]{1,0:T(1,128)S(1)}, f32[1,1024]{1,0:T(1,128)S(1)}, u32[]{:S(2)}, u32[]{:S(2)}) %collective-permute-start.2) | collective-permute-done | bytes 4128 | tf_op jit(solution)/shard_map/ppermute | solution.py:398
  38.5 1.5 %collective-permute-done.3.yo = f32[1,1024]{1,0:T(1,128)S(1)} collective-permute-done((f32[1,1024]{1,0:T(1,128)S(1)}, f32[1,1024]{1,0:T(1,128)S(1)}, u32[]{:S(2)}, u32[]{:S(2)}) %collective-permute-start.3) | collective-permute-done | bytes 4128 | tf_op jit(solution)/shard_map/ppermute | solution.py:399
  40.0 0.0 collective-permute-done.4.z
  40.0 0.4 shard_map.81
  40.4 1.6 %collective-permute-start.7 = (f32[32,128]{1,0:T(8,128)S(1)}, f32[32,128]{1,0:T(8,128)S(1)}, u32[]{:S(2)}, u32[]{:S(2)}) collective-permute-start(f32[32,128]{1,0:T(8,128)S(1)} %get-tuple-element.40), channel_id=1, source_target_pairs={{0,1},{1,0},{2,3},{3,2},{4,5},{5,4},{6,7},{7,6},{8,9},{9,8},{10,11... | collective-permute-start | bytes 49160 | tf_op jit(solution)/shard_map/ppermute | solution.py:406
  42.0 0.0 collective-permute-start.5
  42.0 0.4 collective-permute-start.6
  42.5 0.0 copy-done
  42.5 0.7 shard_map.82
  43.1 1.4 %collective-permute-done.5.ye = f32[1,1024]{1,0:T(1,128)S(1)} collective-permute-done((f32[1,1024]{1,0:T(1,128)S(1)}, f32[1,1024]{1,0:T(1,128)S(1)}, u32[]{:S(2)}, u32[]{:S(2)}) %collective-permute-start.5) | collective-permute-done | bytes 4128 | tf_op jit(solution)/shard_map/ppermute | solution.py:398
  44.5 1.2 %collective-permute-done.6.yo = f32[1,1024]{1,0:T(1,128)S(1)} collective-permute-done((f32[1,1024]{1,0:T(1,128)S(1)}, f32[1,1024]{1,0:T(1,128)S(1)}, u32[]{:S(2)}, u32[]{:S(2)}) %collective-permute-start.6) | collective-permute-done | bytes 4128 | tf_op jit(solution)/shard_map/ppermute | solution.py:399
  45.7 0.0 collective-permute-done.7.z
  45.7 0.4 shard_map.83
  46.1 1.6 %collective-permute-start.10 = (f32[32,128]{1,0:T(8,128)S(1)}, f32[32,128]{1,0:T(8,128)S(1)}, u32[]{:S(2)}, u32[]{:S(2)}) collective-permute-start(f32[32,128]{1,0:T(8,128)S(1)} %get-tuple-element.46), channel_id=1, source_target_pairs={{0,1},{1,0},{2,3},{3,2},{4,5},{5,4},{6,7},{7,6},{8,9},{9,8},{10,11... | collective-permute-start | bytes 49160 | tf_op jit(solution)/shard_map/ppermute | solution.py:406
  47.7 0.3 collective-permute-start.8
  48.0 0.4 collective-permute-start.9
  48.4 0.6 shard_map.84
  49.0 1.1 %collective-permute-done.8.ye = f32[1,1024]{1,0:T(1,128)S(1)} collective-permute-done((f32[1,1024]{1,0:T(1,128)S(1)}, f32[1,1024]{1,0:T(1,128)S(1)}, u32[]{:S(2)}, u32[]{:S(2)}) %collective-permute-start.8) | collective-permute-done | bytes 4128 | tf_op jit(solution)/shard_map/ppermute | solution.py:398
  50.2 1.5 %collective-permute-done.9.yo = f32[1,1024]{1,0:T(1,128)S(1)} collective-permute-done((f32[1,1024]{1,0:T(1,128)S(1)}, f32[1,1024]{1,0:T(1,128)S(1)}, u32[]{:S(2)}, u32[]{:S(2)}) %collective-permute-start.9) | collective-permute-done | bytes 4128 | tf_op jit(solution)/shard_map/ppermute | solution.py:399
  51.7 0.0 collective-permute-done.10.z
  51.7 1.0 %shard_map.85 = (f32[512,128]{1,0:T(8,128)}, f32[640,128]{1,0:T(8,128)S(1)}) custom-call(f32[1024,128]{1,0:T(8,128)S(1)} %get-tuple-element.43.kept_ref, f32[1,1024]{1,0:T(1,128)S(1)} %collective-permute-done.8.ye, f32[1,1024]{1,0:T(1,128)S(1)} %collective-permute-done.9.yo, f32[32,128]{1,0:T(8,128)S(1)} %collective-permute-done.10.z, ...), custom_call_target="tpu_custom_call" | custom-call | tf_op jit(solution)/shard_map/pallas_call | solution.py:415
  52.7 13.2 %all_to_all.15 = f32[8,80,128]{2,1,0:T(8,128)S(1)} all-to-all(f32[8,80,128]{2,1,0:T(8,128)S(1)} %bitcast.24), channel_id=1, replica_groups=mesh['gx'=16,'gy'=8,'gz'=2] {'gy'}, dimensions={0} | all-to-all | bytes 655360 | tf_op jit(solution)/shard_map/all_to_all | solution.py:507
  65.8 0.2 shard_map.86
  66.1 10.4 %all_to_all.16 = f32[16,32,128]{2,1,0:T(8,128)S(1)} all-to-all(f32[16,32,128]{2,1,0:T(8,128)S(1)} %bitcast.22), channel_id=1, replica_groups=mesh['gx'=16,'gy'=8,'gz'=2] {'gx'}, dimensions={0} | all-to-all | bytes 524288 | tf_op jit(solution)/shard_map/all_to_all | solution.py:511
  76.5 5.0 %collective-permute-start.11 = (f32[16,16,128]{2,1,0:T(8,128)S(1)}, f32[16,16,128]{2,1,0:T(8,128)S(1)}, u32[]{:S(2)}, u32[]{:S(2)}) collective-permute-start(f32[16,16,128]{2,1,0:T(8,128)S(1)} %slice.4), channel_id=1, source_target_pairs={{0,1},{1,0},{2,3},{3,2},{4,5},{5,4},{6,7},{7,6},{8,9},{9,8},{10,11... | collective-permute-start | bytes 393224 | tf_op jit(solution)/shard_map/ppermute | solution.py:515
  81.4 0.3 shard_map.87
  81.7 0.7 collective-permute-done.11
  82.4 1.2 %shard_map.88 = f32[256,256]{1,0:T(8,128)} custom-call(f32[128,256]{1,0:T(8,128)S(1)} %get-tuple-element.50.own_ref, f32[256,256]{1,0:T(8,128)S(1)} %get-tuple-element.51.table_ref, f32[256,128]{1,0:T(8,128)S(1)} %bitcast.27), custom_call_target="tpu_custom_call" | custom-call | tf_op jit(solution)/shard_map/pallas_call | solution.py:415
  (1 shorter events, 0.0 us)
Async XLA Ops:
  2.8 18.1 %collective-permute-start = (f32[6,32,3,1,128]{4,3,2,1,0:T(1,128)S(1)}, f32[6,32,3,1,128]{4,3,2,1,0:T(1,128)S(1)}, u32[]{:S(2)}, u32[]{:S(2)}) collective-permute-start(f32[6,32,3,1,128]{4,3,2,1,0:T(1,128)S(1)} %get-tuple-element.28), channel_id=1, source_target_pairs={{0,16},{16,0},{32,48},{48,32},{64,80},{80,64},{96,112},{112,96},{1... | collective-permute-start | bytes 884744 | tf_op jit(solution)/shard_map/ppermute | solution.py:398
  5.0 16.6 %collective-permute-start.1 = (f32[6,32,3,1,128]{4,3,2,1,0:T(1,128)S(1)}, f32[6,32,3,1,128]{4,3,2,1,0:T(1,128)S(1)}, u32[]{:S(2)}, u32[]{:S(2)}) collective-permute-start(f32[6,32,3,1,128]{4,3,2,1,0:T(1,128)S(1)} %get-tuple-element.29), channel_id=1, source_target_pairs={{16,32},{48,64},{80,96},{112,128},{144,160},{176,192},{208,224},{2... | collective-permute-start | bytes 884744 | tf_op jit(solution)/shard_map/ppermute | solution.py:399
  9.1 23.2 %all-to-all-start = ((f32[128,2,128]{2,1,0:T(2,128)}), f32[128,2,128]{2,1,0:T(2,128)S(1)}, u32[]{:S(2)}, u32[]{:S(2)}) async-start(f32[128,2,128]{2,1,0:T(2,128)} %bitcast.5), calls=%async_computation | async-start | bytes 262144 | tf_op jit(solution)/shard_map/all_to_all | solution.py:461
  20.9 0.7 copy-start.1
  21.6 0.7 copy-start.3
  22.3 1.0 %copy-start.2 = (f32[6,32,3,1,128]{4,3,2,1,0:T(1,128)S(1)}, f32[6,32,3,1,128]{4,3,2,1,0:T(1,128)}, u32[]{:S(2)}) copy-start(f32[6,32,3,1,128]{4,3,2,1,0:T(1,128)} %copy-done.1) | copy-start | bytes 884740
  23.3 1.0 %copy-start.4 = (f32[6,32,3,1,128]{4,3,2,1,0:T(1,128)S(1)}, f32[6,32,3,1,128]{4,3,2,1,0:T(1,128)}, u32[]{:S(2)}) copy-start(f32[6,32,3,1,128]{4,3,2,1,0:T(1,128)} %copy-done.3) | copy-start | bytes 884740
  33.6 6.4 %collective-permute-start.4 = (f32[32,128]{1,0:T(8,128)S(1)}, f32[32,128]{1,0:T(8,128)S(1)}, u32[]{:S(2)}, u32[]{:S(2)}) collective-permute-start(f32[32,128]{1,0:T(8,128)S(1)} %get-tuple-element.35), channel_id=1, source_target_pairs={{0,1},{1,0},{2,3},{3,2},{4,5},{5,4},{6,7},{7,6},{8,9},{9,8},{10,11... | collective-permute-start | bytes 49160 | tf_op jit(solution)/shard_map/ppermute | solution.py:406
  36.0 2.5 %collective-permute-start.2 = (f32[1,1024]{1,0:T(1,128)S(1)}, f32[1,1024]{1,0:T(1,128)S(1)}, u32[]{:S(2)}, u32[]{:S(2)}) collective-permute-start(f32[1,1024]{1,0:T(1,128)S(1)} %get-tuple-element.33), channel_id=1, source_target_pairs={{0,2},{2,0},{4,6},{6,4},{8,10},{10,8},{12,14},{14,12},{1,3},{3,1},... | collective-permute-start | bytes 12296 | tf_op jit(solution)/shard_map/ppermute | solution.py:398
  36.3 3.7 %collective-permute-start.3 = (f32[1,1024]{1,0:T(1,128)S(1)}, f32[1,1024]{1,0:T(1,128)S(1)}, u32[]{:S(2)}, u32[]{:S(2)}) collective-permute-start(f32[1,1024]{1,0:T(1,128)S(1)} %get-tuple-element.34), channel_id=1, source_target_pairs={{2,4},{6,8},{10,12},{14,0},{4,2},{8,6},{12,10},{0,14},{3,5},{7,9},... | collective-permute-start | bytes 12296 | tf_op jit(solution)/shard_map/ppermute | solution.py:399
  37.3 5.1 %copy-start = (f32[3,32,16,128]{3,2,1,0:T(8,128)S(1)}, f32[3,32,16,128]{3,2,1,0:T(8,128)}, u32[]{:S(2)}) copy-start(f32[3,32,16,128]{3,2,1,0:T(8,128)} %param.11) | copy-start | bytes 2359300
  40.4 5.3 %collective-permute-start.7 = (f32[32,128]{1,0:T(8,128)S(1)}, f32[32,128]{1,0:T(8,128)S(1)}, u32[]{:S(2)}, u32[]{:S(2)}) collective-permute-start(f32[32,128]{1,0:T(8,128)S(1)} %get-tuple-element.40), channel_id=1, source_target_pairs={{0,1},{1,0},{2,3},{3,2},{4,5},{5,4},{6,7},{7,6},{8,9},{9,8},{10,11... | collective-permute-start | bytes 49160 | tf_op jit(solution)/shard_map/ppermute | solution.py:406
  42.0 2.5 %collective-permute-start.5 = (f32[1,1024]{1,0:T(1,128)S(1)}, f32[1,1024]{1,0:T(1,128)S(1)}, u32[]{:S(2)}, u32[]{:S(2)}) collective-permute-start(f32[1,1024]{1,0:T(1,128)S(1)} %get-tuple-element.38), channel_id=1, source_target_pairs={{0,2},{2,0},{4,6},{6,4},{8,10},{10,8},{12,14},{14,12},{1,3},{3,1},... | collective-permute-start | bytes 12296 | tf_op jit(solution)/shard_map/ppermute | solution.py:398
  42.0 3.7 %collective-permute-start.6 = (f32[1,1024]{1,0:T(1,128)S(1)}, f32[1,1024]{1,0:T(1,128)S(1)}, u32[]{:S(2)}, u32[]{:S(2)}) collective-permute-start(f32[1,1024]{1,0:T(1,128)S(1)} %get-tuple-element.39), channel_id=1, source_target_pairs={{2,4},{6,8},{10,12},{14,0},{4,2},{8,6},{12,10},{0,14},{3,5},{7,9},... | collective-permute-start | bytes 12296 | tf_op jit(solution)/shard_map/ppermute | solution.py:399
  46.1 5.5 %collective-permute-start.10 = (f32[32,128]{1,0:T(8,128)S(1)}, f32[32,128]{1,0:T(8,128)S(1)}, u32[]{:S(2)}, u32[]{:S(2)}) collective-permute-start(f32[32,128]{1,0:T(8,128)S(1)} %get-tuple-element.46), channel_id=1, source_target_pairs={{0,1},{1,0},{2,3},{3,2},{4,5},{5,4},{6,7},{7,6},{8,9},{9,8},{10,11... | collective-permute-start | bytes 49160 | tf_op jit(solution)/shard_map/ppermute | solution.py:406
  47.7 2.5 %collective-permute-start.8 = (f32[1,1024]{1,0:T(1,128)S(1)}, f32[1,1024]{1,0:T(1,128)S(1)}, u32[]{:S(2)}, u32[]{:S(2)}) collective-permute-start(f32[1,1024]{1,0:T(1,128)S(1)} %get-tuple-element.44), channel_id=1, source_target_pairs={{0,2},{2,0},{4,6},{6,4},{8,10},{10,8},{12,14},{14,12},{1,3},{3,1},... | collective-permute-start | bytes 12296 | tf_op jit(solution)/shard_map/ppermute | solution.py:398
  48.0 3.7 %collective-permute-start.9 = (f32[1,1024]{1,0:T(1,128)S(1)}, f32[1,1024]{1,0:T(1,128)S(1)}, u32[]{:S(2)}, u32[]{:S(2)}) collective-permute-start(f32[1,1024]{1,0:T(1,128)S(1)} %get-tuple-element.45), channel_id=1, source_target_pairs={{2,4},{6,8},{10,12},{14,0},{4,2},{8,6},{12,10},{0,14},{3,5},{7,9},... | collective-permute-start | bytes 12296 | tf_op jit(solution)/shard_map/ppermute | solution.py:399
  76.5 6.0 %collective-permute-start.11 = (f32[16,16,128]{2,1,0:T(8,128)S(1)}, f32[16,16,128]{2,1,0:T(8,128)S(1)}, u32[]{:S(2)}, u32[]{:S(2)}) collective-permute-start(f32[16,16,128]{2,1,0:T(8,128)S(1)} %slice.4), channel_id=1, source_target_pairs={{0,1},{1,0},{2,3},{3,2},{4,5},{5,4},{6,7},{7,6},{8,9},{9,8},{10,11... | collective-permute-start | bytes 393224 | tf_op jit(solution)/shard_map/ppermute | solution.py:515

commit v7 on v6

--- a/solution.py
+++ b/solution.py
@@ -353,32 +353,36 @@
             out_ref[start + across : start + 2 * across, :] = jnp.where(first_core, values[0], values[1])
 
 
-def smooth_own_kernel(across, length, data_ref, own_ref, table_ref):
-    full_x = own_ref.shape[1]
+def depth_table(depth, length, core):
+    z_out, z_in = iota((2 * depth, depth), 0), iota((2 * depth, depth), 1) + core * depth
+    return jnp.exp(-jnp.abs(z_out - z_in).astype(F32) / length) * (1.0 / math.sqrt(length))
+
+
+def smooth_own_kernel(depth, across, length_x, length_z, data_ref, sum_ref, high_ref, low_ref):
+    full_x = sum_ref.shape[1]
     x_in, x_out = iota((full_x, full_x), 0), iota((full_x, full_x), 1)
-    table = jnp.exp(-jnp.abs(x_in - x_out).astype(F32) / length) * (1.0 / math.sqrt(length))
-    table_ref[...] = table
+    table = jnp.exp(-jnp.abs(x_in - x_out).astype(F32) / length_x) * (1.0 / math.sqrt(length_x))
+    high_ref[...], low_ref[...] = halves(table)
     own = jnp.concatenate(
         [data_ref[(2 * g + 1) * across : (2 * g + 2) * across, :] for g in range(full_x // across)], axis=0
     )
-    own_ref[...] = dot3(own, table, ((0,), (0,)))
-
-
-def smooth_xz_kernel(depth, length, own_ref, table_ref, other_ref, out_hbm, work_ref, sems):
-    rows_each = own_ref.shape[0] // depth
-    gz = lax.axis_index("gz")
-    own = own_ref[...]
-    other = dot3(other_ref[...], table_ref[...], ((0,), (0,)))
-    full_z = 2 * depth
-    z_out, z_in = iota((full_z, full_z), 0), iota((full_z, full_z), 1)
-    z_in = z_in % depth + jnp.where(z_in < depth, gz, 1 - gz) * depth
-    table = jnp.exp(-jnp.abs(z_out - z_in).astype(F32) / length) * (1.0 / math.sqrt(length))
+    own = dot3(own, table, ((0,), (0,)))
+    table = depth_table(depth, length_z, lax.axis_index("gz"))
+    for r in range(own.shape[0] // depth):
+        here = slice(2 * r * depth, 2 * (r + 1) * depth)
+        sum_ref[here, :] = dot3(table, own[r * depth : (r + 1) * depth], ((1,), (0,)))
+
+
+def smooth_xz_kernel(depth, length, sum_ref, high_ref, low_ref, other_ref, out_hbm, work_ref, sems):
+    rows_each = other_ref.shape[1] // depth
+    high, low = halves(other_ref[...])
+    sides = ((0,), (0,))
+    other = dot(high, high_ref[...], sides) + (dot(high, low_ref[...], sides) + dot(low, high_ref[...], sides))
+    table = depth_table(depth, length, 1 - lax.axis_index("gz"))
     copies = []
     for r in range(rows_each):
-        part = slice(r * depth, (r + 1) * depth)
-        column = jnp.concatenate([own[part], other[part]], axis=0)
-        here = slice(r * full_z, (r + 1) * full_z)
-        work_ref[here, :] = dot3(table, column, ((1,), (0,)))
+        here = slice(2 * r * depth, 2 * (r + 1) * depth)
+        work_ref[here, :] = sum_ref[here, :] + dot3(table, other[r * depth : (r + 1) * depth], ((1,), (0,)))
         copy = pltpu.make_async_copy(work_ref.at[here], out_hbm.at[here], sems.at[r])
         copy.start()
         copies.append(copy)
@@ -513,14 +517,15 @@
     )
     full_x, full_z = sizes[0] * brick_x, sizes[2] * brick_z
     other = lax.ppermute(planes[:, :brick_x], "gz", [(0, 1), (1, 0)])
-    own, table = local(
-        functools.partial(smooth_own_kernel, brick_x, 2.0 * brick_x),
+    table = ((full_x, full_x), BF16)
+    partial, high, low = local(
+        functools.partial(smooth_own_kernel, brick_z, brick_x, 2.0 * brick_x, 2.0 * brick_z),
         [planes.reshape(field)],
-        [(brick_y, full_x), (full_x, full_x)],
+        [(rows_each * full_z, full_x), table, table],
     )
     (smoothed,) = local(
         functools.partial(smooth_xz_kernel, brick_z, 2.0 * brick_z),
-        [own, table, other.reshape(full_x, brick_y)],
+        [partial, high, low, other.reshape(full_x, brick_y)],
         [(rows_each * full_z, full_x)],
         [pltpu.VMEM((rows_each * full_z, full_x), F32), pltpu.SemaphoreType.DMA((rows_each,))],
         far_outputs=(0,),

time: 84.1 us -> 84.1 us (level)
  transfers between devices with their start and end apart: 13 -> 13, of which waited for: 8 -> 8; matrix products, arithmetic and copies ran while one was open for 0% -> 0% of each run, Pallas kernels for 4% -> 5%
where the time goes in v7:
time: 84.1 us; the launch traced here: 83.8 us
  starting transfers between devices  30.6 us (36%)
  blocking collectives  23.5 us (28%)
  waiting for transfers between devices  14.9 us (18%)
  Pallas kernels  10.6 us (13%)
  local copies, waits for them, and re-layouts  3.36 us (4%)
  between operations  0.92 us (1%)
    all_to_all x1, blocking collectives, per_device(): lax.all_to_all(lines.reshape(sizes[1], block, brick_y), 'gy', split_axis=...  13.2 us
    all_to_all x1, starting transfers between devices, per_device(): lax.all_to_all(outgoing.reshape(owners, CAP, 128), ('gx', 'gy'), split_ax...  11.8 us
    pallas_call x12, Pallas kernels, local(): pl.pallas_call(kernel, in_specs=[vmem] * near + [hbm] * far, out_specs=[h...  10.6 us
    all_to_all x1, blocking collectives, per_device(): lax.all_to_all(planes.reshape(sizes[0], sizes[2] * brick_x, brick_y), 'gx...  10.4 us
    all_to_all x1, waiting for transfers between devices, per_device(): lax.all_to_all(outgoing.reshape(owners, CAP, 128), ('gx', 'gy'), split_ax...  6.64 us
    ppermute x3, starting transfers between devices, exchange(): z = lax.ppermute(z, 'gz', [(0, 1), (1, 0)])  5.68 us
    ppermute x4, starting transfers between devices, swap(): odd = lax.ppermute(odd, axis, pairs[1])  5.34 us
    ppermute x1, starting transfers between devices, per_device(): other = lax.ppermute(planes[:, :brick_x], 'gz', [(0, 1), (1, 0)])  4.98 us
  transfers between devices with their start and end apart: 13, of which 8 were waited for; matrix products, arithmetic and copies ran while one was open for 0% of the time, Pallas kernels for 5%

profile of v7, /device:TPU:1, one launch (start us, length us, event | category | flops | bytes accessed | tf_op | source)
XLA Modules:
  0.0 83.8 jit_solution(944081368237589636)
XLA Ops:
  0.6 2.1 %shard_map.77 = (f32[256,128]{1,0:T(8,128)}, f32[6,32,3,1,128]{4,3,2,1,0:T(1,128)S(1)}, f32[6,32,3,1,128]{4,3,2,1,0:T(1,128)S(1)}) custom-call(f32[32,96]{1,0:T(8,128)} %bitcast.31, s32[1,96]{1,0:T(1,128)} %bitcast.32, s32[1,96]{1,0:T(1,128)} %bitcast.33, f32[3,32,16,1,128]{4,3,2,1,0:T(1,128)} %bitcast.28, s32[3,32,16,1,128]{4,3,2,1,0:T(1,128)} %bitcast.29), custom_call_target="tpu_custom_call" | custom-call | tf_op jit(solution)/shard_map/pallas_call | solution.py:419
  2.8 2.2 %collective-permute-start = (f32[6,32,3,1,128]{4,3,2,1,0:T(1,128)S(1)}, f32[6,32,3,1,128]{4,3,2,1,0:T(1,128)S(1)}, u32[]{:S(2)}, u32[]{:S(2)}) collective-permute-start(f32[6,32,3,1,128]{4,3,2,1,0:T(1,128)S(1)} %get-tuple-element.29), channel_id=1, source_target_pairs={{0,16},{16,0},{32,48},{48,32},{64,80},{80,64},{96,112},{112,96},{1... | collective-permute-start | bytes 884744 | tf_op jit(solution)/shard_map/ppermute | solution.py:402
  5.0 4.1 %collective-permute-start.1 = (f32[6,32,3,1,128]{4,3,2,1,0:T(1,128)S(1)}, f32[6,32,3,1,128]{4,3,2,1,0:T(1,128)S(1)}, u32[]{:S(2)}, u32[]{:S(2)}) collective-permute-start(f32[6,32,3,1,128]{4,3,2,1,0:T(1,128)S(1)} %get-tuple-element.30), channel_id=1, source_target_pairs={{16,32},{48,64},{80,96},{112,128},{144,160},{176,192},{208,224},{2... | collective-permute-start | bytes 884744 | tf_op jit(solution)/shard_map/ppermute | solution.py:403
  9.1 11.8 %all-to-all-start = ((f32[128,2,128]{2,1,0:T(2,128)}), f32[128,2,128]{2,1,0:T(2,128)S(1)}, u32[]{:S(2)}, u32[]{:S(2)}) async-start(f32[128,2,128]{2,1,0:T(2,128)} %bitcast.5), calls=%async_computation | async-start | bytes 262144 | tf_op jit(solution)/shard_map/all_to_all | solution.py:465
  20.9 0.0 collective-permute-done
  20.9 0.0 copy-start.1
  20.9 0.7 copy-done.1
  21.6 0.0 collective-permute-done.1
  21.6 0.0 copy-start.3
  21.6 0.7 copy-done.3
  22.3 0.0 copy-start.2
  22.3 1.0 %copy-done.2 = f32[6,32,3,1,128]{4,3,2,1,0:T(1,128)S(1)} copy-done((f32[6,32,3,1,128]{4,3,2,1,0:T(1,128)S(1)}, f32[6,32,3,1,128]{4,3,2,1,0:T(1,128)}, u32[]{:S(2)}) %copy-start.2) | copy-done | bytes 294936
  23.3 0.0 copy-start.4
  23.3 1.0 %copy-done.4 = f32[6,32,3,1,128]{4,3,2,1,0:T(1,128)S(1)} copy-done((f32[6,32,3,1,128]{4,3,2,1,0:T(1,128)S(1)}, f32[6,32,3,1,128]{4,3,2,1,0:T(1,128)}, u32[]{:S(2)}) %copy-start.4) | copy-done | bytes 294936
  24.2 1.4 %shard_map.78 = (f32[3,32,32,128]{3,2,1,0:T(8,128)S(1)}, s32[3,32,32,128]{3,2,1,0:T(8,128)S(1)}) custom-call(f32[6,96,128]{2,1,0:T(8,128)S(1)} %bitcast.25, f32[6,96,128]{2,1,0:T(8,128)S(1)} %bitcast.26, f32[3,32,16,128]{3,2,1,0:T(8,128)} %courant_hbm.1, s32[3,32,16,128]{3,2,1,0:T(8,128)} %sign_hbm.1), custom_call_target="tpu_custom_call" | custom-call | tf_op jit(solution)/shard_map/pallas_call | solution.py:419
  25.7 6.6 %all-to-all-done = f32[128,2,128]{2,1,0:T(2,128)S(1)} async-done(((f32[128,2,128]{2,1,0:T(2,128)}), f32[128,2,128]{2,1,0:T(2,128)S(1)}, u32[]{:S(2)}, u32[]{:S(2)}) %all-to-all-start) | async-done | bytes 131104 | tf_op jit(solution)/shard_map/all_to_all | solution.py:465
  32.3 1.3 %shard_map.79 = (f32[1024,128]{1,0:T(8,128)S(1)}, f32[1,1024]{1,0:T(1,128)S(1)}, f32[1,1024]{1,0:T(1,128)S(1)}, f32[32,128]{1,0:T(8,128)S(1)}) custom-call(f32[256,128]{1,0:T(8,128)S(1)} %bitcast.23, f32[3,32,32,128]{3,2,1,0:T(8,128)S(1)} %get-tuple-element.31.courant_ref, s32[3,32,32,128]{3,2,1,0:T(8,128)S(1)} %get-tuple-element.32.sign_ref), custom_call_target="tpu_custom_call" | custom-call | tf_op jit(solution)/shard_map/pallas_call | solution.py:419
  33.6 2.5 %collective-permute-start.4 = (f32[32,128]{1,0:T(8,128)S(1)}, f32[32,128]{1,0:T(8,128)S(1)}, u32[]{:S(2)}, u32[]{:S(2)}) collective-permute-start(f32[32,128]{1,0:T(8,128)S(1)} %get-tuple-element.36), channel_id=1, source_target_pairs={{0,1},{1,0},{2,3},{3,2},{4,5},{5,4},{6,7},{7,6},{8,9},{9,8},{10,11... | collective-permute-start | bytes 49160 | tf_op jit(solution)/shard_map/ppermute | solution.py:410
  36.0 0.3 collective-permute-start.2
  36.3 0.4 collective-permute-start.3
  36.7 0.6 shard_map.80.kept_ref
  37.3 0.0 copy-start
  37.4 1.1 %collective-permute-done.2.ye = f32[1,1024]{1,0:T(1,128)S(1)} collective-permute-done((f32[1,1024]{1,0:T(1,128)S(1)}, f32[1,1024]{1,0:T(1,128)S(1)}, u32[]{:S(2)}, u32[]{:S(2)}) %collective-permute-start.2) | collective-permute-done | bytes 4128 | tf_op jit(solution)/shard_map/ppermute | solution.py:402
  38.5 1.5 %collective-permute-done.3.yo = f32[1,1024]{1,0:T(1,128)S(1)} collective-permute-done((f32[1,1024]{1,0:T(1,128)S(1)}, f32[1,1024]{1,0:T(1,128)S(1)}, u32[]{:S(2)}, u32[]{:S(2)}) %collective-permute-start.3) | collective-permute-done | bytes 4128 | tf_op jit(solution)/shard_map/ppermute | solution.py:403
  40.0 0.0 collective-permute-done.4.z
  40.0 0.4 shard_map.81
  40.4 1.6 %collective-permute-start.7 = (f32[32,128]{1,0:T(8,128)S(1)}, f32[32,128]{1,0:T(8,128)S(1)}, u32[]{:S(2)}, u32[]{:S(2)}) collective-permute-start(f32[32,128]{1,0:T(8,128)S(1)} %get-tuple-element.41), channel_id=1, source_target_pairs={{0,1},{1,0},{2,3},{3,2},{4,5},{5,4},{6,7},{7,6},{8,9},{9,8},{10,11... | collective-permute-start | bytes 49160 | tf_op jit(solution)/shard_map/ppermute | solution.py:410
  42.0 0.0 collective-permute-start.5
  42.0 0.4 collective-permute-start.6
  42.5 0.0 copy-done
  42.5 0.7 shard_map.82
  43.1 1.4 %collective-permute-done.5.ye = f32[1,1024]{1,0:T(1,128)S(1)} collective-permute-done((f32[1,1024]{1,0:T(1,128)S(1)}, f32[1,1024]{1,0:T(1,128)S(1)}, u32[]{:S(2)}, u32[]{:S(2)}) %collective-permute-start.5) | collective-permute-done | bytes 4128 | tf_op jit(solution)/shard_map/ppermute | solution.py:402
  44.5 1.2 %collective-permute-done.6.yo = f32[1,1024]{1,0:T(1,128)S(1)} collective-permute-done((f32[1,1024]{1,0:T(1,128)S(1)}, f32[1,1024]{1,0:T(1,128)S(1)}, u32[]{:S(2)}, u32[]{:S(2)}) %collective-permute-start.6) | collective-permute-done | bytes 4128 | tf_op jit(solution)/shard_map/ppermute | solution.py:403
  45.7 0.0 collective-permute-done.7.z
  45.7 0.4 shard_map.83
  46.1 1.6 %collective-permute-start.10 = (f32[32,128]{1,0:T(8,128)S(1)}, f32[32,128]{1,0:T(8,128)S(1)}, u32[]{:S(2)}, u32[]{:S(2)}) collective-permute-start(f32[32,128]{1,0:T(8,128)S(1)} %get-tuple-element.47), channel_id=1, source_target_pairs={{0,1},{1,0},{2,3},{3,2},{4,5},{5,4},{6,7},{7,6},{8,9},{9,8},{10,11... | collective-permute-start | bytes 49160 | tf_op jit(solution)/shard_map/ppermute | solution.py:410
  47.7 0.3 collective-permute-start.8
  48.0 0.4 collective-permute-start.9
  48.4 0.6 shard_map.84
  49.0 1.1 %collective-permute-done.8.ye = f32[1,1024]{1,0:T(1,128)S(1)} collective-permute-done((f32[1,1024]{1,0:T(1,128)S(1)}, f32[1,1024]{1,0:T(1,128)S(1)}, u32[]{:S(2)}, u32[]{:S(2)}) %collective-permute-start.8) | collective-permute-done | bytes 4128 | tf_op jit(solution)/shard_map/ppermute | solution.py:402
  50.2 1.5 %collective-permute-done.9.yo = f32[1,1024]{1,0:T(1,128)S(1)} collective-permute-done((f32[1,1024]{1,0:T(1,128)S(1)}, f32[1,1024]{1,0:T(1,128)S(1)}, u32[]{:S(2)}, u32[]{:S(2)}) %collective-permute-start.9) | collective-permute-done | bytes 4128 | tf_op jit(solution)/shard_map/ppermute | solution.py:403
  51.7 0.0 collective-permute-done.10.z
  51.7 1.0 %shard_map.85 = (f32[512,128]{1,0:T(8,128)}, f32[640,128]{1,0:T(8,128)S(1)}) custom-call(f32[1024,128]{1,0:T(8,128)S(1)} %get-tuple-element.44.kept_ref, f32[1,1024]{1,0:T(1,128)S(1)} %collective-permute-done.8.ye, f32[1,1024]{1,0:T(1,128)S(1)} %collective-permute-done.9.yo, f32[32,128]{1,0:T(8,128)S(1)} %collective-permute-done.10.z, ...), custom_call_target="tpu_custom_call" | custom-call | tf_op jit(solution)/shard_map/pallas_call | solution.py:419
  52.7 13.2 %all_to_all.15 = f32[8,80,128]{2,1,0:T(8,128)S(1)} all-to-all(f32[8,80,128]{2,1,0:T(8,128)S(1)} %bitcast.24), channel_id=1, replica_groups=mesh['gx'=16,'gy'=8,'gz'=2] {'gy'}, dimensions={0} | all-to-all | bytes 655360 | tf_op jit(solution)/shard_map/all_to_all | solution.py:511
  65.8 0.2 shard_map.86
  66.1 10.4 %all_to_all.16 = f32[16,32,128]{2,1,0:T(8,128)S(1)} all-to-all(f32[16,32,128]{2,1,0:T(8,128)S(1)} %bitcast.22), channel_id=1, replica_groups=mesh['gx'=16,'gy'=8,'gz'=2] {'gx'}, dimensions={0} | all-to-all | bytes 524288 | tf_op jit(solution)/shard_map/all_to_all | solution.py:515
  76.5 5.0 %collective-permute-start.11 = (f32[16,16,128]{2,1,0:T(8,128)S(1)}, f32[16,16,128]{2,1,0:T(8,128)S(1)}, u32[]{:S(2)}, u32[]{:S(2)}) collective-permute-start(f32[16,16,128]{2,1,0:T(8,128)S(1)} %slice.4), channel_id=1, source_target_pairs={{0,1},{1,0},{2,3},{3,2},{4,5},{5,4},{6,7},{7,6},{8,9},{9,8},{10,11... | collective-permute-start | bytes 393224 | tf_op jit(solution)/shard_map/ppermute | solution.py:519
  81.4 0.6 shard_map.87
  82.0 0.4 collective-permute-done.11
  82.4 1.2 %shard_map.88 = f32[256,256]{1,0:T(8,128)} custom-call(f32[256,256]{1,0:T(8,128)S(1)} %get-tuple-element.51.sum_ref, bf16[256,256]{1,0:T(8,128)(2,1)S(1)} %get-tuple-element.52.high_ref, bf16[256,256]{1,0:T(8,128)(2,1)S(1)} %get-tuple-element.53.low_ref, f32[256,128]{1,0:T(8,128)S(1)} %bitcast.27), custom_call_target="tpu_custom_call" | custom-call | tf_op jit(solution)/shard_map/pallas_call | solution.py:419
  (1 shorter events, 0.0 us)
Async XLA Ops:
  2.8 18.1 %collective-permute-start = (f32[6,32,3,1,128]{4,3,2,1,0:T(1,128)S(1)}, f32[6,32,3,1,128]{4,3,2,1,0:T(1,128)S(1)}, u32[]{:S(2)}, u32[]{:S(2)}) collective-permute-start(f32[6,32,3,1,128]{4,3,2,1,0:T(1,128)S(1)} %get-tuple-element.29), channel_id=1, source_target_pairs={{0,16},{16,0},{32,48},{48,32},{64,80},{80,64},{96,112},{112,96},{1... | collective-permute-start | bytes 884744 | tf_op jit(solution)/shard_map/ppermute | solution.py:402
  5.0 16.6 %collective-permute-start.1 = (f32[6,32,3,1,128]{4,3,2,1,0:T(1,128)S(1)}, f32[6,32,3,1,128]{4,3,2,1,0:T(1,128)S(1)}, u32[]{:S(2)}, u32[]{:S(2)}) collective-permute-start(f32[6,32,3,1,128]{4,3,2,1,0:T(1,128)S(1)} %get-tuple-element.30), channel_id=1, source_target_pairs={{16,32},{48,64},{80,96},{112,128},{144,160},{176,192},{208,224},{2... | collective-permute-start | bytes 884744 | tf_op jit(solution)/shard_map/ppermute | solution.py:403
  9.1 23.2 %all-to-all-start = ((f32[128,2,128]{2,1,0:T(2,128)}), f32[128,2,128]{2,1,0:T(2,128)S(1)}, u32[]{:S(2)}, u32[]{:S(2)}) async-start(f32[128,2,128]{2,1,0:T(2,128)} %bitcast.5), calls=%async_computation | async-start | bytes 262144 | tf_op jit(solution)/shard_map/all_to_all | solution.py:465
  20.9 0.7 copy-start.1
  21.6 0.7 copy-start.3
  22.3 1.0 %copy-start.2 = (f32[6,32,3,1,128]{4,3,2,1,0:T(1,128)S(1)}, f32[6,32,3,1,128]{4,3,2,1,0:T(1,128)}, u32[]{:S(2)}) copy-start(f32[6,32,3,1,128]{4,3,2,1,0:T(1,128)} %copy-done.1) | copy-start | bytes 884740
  23.3 1.0 %copy-start.4 = (f32[6,32,3,1,128]{4,3,2,1,0:T(1,128)S(1)}, f32[6,32,3,1,128]{4,3,2,1,0:T(1,128)}, u32[]{:S(2)}) copy-start(f32[6,32,3,1,128]{4,3,2,1,0:T(1,128)} %copy-done.3) | copy-start | bytes 884740
  33.6 6.4 %collective-permute-start.4 = (f32[32,128]{1,0:T(8,128)S(1)}, f32[32,128]{1,0:T(8,128)S(1)}, u32[]{:S(2)}, u32[]{:S(2)}) collective-permute-start(f32[32,128]{1,0:T(8,128)S(1)} %get-tuple-element.36), channel_id=1, source_target_pairs={{0,1},{1,0},{2,3},{3,2},{4,5},{5,4},{6,7},{7,6},{8,9},{9,8},{10,11... | collective-permute-start | bytes 49160 | tf_op jit(solution)/shard_map/ppermute | solution.py:410
  36.0 2.5 %collective-permute-start.2 = (f32[1,1024]{1,0:T(1,128)S(1)}, f32[1,1024]{1,0:T(1,128)S(1)}, u32[]{:S(2)}, u32[]{:S(2)}) collective-permute-start(f32[1,1024]{1,0:T(1,128)S(1)} %get-tuple-element.34), channel_id=1, source_target_pairs={{0,2},{2,0},{4,6},{6,4},{8,10},{10,8},{12,14},{14,12},{1,3},{3,1},... | collective-permute-start | bytes 12296 | tf_op jit(solution)/shard_map/ppermute | solution.py:402
  36.3 3.7 %collective-permute-start.3 = (f32[1,1024]{1,0:T(1,128)S(1)}, f32[1,1024]{1,0:T(1,128)S(1)}, u32[]{:S(2)}, u32[]{:S(2)}) collective-permute-start(f32[1,1024]{1,0:T(1,128)S(1)} %get-tuple-element.35), channel_id=1, source_target_pairs={{2,4},{6,8},{10,12},{14,0},{4,2},{8,6},{12,10},{0,14},{3,5},{7,9},... | collective-permute-start | bytes 12296 | tf_op jit(solution)/shard_map/ppermute | solution.py:403
  37.3 5.1 %copy-start = (f32[3,32,16,128]{3,2,1,0:T(8,128)S(1)}, f32[3,32,16,128]{3,2,1,0:T(8,128)}, u32[]{:S(2)}) copy-start(f32[3,32,16,128]{3,2,1,0:T(8,128)} %param.11) | copy-start | bytes 2359300
  40.4 5.3 %collective-permute-start.7 = (f32[32,128]{1,0:T(8,128)S(1)}, f32[32,128]{1,0:T(8,128)S(1)}, u32[]{:S(2)}, u32[]{:S(2)}) collective-permute-start(f32[32,128]{1,0:T(8,128)S(1)} %get-tuple-element.41), channel_id=1, source_target_pairs={{0,1},{1,0},{2,3},{3,2},{4,5},{5,4},{6,7},{7,6},{8,9},{9,8},{10,11... | collective-permute-start | bytes 49160 | tf_op jit(solution)/shard_map/ppermute | solution.py:410
  42.0 2.5 %collective-permute-start.5 = (f32[1,1024]{1,0:T(1,128)S(1)}, f32[1,1024]{1,0:T(1,128)S(1)}, u32[]{:S(2)}, u32[]{:S(2)}) collective-permute-start(f32[1,1024]{1,0:T(1,128)S(1)} %get-tuple-element.39), channel_id=1, source_target_pairs={{0,2},{2,0},{4,6},{6,4},{8,10},{10,8},{12,14},{14,12},{1,3},{3,1},... | collective-permute-start | bytes 12296 | tf_op jit(solution)/shard_map/ppermute | solution.py:402
  42.0 3.7 %collective-permute-start.6 = (f32[1,1024]{1,0:T(1,128)S(1)}, f32[1,1024]{1,0:T(1,128)S(1)}, u32[]{:S(2)}, u32[]{:S(2)}) collective-permute-start(f32[1,1024]{1,0:T(1,128)S(1)} %get-tuple-element.40), channel_id=1, source_target_pairs={{2,4},{6,8},{10,12},{14,0},{4,2},{8,6},{12,10},{0,14},{3,5},{7,9},... | collective-permute-start | bytes 12296 | tf_op jit(solution)/shard_map/ppermute | solution.py:403
  46.1 5.5 %collective-permute-start.10 = (f32[32,128]{1,0:T(8,128)S(1)}, f32[32,128]{1,0:T(8,128)S(1)}, u32[]{:S(2)}, u32[]{:S(2)}) collective-permute-start(f32[32,128]{1,0:T(8,128)S(1)} %get-tuple-element.47), channel_id=1, source_target_pairs={{0,1},{1,0},{2,3},{3,2},{4,5},{5,4},{6,7},{7,6},{8,9},{9,8},{10,11... | collective-permute-start | bytes 49160 | tf_op jit(solution)/shard_map/ppermute | solution.py:410
  47.7 2.5 %collective-permute-start.8 = (f32[1,1024]{1,0:T(1,128)S(1)}, f32[1,1024]{1,0:T(1,128)S(1)}, u32[]{:S(2)}, u32[]{:S(2)}) collective-permute-start(f32[1,1024]{1,0:T(1,128)S(1)} %get-tuple-element.45), channel_id=1, source_target_pairs={{0,2},{2,0},{4,6},{6,4},{8,10},{10,8},{12,14},{14,12},{1,3},{3,1},... | collective-permute-start | bytes 12296 | tf_op jit(solution)/shard_map/ppermute | solution.py:402
  48.0 3.7 %collective-permute-start.9 = (f32[1,1024]{1,0:T(1,128)S(1)}, f32[1,1024]{1,0:T(1,128)S(1)}, u32[]{:S(2)}, u32[]{:S(2)}) collective-permute-start(f32[1,1024]{1,0:T(1,128)S(1)} %get-tuple-element.46), channel_id=1, source_target_pairs={{2,4},{6,8},{10,12},{14,0},{4,2},{8,6},{12,10},{0,14},{3,5},{7,9},... | collective-permute-start | bytes 12296 | tf_op jit(solution)/shard_map/ppermute | solution.py:403
  76.5 6.0 %collective-permute-start.11 = (f32[16,16,128]{2,1,0:T(8,128)S(1)}, f32[16,16,128]{2,1,0:T(8,128)S(1)}, u32[]{:S(2)}, u32[]{:S(2)}) collective-permute-start(f32[16,16,128]{2,1,0:T(8,128)S(1)} %slice.4), channel_id=1, source_target_pairs={{0,1},{1,0},{2,3},{3,2},{4,5},{5,4},{6,7},{7,6},{8,9},{9,8},{10,11... | collective-permute-start | bytes 393224 | tf_op jit(solution)/shard_map/ppermute | solution.py:519
